TPU v7x, 128 devices: a whole 4x4x4 slice. The times are simulated.
128 devices in a mesh: dp: 4 (over y_lo, core), context: 32 (over y_hi, x, z).
Axes of the slice: x: 4, y: 4 (y_hi: 2, y_lo: 2; y = y_hi * 2 + y_lo), z: 4, core: 2. Of those that a mesh axis runs over, the one named last changes fastest.
Arguments:
- query_in: bfloat16 [4, 4096, 8192], P('dp', 'context'), may hold values from -6 to 6
- key_in: bfloat16 [4, 4096, 8192], P('dp', 'context'), may hold values from -6 to 6
- value_in: bfloat16 [4, 4096, 8192], P('dp', 'context'), may hold values from -6 to 6
- grad_out: bfloat16 [4, 4096, 8192], P('dp', 'context'), may hold values from -6 to 6
- med_filter: float32 [8192, 128], P('context', 'dp'), may hold values from -0.5 to 0.5
- short_filter: float32 [3, 8192, 7], P(None, 'context'), may hold values from -2 to 2
Outputs:
- mixed: bfloat16 [4, 4096, 8192], P('dp', 'context')
- grad_q: bfloat16 [4, 4096, 8192], P('dp', 'context')
- grad_k: bfloat16 [4, 4096, 8192], P('dp', 'context')
- grad_v: bfloat16 [4, 4096, 8192], P('dp', 'context')
- grad_med: float32 [8192, 128], P('context', 'dp')
- grad_short: float32 [3, 8192, 7], P(None, 'context')
All inputs are finite; a program needn't handle non-finite values.
Results may differ from a plain program's by a relative error of at most 0.0058.
Values may be sent and summed in bfloat16 or wider, within the bound.
No kernel may reach another device: no remote copies, remote signals or barrier semaphores. Data moves between devices by JAX's collectives and lax.ppermute only.
A program may use at most 256 MiB of HBM per device.

v0:
```python
import jax
import jax.numpy as jnp
from jax import lax
from jax.sharding import PartitionSpec as P


def short_forward(rows, before, taps):
    width = taps.shape[1]
    count = rows.shape[1]
    padded = jnp.concatenate([before, rows], axis=1).astype(jnp.float32)
    total = jnp.zeros(rows.shape, jnp.float32)
    for offset in range(width):
        start = width - 1 - offset
        total = total + taps[:, offset : offset + 1] * padded[:, start : start + count]
    return total


def short_backward(grads, after, taps):
    width = taps.shape[1]
    count = grads.shape[1]
    padded = jnp.concatenate([grads, after], axis=1)
    total = jnp.zeros(grads.shape, jnp.float32)
    for offset in range(width):
        total = total + taps[:, offset : offset + 1] * padded[:, offset : offset + count]
    return total


def short_weight(grads, rows, before):
    width = before.shape[1] + 1
    count = rows.shape[1]
    padded = jnp.concatenate([before, rows], axis=1).astype(jnp.float32)
    columns = []
    for offset in range(width):
        start = width - 1 - offset
        columns.append(jnp.sum(grads * padded[:, start : start + count], axis=1))
    return jnp.stack(columns, axis=1)


def band_table(size):
    shape = (size, 2 * size * size)
    tap = lax.broadcasted_iota(jnp.int32, shape, 0)
    place = lax.broadcasted_iota(jnp.int32, shape, 1)
    outpos = place // (2 * size)
    inpos = place % (2 * size)
    return (outpos + size - inpos == tap).astype(jnp.float32)


def toeplitz(taps, table):
    size = taps.shape[1]
    flat = jnp.dot(taps, table.astype(jnp.bfloat16), preferred_element_type=jnp.bfloat16)
    return flat.reshape(taps.shape[0], size, 2 * size)


def windows(rows, before):
    size = before.shape[1] + 1
    chans = rows.shape[0]
    first = jnp.concatenate([jnp.zeros((chans, 1), rows.dtype), before], axis=1)
    blocks = rows.reshape(chans, rows.shape[1] // size, size)
    earlier = jnp.concatenate([first[:, None], blocks[:, :-1]], axis=1)
    return jnp.concatenate([earlier, blocks], axis=2)


def medium_conv(rows, before, toep):
    frames = windows(rows, before)
    out = jnp.einsum("cbr,csr->cbs", frames, toep, preferred_element_type=jnp.float32)
    return out.reshape(rows.shape)


def medium_weight(grads, rows, before, table):
    size = before.shape[1] + 1
    chans = rows.shape[0]
    frames = windows(rows, before)
    blocks = grads.reshape(chans, -1, size)
    outer = jnp.einsum("cbs,cbr->csr", blocks, frames, preferred_element_type=jnp.float32)
    flat = outer.reshape(chans, 2 * size * size)
    return jnp.einsum(
        "cq,jq->cj",
        flat,
        table,
        precision=lax.Precision.HIGHEST,
        preferred_element_type=jnp.float32,
    )


def channel_forward(query, keys, values, htaps, shorts, table):
    chans = query.shape[0]
    rim_short = jnp.zeros((chans, shorts.shape[2] - 1), jnp.bfloat16)
    rim_med = jnp.zeros((chans, htaps.shape[1] - 1), jnp.bfloat16)
    toep = toeplitz(htaps, table)
    q_short = short_forward(query, rim_short, shorts[0])
    k_short = short_forward(keys, rim_short, shorts[1])
    v_short = short_forward(values, rim_short, shorts[2])
    product = (k_short * v_short).astype(jnp.bfloat16)
    conv_out = medium_conv(product, rim_med, toep)
    mixed = (q_short * conv_out).astype(jnp.bfloat16)
    saved = (
        query,
        keys,
        values,
        q_short,
        k_short,
        v_short,
        product,
        conv_out,
        toep,
        rim_short,
        rim_med,
    )
    return (mixed, saved)


def channel_backward(saved, cotangent, shorts, table):
    query, keys, values, q_short, k_short, v_short, product, conv_out, toep, rim_short, rim_med = (
        saved
    )
    after_short = jnp.zeros(rim_short.shape, jnp.float32)
    grad_f = cotangent.astype(jnp.float32)
    grad_z = (grad_f * q_short).astype(jnp.bfloat16)
    grad_qs = grad_f * conv_out
    grad_u = jnp.flip(medium_conv(jnp.flip(grad_z, 1), rim_med, toep), 1)
    grad_ks = grad_u * v_short
    grad_vs = grad_u * k_short
    grad_q = short_backward(grad_qs, after_short, shorts[0]).astype(jnp.bfloat16)
    grad_k = short_backward(grad_ks, after_short, shorts[1]).astype(jnp.bfloat16)
    grad_v = short_backward(grad_vs, after_short, shorts[2]).astype(jnp.bfloat16)
    grad_med = medium_weight(grad_z, product, rim_med, table)
    grad_short = jnp.stack(
        [
            short_weight(grad_qs, query, rim_short),
            short_weight(grad_ks, keys, rim_short),
            short_weight(grad_vs, values, rim_short),
        ],
        axis=0,
    )
    return (grad_q, grad_k, grad_v, grad_med, grad_short)


def to_tokens(rows):
    return rows.T[None]


def per_device(query_in, key_in, value_in, grad_out, med_filter, short_filter):
    htaps = lax.all_gather(med_filter.astype(jnp.bfloat16), "dp", axis=1, tiled=True)
    table = band_table(htaps.shape[1])
    query, keys, values = (
        lax.all_to_all(query_in, "context", split_axis=2, concat_axis=1, tiled=True),
        lax.all_to_all(key_in, "context", split_axis=2, concat_axis=1, tiled=True),
        lax.all_to_all(value_in, "context", split_axis=2, concat_axis=1, tiled=True),
    )
    mixed_c, saved = channel_forward(query[0].T, keys[0].T, values[0].T, htaps, short_filter, table)
    mixed = lax.all_to_all(to_tokens(mixed_c), "context", split_axis=1, concat_axis=2, tiled=True)
    cotangent = lax.all_to_all(grad_out, "context", split_axis=2, concat_axis=1, tiled=True)
    grad_qc, grad_kc, grad_vc, med_block, short_block = channel_backward(
        saved, cotangent[0].T, short_filter, table
    )
    grad_q, grad_k, grad_v = (
        lax.all_to_all(to_tokens(grad_qc), "context", split_axis=1, concat_axis=2, tiled=True),
        lax.all_to_all(to_tokens(grad_kc), "context", split_axis=1, concat_axis=2, tiled=True),
        lax.all_to_all(to_tokens(grad_vc), "context", split_axis=1, concat_axis=2, tiled=True),
    )
    grad_med = lax.psum_scatter(med_block, "dp", scatter_dimension=1, tiled=True)
    grad_short = lax.psum(short_block, "dp")
    return (mixed, grad_q, grad_k, grad_v, grad_med, grad_short)


def solution(mesh):
    placed = (
        P("dp", "context", None),
        P("dp", "context", None),
        P("dp", "context", None),
        P("dp", "context", None),
        P("context", "dp"),
        P(None, "context", None),
    )
    return jax.shard_map(
        per_device,
        mesh=mesh,
        in_specs=placed,
        out_specs=(
            P("dp", "context", None),
            P("dp", "context", None),
            P("dp", "context", None),
            P("dp", "context", None),
            P("context", "dp"),
            P(None, "context", None),
        ),
        check_vma=False,
    )
```

profile of v0, /device:TPU:1, one launch (start us, length us, event | category | flops | bytes accessed | tf_op | source)
XLA Modules:
  0.0 1043.7 jit_solution(7348063438053335663)
XLA Ops:
  17.2 45.2 %reduce = bf16[8192,128]{1,0:T(8,128)(2,1)S(1)} reduce(bf16[8192,1,128]{2,1,0:T(2,128)(2,1)} %bitcast.163, bf16[]{:T(256)} %broadcast.71), dimensions={1}, to_apply=%bitcast.124.reduce_sub_computation | reduce | bytes 4194306
  64.4 11.3 %all-to-all-start = ((bf16[32,2,16384]{2,1,0:T(2,128)(2,1)}), bf16[32,2,16384]{2,1,0:T(2,128)(2,1)S(1)}, u32[]{:S(2)}, u32[]{:S(2)}) async-start(bf16[32,2,16384]{2,1,0:T(2,128)(2,1)} %reshape.51), calls=%async_computation | async-start | bytes 4194304 | tf_op jit(solution)/shard_map/all_to_all | solution.py:146
  85.2 46.5 %reduce.1 = bf16[8192,128]{1,0:T(8,128)(2,1)} reduce(bf16[8192,1,128]{2,1,0:T(2,128)(2,1)} %bitcast.175, bf16[]{:T(256)} %broadcast.71), dimensions={1}, to_apply=%bitcast.128.reduce_sub_computation | reduce | bytes 4194306
  154.8 46.5 %reduce.2 = bf16[8192,128]{1,0:T(8,128)(2,1)} reduce(bf16[8192,1,128]{2,1,0:T(2,128)(2,1)} %bitcast.176, bf16[]{:T(256)} %broadcast.71), dimensions={1}, to_apply=%bitcast.126.reduce_sub_computation | reduce | bytes 4194306
  224.3 46.5 %reduce.3 = bf16[8192,128]{1,0:T(8,128)(2,1)} reduce(bf16[8192,1,128]{2,1,0:T(2,128)(2,1)} %bitcast.177, bf16[]{:T(256)} %broadcast.71), dimensions={1}, to_apply=%bitcast.132.reduce_sub_computation | reduce | bytes 4194306
  299.8 23.0 %copy.68 = bf16[256,128,256]{2,1,0:T(8,128)(2,1)} copy(bf16[256,128,256]{0,2,1:T(8,128)(2,1)} %bitcast.178) | data formatting | bytes 33554432 | tf_op jit(solution)/shard_map/reshape | solution.py:51
  335.0 10.5 %reshape.56 = bf16[8192,1,128]{2,1,0:T(2,128)(2,1)} reshape(bf16[32,2,16384]{2,1,0:T(2,128)(2,1)} %all-to-all-done.2) | data formatting | bytes 4194304
  350.8 10.5 %reshape.54 = bf16[8192,1,128]{2,1,0:T(2,128)(2,1)} reshape(bf16[32,2,16384]{2,1,0:T(2,128)(2,1)} %all-to-all-done.1) | data formatting | bytes 4194304
  370.5 10.5 %reshape.60 = bf16[8192,1,128]{2,1,0:T(2,128)(2,1)} reshape(bf16[32,2,16384]{2,1,0:T(2,128)(2,1)} %all-to-all-done.4) | data formatting | bytes 4194304
  395.1 15.0 %fusion.11 = (bf16[256,4096]{0,1:T(8,128)(2,1)S(1)}, f32[256,4096]{0,1:T(8,128)}) fusion(f32[1,128,32,256]{3,1,2,0:T(8,128)} %copy.73, f32[256,4102]{0,1:T(8,128)} %pad_convert_fusion.2, f32[256]{0:T(256)S(1)} %bitcast.204, f32[256]{0:T(256)S(1)} %bitcast.206, f32[256]{0:T(256)S(1)} %bitcast.208, f32[256]{0:T(256)S(1)} %bitcast.210, f32[256]{0:T(256)S(1)} %bitcast.212, ...), kind=kLoop, calls=%fused_computation.16 | loop fusion | flops 15728640 | bytes 39853056 | tf_op jit(solution)/shard_map/convert_element_type | solution.py:118
  410.1 20.8 %rev.8 = bf16[256,4096]{0,1:T(8,128)(2,1)} reverse(bf16[256,4096]{0,1:T(8,128)(2,1)S(1)} %get-tuple-element.38), dimensions={1} | reverse | bytes 4194304 | tf_op jit(solution)/shard_map/jit(_flip)/rev | solution.py:120
  435.4 11.9 %fusion.5 = f32[256,32,128]{2,1,0:T(8,128)} fusion(bf16[256,128,256]{2,1,0:T(8,128)(2,1)} %copy.68, bf16[256,31,128]{2,1,0:T(8,128)(2,1)} %bitcast.198, bf16[256,32,128]{2,1,0:T(8,128)(2,1)} %copy.90), kind=kOutput, calls=%fused_computation.8 | convolution fusion | flops 549453824 | bytes 25100288 | tf_op jit(solution)/shard_map/cbr,csr->cbs/dot_general | solution.py:65
  452.6 32.7 %rev.9 = f32[256,4096]{0,1:T(8,128)} reverse(f32[256,4096]{0,1:T(8,128)} %bitcast.180), dimensions={1} | reverse | bytes 8388608 | tf_op jit(solution)/shard_map/jit(_flip)/rev | solution.py:120
  489.6 21.9 %multiply_reduce_fusion = (f32[256]{0:T(256)S(1)}, f32[256]{0:T(256)S(1)}, f32[256]{0:T(256)S(1)}, f32[256]{0:T(256)S(1)}, f32[256]{0:T(256)S(1)}, /*index=5*/f3...) fusion(f32[256,4102]{0,1:T(8,128)S(1)} %get-tuple-element.78, f32[256,4096]{0,1:T(8,128)} %rev.9, ...), kind=kLoop, calls=%fused_computation.17 | loop fusion | flops 29358336 | bytes 71317504 | tf_op jit(solution)/shard_map/reduce_sum | solution.py:35
  511.5 21.7 %multiply_reduce_fusion.7 = (f32[256]{0:T(256)S(1)}, f32[256]{0:T(256)S(1)}, f32[256]{0:T(256)S(1)}, f32[256]{0:T(256)S(1)}, f32[256]{0:T(256)S(1)}, /*index=5*/...) fusion(f32[256,4102]{0,1:T(8,128)} %get-tuple-element.79, f32[256,4096]{0,1:T(8,128)} %rev.9, ...), kind=kLoop, calls=%fused_computation.24 | loop fusion | flops 29358336 | bytes 71317504 | tf_op jit(solution)/shard_map/reduce_sum | solution.py:35
  541.8 10.7 %fusion.18 = f32[256,32,128]{2,1,0:T(8,128)} fusion(bf16[256,128,256]{2,1,0:T(8,128)(2,1)} %copy.68, bf16[256,31,128]{2,1,0:T(8,128)(2,1)S(1)} %bitcast.160, bf16[256,32,128]{2,1,0:T(8,128)(2,1)S(1)} %copy.89), kind=kOutput, calls=%fused_computation.53 | convolution fusion | flops 549453824 | bytes 25100288 | tf_op jit(solution)/shard_map/cbr,csr->cbs/dot_general | solution.py:65
  557.8 17.6 %multiply_reduce_fusion.14 = (f32[256]{0:T(256)S(1)}, f32[256]{0:T(256)S(1)}, f32[256]{0:T(256)S(1)}, f32[256]{0:T(256)S(1)}, f32[256]{0:T(256)S(1)}, /*index=5*...) fusion(f32[256,4102]{0,1:T(8,128)} %pad_convert_fusion.2, ...), kind=kLoop, calls=%fused_computation.31 | loop fusion | flops 17824000 | bytes 48241664 | tf_op jit(solution)/shard_map/reduce_sum | solution.py:35
  575.4 25.3 %copy.108 = bf16[1,4096,256]{2,0,1:T(2,128)(2,1)} copy(bf16[1,4096,256]{2,1,0:T(8,128)(2,1)S(1)} %bitcast.181) | data formatting | bytes 4194304 | tf_op jit(solution)/shard_map/broadcast_in_dim | solution.py:139
  600.7 22.9 %reduce.4 = bf16[4096,256]{1,0:T(8,128)(2,1)} reduce(bf16[4096,1,256]{2,1,0:T(2,128)(2,1)} %bitcast.168, bf16[]{:T(256)} %broadcast.71), dimensions={1}, to_apply=%bitcast.155.reduce_sub_computation | reduce | bytes 4194306
  637.1 12.6 %fusion.13 = bf16[1,4096,256]{2,1,0:T(8,128)(2,1)S(1)} fusion(f32[256]{0:T(256)S(1)} %bitcast.205, f32[256]{0:T(256)S(1)} %bitcast.207, f32[256]{0:T(256)S(1)} %bitcast.209, f32[256]{0:T(256)S(1)} %bitcast.211, f32[256]{0:T(256)S(1)} %bitcast.213, f32[256,4096]{0,1:T(8,128)} %get-tuple-element.33, f32[256]{0:T(256)S(1)} %bitcast.215, f32[256]{0:T(256)S(1)} %bitcast.203), kind=kLoop, calls=%fused_computation.49 | loop fusion | flops 14680064 | bytes 6298624 | tf_op jit(solution)/shard_map/broadcast_in_dim | solution.py:139
  649.7 25.0 %copy.107 = bf16[1,4096,256]{2,0,1:T(2,128)(2,1)} copy(bf16[1,4096,256]{2,1,0:T(8,128)(2,1)S(1)} %fusion.13) | data formatting | bytes 4194304 | tf_op jit(solution)/shard_map/broadcast_in_dim | solution.py:139
  674.7 22.9 %reduce.5 = bf16[4096,256]{1,0:T(8,128)(2,1)} reduce(bf16[4096,1,256]{2,1,0:T(2,128)(2,1)} %bitcast.169, bf16[]{:T(256)} %broadcast.71), dimensions={1}, to_apply=%bitcast.154.reduce_sub_computation | reduce | bytes 4194306
  711.6 12.7 %fusion.14 = bf16[1,4096,256]{2,1,0:T(8,128)(2,1)S(1)} fusion(f32[256]{0:T(256)S(1)} %bitcast.241, f32[256]{0:T(256)S(1)} %bitcast.239, f32[256]{0:T(256)S(1)} %bitcast.237, f32[256]{0:T(256)S(1)} %bitcast.235, f32[256]{0:T(256)S(1)} %bitcast.233, f32[256,4096]{0,1:T(8,128)} %get-tuple-element.34, f32[256]{0:T(256)S(1)} %bitcast.231, f32[256]{0:T(256)S(1)} %bitcast.243), kind=kLoop, calls=%fused_computation.50 | loop fusion | flops 14680064 | bytes 6298624 | tf_op jit(solution)/shard_map/broadcast_in_dim | solution.py:139
  724.2 25.1 %copy.106 = bf16[1,4096,256]{2,0,1:T(2,128)(2,1)} copy(bf16[1,4096,256]{2,1,0:T(8,128)(2,1)S(1)} %fusion.14) | data formatting | bytes 4194304 | tf_op jit(solution)/shard_map/broadcast_in_dim | solution.py:139
  749.3 22.9 %reduce.6 = bf16[4096,256]{1,0:T(8,128)(2,1)} reduce(bf16[4096,1,256]{2,1,0:T(2,128)(2,1)} %bitcast.170, bf16[]{:T(256)} %broadcast.71), dimensions={1}, to_apply=%bitcast.153.reduce_sub_computation | reduce | bytes 4194306
  785.9 12.6 %fusion.15 = bf16[1,4096,256]{2,1,0:T(8,128)(2,1)S(1)} fusion(f32[256]{0:T(256)S(1)} %bitcast.219, f32[256]{0:T(256)S(1)} %bitcast.221, f32[256]{0:T(256)S(1)} %bitcast.223, f32[256]{0:T(256)S(1)} %bitcast.225, f32[256]{0:T(256)S(1)} %bitcast.227, f32[256,4096]{0,1:T(8,128)} %get-tuple-element.36, f32[256]{0:T(256)S(1)} %bitcast.229, f32[256]{0:T(256)S(1)} %bitcast.217), kind=kLoop, calls=%fused_computation.51 | loop fusion | flops 14680064 | bytes 6298624 | tf_op jit(solution)/shard_map/broadcast_in_dim | solution.py:139
  798.5 25.1 %copy.105 = bf16[1,4096,256]{2,0,1:T(2,128)(2,1)} copy(bf16[1,4096,256]{2,1,0:T(8,128)(2,1)S(1)} %fusion.15) | data formatting | bytes 4194304 | tf_op jit(solution)/shard_map/broadcast_in_dim | solution.py:139
  823.5 22.9 %reduce.7 = bf16[4096,256]{1,0:T(8,128)(2,1)} reduce(bf16[4096,1,256]{2,1,0:T(2,128)(2,1)} %bitcast.164, bf16[]{:T(256)} %broadcast.71), dimensions={1}, to_apply=%bitcast.152.reduce_sub_computation | reduce | bytes 4194306
  855.1 17.2 %fusion.16 = f32[256,128,256]{2,1,0:T(8,128)} fusion(bf16[256,32,128]{2,1,0:T(8,128)(2,1)} %copy.84, bf16[256,31,128]{2,1,0:T(8,128)(2,1)S(1)} %bitcast.161, bf16[256,32,128]{2,1,0:T(8,128)(2,1)S(1)} %copy.89), kind=kOutput, calls=%fused_computation.52 | convolution fusion | flops 549453824 | bytes 39780352 | tf_op jit(solution)/shard_map/cbs,cbr->csr/dot_general | solution.py:74
  872.3 31.7 %copy.100 = f32[32,8,128,256]{3,1,2,0:T(8,128)} copy(f32[32,8,128,256]{3,2,1,0:T(8,128)} %bitcast.158) | data formatting | bytes 67108864
  913.7 26.2 %fusion.35 = f32[256,128]{0,1:T(8,128)} fusion(f32[256,32768]{1,0:T(8,128)} %bitcast.159, s32[32768]{0:T(1024)S(1)} %copy-done.5, s32[32768]{0:T(1024)S(1)} %copy-done.7, s32[32768]{0:T(1024)S(1)} %copy-done.3, s32[32768]{0:T(1024)S(1)} %copy-done.9, pred[32768]{0:T(1024)(128)(4,1)S(1)} %copy-done.12, pred[32768]{0:T(1024)(128)(4,1)S(1)} %copy-done.14), kind=kOutput, calls=%fused_computation.77 | convolution fusion | flops 12905873408 | bytes 34275328 | tf_op jit(solution)/shard_map/cq,jq->cj/dot_general | solution.py:76
  940.0 12.7 %psum.7 = f32[3,256,7]{1,2,0:T(8,128)} all-reduce(f32[3,256,7]{1,2,0:T(8,128)S(1)} %pad_maximum_fusion), channel_id=1, replica_groups=mesh['dp'=4,'context'=32] {'dp'}, use_global_device_ids=true, to_apply=%region_22.23 | all-reduce | flops 5376 | bytes 43008 | tf_op jit(solution)/shard_map/psum | solution.py:162
  (109 shorter events, 308.5 us)
Async XLA Ops:
  64.4 71.3 %all-to-all-start = ((bf16[32,2,16384]{2,1,0:T(2,128)(2,1)}), bf16[32,2,16384]{2,1,0:T(2,128)(2,1)S(1)}, u32[]{:S(2)}, u32[]{:S(2)}) async-start(bf16[32,2,16384]{2,1,0:T(2,128)(2,1)} %reshape.51), calls=%async_computation | async-start | bytes 4194304 | tf_op jit(solution)/shard_map/all_to_all | solution.py:146
  135.7 69.6 %all-to-all-start.2 = ((bf16[32,2,16384]{2,1,0:T(2,128)(2,1)}), bf16[32,2,16384]{2,1,0:T(2,128)(2,1)}, u32[]{:S(2)}, u32[]{:S(2)}) async-start(bf16[32,2,16384]{2,1,0:T(2,128)(2,1)} %reshape.55), calls=%async_computation.2 | async-start | bytes 4194304 | tf_op jit(solution)/shard_map/all_to_all | solution.py:148
  201.3 13.5 %copy-start.10 = (f32[256,32]{0,1:T(8,128)S(1)}, f32[256,32]{0,1:T(8,128)}, u32[]{:S(2)}) copy-start(f32[256,32]{0,1:T(8,128)} %param.10) | copy-start | bytes 98308
  205.2 76.8 %all-to-all-start.1 = ((bf16[32,2,16384]{2,1,0:T(2,128)(2,1)}), bf16[32,2,16384]{2,1,0:T(2,128)(2,1)}, u32[]{:S(2)}, u32[]{:S(2)}) async-start(bf16[32,2,16384]{2,1,0:T(2,128)(2,1)} %reshape.53), calls=%async_computation.1 | async-start | bytes 4194304 | tf_op jit(solution)/shard_map/all_to_all | solution.py:147
  281.9 17.9 %copy-start.11 = (pred[32768]{0:T(1024)(128)(4,1)}, pred[32768]{0:T(1024)(128)(4,1)S(1)}, u32[]{:S(2)}) copy-start(pred[32768]{0:T(1024)(128)(4,1)S(1)} %get-tuple-element.69) | copy-start | bytes 98308
  281.9 17.9 %copy-start.13 = (pred[32768]{0:T(1024)(128)(4,1)}, pred[32768]{0:T(1024)(128)(4,1)S(1)}, u32[]{:S(2)}) copy-start(pred[32768]{0:T(1024)(128)(4,1)S(1)} %get-tuple-element.70) | copy-start | bytes 98308
  281.9 17.8 %copy-start.2 = (s32[32768]{0:T(1024)}, s32[32768]{0:T(1024)S(1)}, u32[]{:S(2)}) copy-start(s32[32768]{0:T(1024)S(1)} %get-tuple-element.65) | copy-start | bytes 393220
  281.9 17.8 %copy-start.4 = (s32[32768]{0:T(1024)}, s32[32768]{0:T(1024)S(1)}, u32[]{:S(2)}) copy-start(s32[32768]{0:T(1024)S(1)} %get-tuple-element.66) | copy-start | bytes 393220
  282.0 17.8 %copy-start.6 = (s32[32768]{0:T(1024)}, s32[32768]{0:T(1024)S(1)}, u32[]{:S(2)}) copy-start(s32[32768]{0:T(1024)S(1)} %get-tuple-element.67) | copy-start | bytes 393220
  282.0 17.8 %copy-start.8 = (s32[32768]{0:T(1024)}, s32[32768]{0:T(1024)S(1)}, u32[]{:S(2)}) copy-start(s32[32768]{0:T(1024)S(1)} %get-tuple-element.68) | copy-start | bytes 393220
  282.0 88.5 %all-to-all-start.4 = ((bf16[32,2,16384]{2,1,0:T(2,128)(2,1)}), bf16[32,2,16384]{2,1,0:T(2,128)(2,1)}, u32[]{:S(2)}, u32[]{:S(2)}) async-start(bf16[32,2,16384]{2,1,0:T(2,128)(2,1)} %reshape.59), calls=%async_computation.4 | async-start | bytes 4194304 | tf_op jit(solution)/shard_map/all_to_all | solution.py:152
  299.8 23.0 %copy-start.15 = (f32[3,256,7]{1,2,0:T(8,128)S(1)}, f32[3,256,7]{1,2,0:T(8,128)}, u32[]{:S(2)}) copy-start(f32[3,256,7]{1,2,0:T(8,128)} %param.11) | copy-start | bytes 64516
  410.1 25.3 %copy-start = (bf16[256,4096]{0,1:T(8,128)(2,1)}, bf16[256,4096]{0,1:T(8,128)(2,1)S(1)}, u32[]{:S(2)}) copy-start(bf16[256,4096]{0,1:T(8,128)(2,1)S(1)} %get-tuple-element.38) | copy-start | bytes 6291460
  452.6 32.7 %copy-start.1 = (bf16[1,32,128,256]{3,2,1,0:T(8,128)(2,1)S(1)}, bf16[1,32,128,256]{3,2,1,0:T(8,128)(2,1)}, u32[]{:S(2)}) copy-start(bf16[1,32,128,256]{3,2,1,0:T(8,128)(2,1)} %copy.66) | copy-start | bytes 6291460
  627.5 74.1 %all-to-all-start.3 = ((bf16[32,2,16384]{2,1,0:T(2,128)(2,1)}), bf16[32,2,16384]{2,1,0:T(2,128)(2,1)}, u32[]{:S(2)}, u32[]{:S(2)}) async-start(bf16[32,2,16384]{2,1,0:T(2,128)(2,1)} %reshape.57), calls=%async_computation.3 | async-start | bytes 4194304 | tf_op jit(solution)/shard_map/all_to_all | solution.py:151
  701.6 74.6 %all-to-all-start.5 = ((bf16[32,2,16384]{2,1,0:T(2,128)(2,1)}), bf16[32,2,16384]{2,1,0:T(2,128)(2,1)}, u32[]{:S(2)}, u32[]{:S(2)}) async-start(bf16[32,2,16384]{2,1,0:T(2,128)(2,1)} %reshape.61), calls=%async_computation.5 | async-start | bytes 4194304 | tf_op jit(solution)/shard_map/all_to_all | solution.py:157
  776.2 127.9 %all-to-all-start.6 = ((bf16[32,2,16384]{2,1,0:T(2,128)(2,1)}), bf16[32,2,16384]{2,1,0:T(2,128)(2,1)}, u32[]{:S(2)}, u32[]{:S(2)}) async-start(bf16[32,2,16384]{2,1,0:T(2,128)(2,1)} %reshape.63), calls=%async_computation.6 | async-start | bytes 4194304 | tf_op jit(solution)/shard_map/all_to_all | solution.py:158
  904.0 9.6 copy-start.3
  904.0 9.6 copy-start.5
  904.0 9.6 copy-start.7
  904.0 9.6 copy-start.9
  904.0 9.7 copy-start.12
  904.0 9.7 copy-start.14
  904.1 116.1 %all-to-all-start.7 = ((bf16[32,2,16384]{2,1,0:T(2,128)(2,1)}), bf16[32,2,16384]{2,1,0:T(2,128)(2,1)S(1)}, u32[]{:S(2)}, u32[]{:S(2)}) async-start(bf16[32,2,16384]{2,1,0:T(2,128)(2,1)} %reshape.65), calls=%async_computation.7 | async-start | bytes 4194304 | tf_op jit(solution)/shard_map/all_to_all | solution.py:159
  913.6 122.8 %reduce-scatter.2.cloned.1.call-start = ((), (), s32[]{:S(2)}) async-start(), calls=%async_computation.9 | async-start | bytes 163840 | tf_op jit(solution)/shard_map/reduce_scatter | solution.py:161
Sparse Core Ops, SparseCore 0:
  940.1 20.9 reduce-scatter.1
where the time goes:
time: 1060 us; the launch traced here: 1040 us
  local copies, waits for them, and re-layouts  444 us (42%)
  other arithmetic  412 us (39%)
  starting transfers between devices  78.8 us (7%)
  matrix products  74.2 us (7%)
  blocking collectives  19.9 us (2%)
  between operations  14.9 us (1%)
    unnamed x8, other arithmetic  276 us
    unnamed x65, local copies, waits for them, and re-layouts  214 us
    broadcast_in_dim x4, local copies, waits for them, and re-layouts, to_tokens(): return rows.T[None]  100 us
    reduce_sum x3, other arithmetic, short_weight(): columns.append(jnp.sum(grads * padded[:, start:start + count], axis=1))  61.1 us
    rev x2, local copies, waits for them, and re-layouts, channel_backward(): grad_u = jnp.flip(medium_conv(jnp.flip(grad_z, 1), rim_med, toep), 1)  53.4 us
    broadcast_in_dim x3, other arithmetic, to_tokens(): return rows.T[None]  37.9 us
    dot_general x1, matrix products, medium_weight(): jnp.einsum('cq,jq->cj', flat, table, precision=lax.Precision.HIGHEST, pre...  26.2 us
    reshape x1, local copies, waits for them, and re-layouts, toeplitz(): return flat.reshape(taps.shape[0], size, 2 * size)  23 us
  transfers between devices with their start and end apart: 9, of which 0 were waited for; matrix products, arithmetic and copies ran while one was open for 59% of the time, Pallas kernels for 0%

commit v1 on v0

v1 whole, which is shorter than its diff:
```python
import functools

import jax
import jax.numpy as jnp
import numpy as np
from jax import lax
from jax.experimental import pallas as pl
from jax.experimental.pallas import tpu as pltpu
from jax.sharding import PartitionSpec as P

BF = jnp.bfloat16
F32 = jnp.float32
LANES = 128
ROW = 8


def phases(tokens, size):
    angle = 2.0 * np.pi * (np.arange(size // 2)[:, None] + 0.5) * tokens[None, :] / size
    return np.concatenate([np.cos(angle), np.sin(angle)], axis=0)


def split_host(table):
    high = table.astype(BF)
    low = (table - high.astype(np.float64)).astype(BF)
    return jnp.asarray(high), jnp.asarray(low)


def transforms(block, width):
    size = 2 * block
    reach = width - 1
    own = np.arange(block)
    behind = np.where(own < reach, own + block, own - block)
    ahead = own + block
    rows = np.arange(block + ROW)
    forward = [
        split_host(phases(np.concatenate([own, behind]), size)),
        split_host(phases(own, size)),
        split_host(phases(ahead, size)),
    ]
    inverse = split_host(phases(rows, size).T * (2.0 / size))
    return forward, inverse


def split_bf(x):
    high = x.astype(BF)
    low = (x - high.astype(F32)).astype(BF)
    return high, low


def dot(a, b):
    return jnp.dot(a, b, preferred_element_type=F32)


def row_of(ref, index, lanes):
    return ref[pl.ds(index, 1), lanes]


def load_padded(dst, own_ref, before, after, lanes, block):
    dst[pl.ds(0, ROW), :] = before
    dst[pl.ds(ROW, block), :] = own_ref[0, :, lanes].astype(F32)
    dst[pl.ds(ROW + block, ROW), :] = after


def causal(src, taps, first, width, lanes, rows):
    total = None
    for offset in range(width):
        term = row_of(taps, first + offset, lanes) * src[pl.ds(ROW - offset, rows), :]
        total = term if total is None else total + term
    return total


def make_products(block, width, cols, q, k, v, go, back, fore, taps, u_out, dz_out, x_q, x_k, x_v):
    for col in range(cols):
        lanes = pl.ds(col * LANES, LANES)
        for which, (src, dst) in enumerate(((q, x_q), (k, x_k), (v, x_v))):
            load_padded(
                dst.at[col],
                src,
                back[which, :, lanes].astype(F32),
                fore[which, :, lanes].astype(F32),
                lanes,
                block,
            )
        k_s = causal(x_k.at[col], taps, width, width, lanes, block)
        v_s = causal(x_v.at[col], taps, 2 * width, width, lanes, block)
        u_out[:, lanes] = (k_s * v_s).astype(BF)
        q_s = causal(x_q.at[col], taps, 0, width, lanes, block + ROW)
        dz_out[0:block, lanes] = (go[0, :, lanes].astype(F32) * q_s[0:block]).astype(BF)
        dz_out[block : block + ROW, lanes] = (
            fore[3, :, lanes].astype(F32) * q_s[block : block + ROW]
        ).astype(BF)


def mixer(
    block,
    width,
    cols,
    q,
    k,
    v,
    go,
    back,
    fore,
    taps,
    u_prev,
    dz_next,
    h_ref,
    fx_hi,
    fx_lo,
    fo_hi,
    fo_lo,
    fa_hi,
    fa_lo,
    in_hi,
    in_lo,
    mixed,
    g_q,
    g_k,
    g_v,
    g_med,
    g_short,
    x_q,
    x_k,
    x_v,
    s_q,
    s_k,
    s_v,
    g_pad,
    h_pad,
    h_flip,
    z_pad,
    window,
    dz_own,
    edge_u,
    edge_z,
    spec_u,
    spec_h,
    spec_d,
    spec_w,
    prod_hi,
    prod_lo,
):
    rows = block + ROW
    half = block
    rank = lax.broadcasted_iota(jnp.int32, (ROW, LANES), 0)
    for col in range(cols):
        lanes = pl.ds(col * LANES, LANES)
        for which, (src, dst) in enumerate(((q, x_q), (k, x_k), (v, x_v))):
            load_padded(
                dst.at[col],
                src,
                back[which, :, lanes].astype(F32),
                fore[which, :, lanes].astype(F32),
                lanes,
                block,
            )
        q_s = causal(x_q.at[col], taps, 0, width, lanes, rows)
        s_q[col] = q_s
        dz = (go[0, :, lanes].astype(F32) * q_s[0:block]).astype(BF)
        dz_own[:, lanes] = dz
        z_pad[col, 0:ROW, :] = jnp.zeros((ROW, LANES), F32)
        z_pad[col, ROW : 2 * ROW, :] = dz[0:ROW].astype(F32)
        k_s = causal(x_k.at[col], taps, width, width, lanes, rows)
        s_k[col] = k_s
        v_s = causal(x_v.at[col], taps, 2 * width, width, lanes, rows)
        s_v[col] = v_s
        u = (k_s * v_s).astype(BF)
        window[0:block, lanes] = u[0:block]
        u_after = u[block:rows].astype(F32)
        first = u_prev[0 : 2 * ROW, lanes]
        u_before = first.astype(F32)[0:ROW]
        patched = jnp.where(rank < width - 1, u_after, u_before)
        window[block : block + 2 * ROW, lanes] = jnp.concatenate(
            [patched, first.astype(F32)[ROW : 2 * ROW]], axis=0
        ).astype(BF)
        window[block + 2 * ROW : 2 * block, lanes] = u_prev[2 * ROW : block, lanes]
        edge_u[col] = u_before + u_after
        edge_z[col] = dz_next[block : block + ROW, lanes].astype(F32) + dz[0:ROW].astype(F32)
        taps_h = h_ref[0, :, lanes].astype(F32)
        h_pad[col, 0 : 2 * ROW, :] = taps_h[block - 2 * ROW : block]
        h_pad[col, 2 * ROW : 3 * ROW, :] = jnp.zeros((ROW, LANES), F32)
        h_flip[col, 0:ROW, :] = jnp.zeros((ROW, LANES), F32)
        for place in range(ROW):
            h_flip[col, ROW + place : ROW + place + 1, :] = h_pad[
                col, 2 * ROW - 1 - place : 2 * ROW - place, :
            ]

    x = window[...]
    spec_u[...] = dot(fx_hi[...], x) + dot(fx_lo[...], x)
    h = h_ref[0]
    spec_h[...] = dot(fo_hi[...], h) + dot(fo_lo[...], h)
    d = dz_own[...]
    spec_d[...] = dot(fo_hi[...], d) + dot(fo_lo[...], d)
    a = dz_next[0:block, :]
    spec_w[...] = spec_d[...] + (dot(fa_hi[...], a) + dot(fa_lo[...], a))

    def inverse(slot, count):
        high, low = prod_hi[slot], prod_lo[slot]
        top, rest = in_hi[0:count, :], in_lo[0:count, :]
        return dot(top, high) + (dot(rest, high) + dot(top, low))

    def store(slot, cos_part, sin_part):
        for place, part in ((0, cos_part), (half, sin_part)):
            high, low = split_bf(part)
            prod_hi[slot, place : place + half, :] = high
            prod_lo[slot, place : place + half, :] = low

    uc, us = spec_u[0:half, :], spec_u[half:, :]
    hc, hs = spec_h[0:half, :], spec_h[half:, :]
    store(0, uc * hc - us * hs, uc * hs + us * hc)
    wc, ws = spec_w[0:half, :], spec_w[half:, :]
    store(1, wc * hc + ws * hs, ws * hc - wc * hs)
    dc, ds = spec_d[0:half, :], spec_d[half:, :]
    store(2, dc * uc + ds * us, ds * uc - dc * us)

    z_all = inverse(0, rows)
    du_all = inverse(1, rows)
    gm_all = inverse(2, block)

    for col in range(cols):
        lanes = pl.ds(col * LANES, LANES)
        lo, hi = col * LANES, (col + 1) * LANES
        z = z_all[:, lo:hi]
        du = du_all[:, lo:hi]
        gm = gm_all[:, lo:hi]
        z_fix = jnp.zeros((ROW, LANES), F32)
        g_fix = jnp.zeros((ROW, LANES), F32)
        for place in range(1, width - 1):
            held = edge_u[col, place : place + 1, :]
            z_fix = z_fix + held * h_pad[col, pl.ds(2 * ROW - place, ROW), :]
            g_fix = g_fix + held * z_pad[col, pl.ds(place, ROW), :]
        du_fix = jnp.zeros((ROW, LANES), F32)
        for place in range(width - 2):
            held = edge_z[col, place : place + 1, :]
            du_fix = du_fix + held * h_flip[col, pl.ds(ROW - 1 - place, ROW), :]
        z = jnp.concatenate([z[0:ROW] + z_fix, z[ROW:]], axis=0)
        du = jnp.concatenate([du[0:block], du[block:] + du_fix], axis=0)
        g_med[0, 0 : block - ROW, lanes] = gm[0 : block - ROW]
        g_med[0, block - ROW : block, lanes] = gm[block - ROW : block] + g_fix
        mixed[0, :, lanes] = (s_q[col, 0:block, :] * z[0:block]).astype(BF)
        g_pad[0, 0:block, :] = go[0, :, lanes].astype(F32) * z[0:block]
        g_pad[0, block:rows, :] = fore[3, :, lanes].astype(F32) * z[block:rows]
        g_pad[1] = du * s_v[col]
        g_pad[2] = du * s_k[col]
        for which, (src, out) in enumerate(((x_q, g_q), (x_k, g_k), (x_v, g_v))):
            values = src[col, ROW : ROW + block, :]
            total = None
            for offset in range(width):
                moved = g_pad[which, pl.ds(offset, block), :]
                term = row_of(taps, which * width + offset, lanes) * moved
                total = term if total is None else total + term
                g_short[0, which * width + offset : which * width + offset + 1, lanes] = jnp.sum(
                    values * moved, axis=0, keepdims=True
                )
            out[0, :, lanes] = total.astype(BF)


def halo_pairs(count):
    return [(i, i + 1) for i in range(count - 1)], [(i + 1, i) for i in range(count - 1)]


def per_device(n_context, n_dp, query_in, key_in, value_in, grad_out, med_filter, short_filter):
    _, block, width_all = query_in.shape
    group, taps_own = med_filter.shape
    width = short_filter.shape[2]
    size = 2 * block
    ahead, behind = halo_pairs(n_context)
    forward, inverse = transforms(block, width)

    back = jnp.concatenate([x[:, block - ROW :] for x in (query_in, key_in, value_in)], axis=0)
    fore = jnp.concatenate([x[:, :ROW] for x in (query_in, key_in, value_in, grad_out)], axis=0)
    back = lax.ppermute(back, "context", ahead)
    fore = lax.ppermute(fore, "context", behind)

    h_all, taps = share_filters(med_filter, short_filter)

    tile = 4 * LANES
    cols = tile // LANES
    tokens = pl.BlockSpec((1, block, tile), lambda i: (0, 0, i))
    flat = lambda height: pl.BlockSpec((height, tile), lambda i: (0, i))
    stack = lambda count: pl.BlockSpec((count, ROW, tile), lambda i: (0, 0, i))
    padded = pltpu.VMEM((cols, block + 2 * ROW, LANES), F32)
    u, dz = pl.pallas_call(
        functools.partial(make_products, block, width, cols),
        grid=(width_all // tile,),
        in_specs=[tokens] * 4 + [stack(3), stack(4), flat(taps.shape[0])],
        out_specs=[flat(block), flat(block + ROW)],
        out_shape=[
            jax.ShapeDtypeStruct((block, width_all), BF),
            jax.ShapeDtypeStruct((block + ROW, width_all), BF),
        ],
        scratch_shapes=[padded] * 3,
        name="products",
    )(query_in, key_in, value_in, grad_out, back, fore, taps)

    u_prev = lax.ppermute(u, "context", ahead)
    dz_next = lax.ppermute(dz, "context", behind)

    tile = group
    cols = tile // LANES
    tokens = pl.BlockSpec((1, block, tile), lambda i: (0, 0, i))
    flat = lambda height: pl.BlockSpec((height, tile), lambda i: (0, i))
    stack = lambda count: pl.BlockSpec((count, ROW, tile), lambda i: (0, 0, i))
    whole = lambda x: pl.BlockSpec(x.shape, lambda i: (0,) * x.ndim)
    per_group = lambda height: pl.BlockSpec((1, height, tile), lambda i: (i, 0, 0))
    tables = [part for pair in forward + [inverse] for part in pair]
    padded = pltpu.VMEM((cols, block + 2 * ROW, LANES), F32)
    shifted = pltpu.VMEM((cols, block + ROW, LANES), F32)
    held_short = 3 * ROW
    mixed, grad_q, grad_k, grad_v, part_med, part_short = pl.pallas_call(
        functools.partial(mixer, block, width, cols),
        grid=(width_all // tile,),
        in_specs=[tokens] * 4
        + [stack(3), stack(4), flat(taps.shape[0]), flat(block), flat(block + ROW), per_group(block)]
        + [whole(x) for x in tables],
        out_specs=[tokens] * 4 + [per_group(block), per_group(held_short)],
        out_shape=[jax.ShapeDtypeStruct(query_in.shape, BF)] * 4
        + [
            jax.ShapeDtypeStruct((n_context, block, group), F32),
            jax.ShapeDtypeStruct((n_context, held_short, group), F32),
        ],
        scratch_shapes=[
            padded,
            padded,
            padded,
            shifted,
            shifted,
            shifted,
            pltpu.VMEM((3, block + ROW, LANES), F32),
            pltpu.VMEM((cols, 3 * ROW, LANES), F32),
            pltpu.VMEM((cols, 2 * ROW, LANES), F32),
            pltpu.VMEM((cols, 2 * ROW, LANES), F32),
            pltpu.VMEM((size, tile), BF),
            pltpu.VMEM((block, tile), BF),
            pltpu.VMEM((cols, ROW, LANES), F32),
            pltpu.VMEM((cols, ROW, LANES), F32),
            pltpu.VMEM((size, tile), F32),
            pltpu.VMEM((size, tile), F32),
            pltpu.VMEM((size, tile), F32),
            pltpu.VMEM((size, tile), F32),
            pltpu.VMEM((3, size, tile), BF),
            pltpu.VMEM((3, size, tile), BF),
        ],
        name="mixer",
    )(
        query_in,
        key_in,
        value_in,
        grad_out,
        back,
        fore,
        taps,
        u_prev,
        dz_next,
        h_all,
        *tables,
    )

    grad_med, grad_short = reduce_filters(part_med, part_short, n_dp, width, taps_own)
    return (mixed, grad_q, grad_k, grad_v, grad_med, grad_short)


def share_filters(med_filter, short_filter):
    mine = med_filter.astype(BF).T
    column = lax.all_gather(mine, "dp", axis=0, tiled=True)
    n = lax.axis_size("context")
    h_all = lax.all_to_all(jnp.broadcast_to(column, (n,) + column.shape), "context", 0, 0)
    short = short_filter.transpose(0, 2, 1).reshape(-1, short_filter.shape[1])
    short = jnp.pad(short, ((0, -short.shape[0] % ROW), (0, 0)))
    taps = lax.all_to_all(jnp.broadcast_to(short, (n,) + short.shape), "context", 0, 0)
    return h_all, taps.transpose(1, 0, 2).reshape(short.shape[0], -1)


def reduce_filters(part_med, part_short, n_dp, width, taps_own):
    med = jnp.sum(lax.all_to_all(part_med, "context", 0, 0), axis=0)
    med = lax.psum_scatter(med, "dp", scatter_dimension=0, tiled=True)
    short = jnp.sum(lax.all_to_all(part_short, "context", 0, 0), axis=0)
    short = lax.psum(short, "dp")
    group = short.shape[1]
    return med.T, short[: 3 * width].reshape(3, width, group).transpose(0, 2, 1)


def solution(mesh):
    tokens = P("dp", "context", None)
    filters = (P("context", "dp"), P(None, "context", None))
    return jax.shard_map(
        functools.partial(per_device, mesh.shape["context"], mesh.shape["dp"]),
        mesh=mesh,
        in_specs=(tokens,) * 4 + filters,
        out_specs=(tokens,) * 4 + filters,
        check_vma=False,
    )
```

time: 1060 us -> 295 us (0.28); the launches traced: 1040 us -> 294 us
  local copies, waits for them, and re-layouts: 444 us -> 8.15 us
  other arithmetic: 412 us -> 3.3 us
  blocking collectives: 19.9 us -> 154 us
  matrix products: 74.2 us -> 0 us
  Pallas kernels: 0 us -> 61.8 us
  starting transfers between devices: 78.8 us -> 29.2 us
  waiting for transfers between devices: 0.04 us -> 23 us
    unnamed x8 -> x0, other arithmetic: 276 us -> none
    unnamed x65 -> x10, local copies, waits for them, and re-layouts: 214 us -> 2.37 us
    all_to_all x0 -> x2, blocking collectives: none -> 133 us  [the longest x1 78.3 us: share_filters(): lax.all_to_all(jnp.broadcast_to(column, (n,) + column.shape), 'context',...]
    broadcast_in_dim x4 -> x2, local copies, waits for them, and re-layouts: 100 us -> 1.16 us  [the longest x1 0.93 us: share_filters(): jnp.broadcast_to(short, (n,) + short.shape)]
    dot_general x5 -> x0, matrix products: 74.2 us -> none  [the longest x1 26.2 us: medium_weight(): jnp.einsum('cq,jq->cj', flat, table, precision=lax.Precision.HIGHEST, pre...]
    pallas_call x0 -> x2, Pallas kernels: none -> 61.8 us  [the longest x1 47.5 us: per_device(): pl.pallas_call(functools.partial(mixer, block, width, cols), grid=(width_...]
    all_to_all x8 -> x2, starting transfers between devices: 78.8 us -> 17.8 us  [the longest x1 12.2 us: share_filters(): lax.all_to_all(jnp.broadcast_to(short, (n,) + short.shape), 'context', 0, 0)]
    reduce_sum x3 -> x2, other arithmetic: 61.1 us -> 3.18 us  [the longest x1 3.12 us: reduce_filters(): med = jnp.sum(lax.all_to_all(part_med, 'context', 0, 0), axis=0)]
  transfers between devices with their start and end apart: 9 -> 7, of which waited for: 0 -> 3; matrix products, arithmetic and copies ran while one was open for 59% -> 2% of each run, Pallas kernels for 0% -> 0%
where the time goes in v1:
time: 295 us; the launch traced here: 294 us
  blocking collectives  154 us (52%)
  Pallas kernels  61.8 us (21%)
  starting transfers between devices  29.2 us (10%)
  waiting for transfers between devices  23 us (8%)
  between operations  14.2 us (5%)
  local copies, waits for them, and re-layouts  8.15 us (3%)
  other arithmetic  3.3 us (1%)
    all_to_all x1, blocking collectives, share_filters(): lax.all_to_all(jnp.broadcast_to(column, (n,) + column.shape), 'context',...  78.3 us
    all_to_all x1, blocking collectives, reduce_filters(): med = jnp.sum(lax.all_to_all(part_med, 'context', 0, 0), axis=0)  54.7 us
    pallas_call x1, Pallas kernels, per_device(): pl.pallas_call(functools.partial(mixer, block, width, cols), grid=(width_...  47.5 us
    psum x1, blocking collectives, reduce_filters(): short = lax.psum(short, 'dp')  14.3 us
    pallas_call x1, Pallas kernels, per_device(): pl.pallas_call(functools.partial(make_products, block, width, cols), grid...  14.3 us
    all_to_all x1, starting transfers between devices, share_filters(): lax.all_to_all(jnp.broadcast_to(short, (n,) + short.shape), 'context', 0, 0)  12.2 us
    all_to_all x1, waiting for transfers between devices, share_filters(): lax.all_to_all(jnp.broadcast_to(short, (n,) + short.shape), 'context', 0, 0)  10.4 us
    all_to_all x1, waiting for transfers between devices, reduce_filters(): short = jnp.sum(lax.all_to_all(part_short, 'context', 0, 0), axis=0)  9.15 us
  transfers between devices with their start and end apart: 7, of which 3 were waited for; matrix products, arithmetic and copies ran while one was open for 2% of the time, Pallas kernels for 0%

profile of v1, /device:TPU:1, one launch (start us, length us, event | category | flops | bytes accessed | tf_op | source)
XLA Modules:
  0.0 293.6 jit_solution(14525296687444401635)
XLA Ops:
  7.2 0.9 slice.30
  8.1 1.0 fusion.2
  9.1 1.1 fusion
  10.2 0.1 pad_maximum_fusion
  10.3 1.3 collective-permute-start.1
  11.6 0.9 broadcast_in_dim.6
  12.6 12.2 %all-to-all-start = ((f32[32,24,256]{2,1,0:T(8,128)}), f32[32,24,256]{2,1,0:T(8,128)S(1)}, u32[]{:S(2)}, u32[]{:S(2)}) async-start(f32[32,24,256]{2,1,0:T(8,128)} %broadcast_in_dim.6), calls=%async_computation | async-start | bytes 1572864 | tf_op jit(solution)/shard_map/all_to_all | solution.py:370
  24.9 3.2 %collective-permute-start = (bf16[3,8,8192]{2,1,0:T(8,128)(2,1)S(1)}, bf16[3,8,8192]{2,1,0:T(8,128)(2,1)S(1)}, u32[]{:S(2)}, u32[]{:S(2)}) collective-permute-start(bf16[3,8,8192]{2,1,0:T(8,128)(2,1)S(1)} %pad_maximum_fusion.1), channel_id=1, source_target_pairs={{0,1},{1,2},{2,3},{3,4},{4,5},{5,6},{6,7},{7,8},{8,9},{9,10},{10,1... | collective-permute-start | bytes 1179656 | tf_op jit(solution)/shard_map/ppermute | solution.py:272
  28.0 10.4 %all-to-all-done = f32[32,24,256]{2,1,0:T(8,128)S(1)} async-done(((f32[32,24,256]{2,1,0:T(8,128)}), f32[32,24,256]{2,1,0:T(8,128)S(1)}, u32[]{:S(2)}, u32[]{:S(2)}) %all-to-all-start) | async-done | bytes 786464 | tf_op jit(solution)/shard_map/all_to_all | solution.py:370
  38.5 1.0 copy.21
  39.4 3.4 %collective-permute-done.back = bf16[3,8,8192]{2,1,0:T(8,128)(2,1)S(1)} collective-permute-done((bf16[3,8,8192]{2,1,0:T(8,128)(2,1)S(1)}, bf16[3,8,8192]{2,1,0:T(8,128)(2,1)S(1)}, u32[]{:S(2)}, u32[]{:S(2)}) %collective-permute-start) | collective-permute-done | bytes 393248 | tf_op jit(solution)/shard_map/ppermute | solution.py:272
  42.8 0.0 collective-permute-done.1.fore
  42.8 0.8 copy-done.2
  43.6 0.2 copy-done.1
  43.8 14.3 %products.1 = (bf16[128,8192]{1,0:T(8,128)(2,1)}, bf16[136,8192]{1,0:T(8,128)(2,1)}) custom-call(bf16[1,128,8192]{2,1,0:T(8,128)(2,1)} %q.3, bf16[1,128,8192]{2,1,0:T(8,128)(2,1)} %k.3, bf16[1,128,8192]{2,1,0:T(8,128)(2,1)} %v.3, bf16[1,128,8192]{2,1,0:T(8,128)(2,1)} %go.3, bf16[3,8,8192]{2,1,0:T(8,128)(2,1)} %copy-done.2, bf16[4,8,8192]{2,1,0:T(8,128)(2,1)} %copy-done.1, ...), custom_call_target="tpu_custom_call" | custom-call | tf_op jit(solution)/shard_map/products/pallas_call | solution.py:283
  58.1 5.6 %collective-permute-start.2 = (bf16[128,8192]{1,0:T(8,128)(2,1)}, bf16[128,8192]{1,0:T(8,128)(2,1)}, u32[]{:S(2)}, u32[]{:S(2)}) collective-permute-start(bf16[128,8192]{1,0:T(8,128)(2,1)} %get-tuple-element.14), channel_id=1, source_target_pairs={{0,1},{1,2},{2,3},{3,4},{4,5},{5,6},{6,7},{7,8},{8,9},{9,10},{10,1... | collective-permute-start | bytes 6291464 | tf_op jit(solution)/shard_map/ppermute | solution.py:296
  63.7 1.3 collective-permute-start.3
  65.0 6.6 %all_gather.3 = bf16[128,256]{1,0:T(8,128)(2,1)S(1)} all-gather(bf16[32,256]{1,0:T(8,128)(2,1)S(1)} %convert_bitcast_fusion), channel_id=1, replica_groups=mesh['dp'=4,'context'=32] {'dp'}, dimensions={0}, use_global_device_ids=true | all-gather | bytes 81920 | tf_op jit(solution)/shard_map/all_gather | solution.py:365
  71.6 0.2 broadcast_in_dim.7
  71.8 78.3 %all_to_all.20.h_ref = bf16[32,128,256]{2,1,0:T(8,128)(2,1)} all-to-all(bf16[32,128,256]{2,1,0:T(8,128)(2,1)S(1)} %broadcast_in_dim.7), channel_id=1, replica_groups=mesh['dp'=4,'context'=32] {'context'}, dimensions={0} | all-to-all | bytes 4194304 | tf_op jit(solution)/shard_map/all_to_all | solution.py:367
  150.2 0.0 collective-permute-done.3.dz_next
  150.2 1.4 copy-done
  151.6 47.5 %mixer.1 = (bf16[1,128,8192]{2,1,0:T(8,128)(2,1)}, bf16[1,128,8192]{2,1,0:T(8,128)(2,1)}, bf16[1,128,8192]{2,1,0:T(8,128)(2,1)}, bf16[1,128,8192]{2,1,0:T(8,128)...) custom-call(bf16[1,128,8192]{2,1,0:T(8,128)(2,1)} %q.3, bf16[1,128,8192]{2,1,0:T(8,128)(2,1)} %k.3, ...), custom_call_target="tpu_custom_call" | custom-call | tf_op jit(solution)/shard_map/mixer/pallas_call | solution.py:310
  199.1 54.7 %all_to_all.21 = f32[32,128,256]{2,1,0:T(8,128)} all-to-all(f32[32,128,256]{2,1,0:T(8,128)} %get-tuple-element.20), channel_id=1, replica_groups=mesh['dp'=4,'context'=32] {'context'}, dimensions={0} | all-to-all | bytes 8388608 | tf_op jit(solution)/shard_map/all_to_all | solution.py:375
  253.8 5.6 %all-to-all-start.3 = ((f32[32,24,256]{2,1,0:T(8,128)}), f32[32,24,256]{2,1,0:T(8,128)S(1)}, u32[]{:S(2)}, u32[]{:S(2)}) async-start(f32[32,24,256]{2,1,0:T(8,128)} %get-tuple-element.21), calls=%async_computation.4 | async-start | bytes 1572864 | tf_op jit(solution)/shard_map/all_to_all | solution.py:377
  259.4 0.0 reduce-scatter.2.cloned.1.call-start
  259.5 3.1 %reduce_sum.18 = f32[128,256]{1,0:T(8,128)} reduce(f32[32,128,256]{2,1,0:T(8,128)} %all_to_all.21, f32[]{:T(128)} %constant.9.clone.1), dimensions={0}, to_apply=%region_0.1 | reduce | flops 1015808 | bytes 4325380 | tf_op jit(solution)/shard_map/reduce_sum | solution.py:375
  262.6 0.0 reduce-scatter.2.cloned.1.call-update
  262.6 9.2 %all-to-all-done.3 = f32[32,24,256]{2,1,0:T(8,128)S(1)} async-done(((f32[32,24,256]{2,1,0:T(8,128)}), f32[32,24,256]{2,1,0:T(8,128)S(1)}, u32[]{:S(2)}, u32[]{:S(2)}) %all-to-all-start.3) | async-done | bytes 786464 | tf_op jit(solution)/shard_map/all_to_all | solution.py:377
  271.8 0.1 reduce_sum.19
  271.8 14.3 %psum.7 = f32[24,256]{1,0:T(8,128)S(1)} all-reduce(f32[24,256]{1,0:T(8,128)S(1)} %reduce_sum.19), channel_id=1, replica_groups=mesh['dp'=4,'context'=32] {'dp'}, use_global_device_ids=true, to_apply=%region_3.4 | all-reduce | flops 6144 | bytes 49152 | tf_op jit(solution)/shard_map/psum | solution.py:378
  286.1 0.6 reshape.23
  (13 shorter events, 0.1 us)
Async XLA Ops:
  7.2 4.4 %copy-start.4 = (f32[3,256,7]{1,2,0:T(8,128)S(1)}, f32[3,256,7]{1,2,0:T(8,128)}, u32[]{:S(2)}) copy-start(f32[3,256,7]{1,2,0:T(8,128)} %param.19) | copy-start | bytes 64516
  10.3 32.5 %collective-permute-start.1 = (bf16[4,8,8192]{2,1,0:T(8,128)(2,1)S(1)}, bf16[4,8,8192]{2,1,0:T(8,128)(2,1)S(1)}, u32[]{:S(2)}, u32[]{:S(2)}) collective-permute-start(bf16[4,8,8192]{2,1,0:T(8,128)(2,1)S(1)} %pad_maximum_fusion), channel_id=1, source_target_pairs={{1,0},{2,1},{3,2},{4,3},{5,4},{6,5},{7,6},{8,7},{9,8},{10,9},{11,1... | collective-permute-start | bytes 1572872 | tf_op jit(solution)/shard_map/ppermute | solution.py:273
  12.6 25.9 %all-to-all-start = ((f32[32,24,256]{2,1,0:T(8,128)}), f32[32,24,256]{2,1,0:T(8,128)S(1)}, u32[]{:S(2)}, u32[]{:S(2)}) async-start(f32[32,24,256]{2,1,0:T(8,128)} %broadcast_in_dim.6), calls=%async_computation | async-start | bytes 1572864 | tf_op jit(solution)/shard_map/all_to_all | solution.py:370
  24.9 17.9 %collective-permute-start = (bf16[3,8,8192]{2,1,0:T(8,128)(2,1)S(1)}, bf16[3,8,8192]{2,1,0:T(8,128)(2,1)S(1)}, u32[]{:S(2)}, u32[]{:S(2)}) collective-permute-start(bf16[3,8,8192]{2,1,0:T(8,128)(2,1)S(1)} %pad_maximum_fusion.1), channel_id=1, source_target_pairs={{0,1},{1,2},{2,3},{3,4},{4,5},{5,6},{6,7},{7,8},{8,9},{9,10},{10,1... | collective-permute-start | bytes 1179656 | tf_op jit(solution)/shard_map/ppermute | solution.py:272
  42.8 0.8 copy-start.2
  42.8 1.0 copy-start.1
  43.8 21.2 %copy-start.3 = (f32[256,32]{0,1:T(8,128)S(1)}, f32[256,32]{0,1:T(8,128)}, u32[]{:S(2)}) copy-start(f32[256,32]{0,1:T(8,128)} %param.18) | copy-start | bytes 98308
  58.1 92.1 %collective-permute-start.2 = (bf16[128,8192]{1,0:T(8,128)(2,1)}, bf16[128,8192]{1,0:T(8,128)(2,1)}, u32[]{:S(2)}, u32[]{:S(2)}) collective-permute-start(bf16[128,8192]{1,0:T(8,128)(2,1)} %get-tuple-element.14), channel_id=1, source_target_pairs={{0,1},{1,2},{2,3},{3,4},{4,5},{5,6},{6,7},{7,8},{8,9},{9,10},{10,1... | collective-permute-start | bytes 6291464 | tf_op jit(solution)/shard_map/ppermute | solution.py:296
  63.7 86.5 %collective-permute-start.3 = (bf16[136,8192]{1,0:T(8,128)(2,1)}, bf16[136,8192]{1,0:T(8,128)(2,1)S(1)}, u32[]{:S(2)}, u32[]{:S(2)}) collective-permute-start(bf16[136,8192]{1,0:T(8,128)(2,1)} %get-tuple-element.15), channel_id=1, source_target_pairs={{1,0},{2,1},{3,2},{4,3},{5,4},{6,5},{7,6},{8,7},{9,8},{10,9},{11,1... | collective-permute-start | bytes 6684680 | tf_op jit(solution)/shard_map/ppermute | solution.py:297
  150.2 1.4 copy-start
  253.8 17.9 %all-to-all-start.3 = ((f32[32,24,256]{2,1,0:T(8,128)}), f32[32,24,256]{2,1,0:T(8,128)S(1)}, u32[]{:S(2)}, u32[]{:S(2)}) async-start(f32[32,24,256]{2,1,0:T(8,128)} %get-tuple-element.21), calls=%async_computation.4 | async-start | bytes 1572864 | tf_op jit(solution)/shard_map/all_to_all | solution.py:377
  259.4 27.3 %reduce-scatter.2.cloned.1.call-start = ((), (), s32[]{:S(2)}) async-start(), calls=%async_computation.5 | async-start | bytes 163840 | tf_op jit(solution)/shard_map/reduce_scatter | solution.py:376
Sparse Core Ops, SparseCore 0:
  263.1 21.1 reduce-scatter.1

commit v2 on v1

--- a/solution.py
+++ b/solution.py
@@ -8,6 +8,8 @@
 from jax.experimental.pallas import tpu as pltpu
 from jax.sharding import PartitionSpec as P
 
+
+PARTS = 4
 BF = jnp.bfloat16
 F32 = jnp.float32
 LANES = 128
@@ -52,7 +54,7 @@
 
 
 def row_of(ref, index, lanes):
-    return ref[pl.ds(index, 1), lanes]
+    return ref[0, pl.ds(index, 1), lanes]
 
 
 def load_padded(dst, own_ref, before, after, lanes, block):
@@ -113,12 +115,16 @@
     fa_lo,
     in_hi,
     in_lo,
+    *rest,
+):
+    rest = rest[len(rest) - 26 :]
+    (
     mixed,
     g_q,
     g_k,
     g_v,
-    g_med,
-    g_short,
+    g_part,
+    sums,
     x_q,
     x_k,
     x_v,
@@ -139,7 +145,7 @@
     spec_w,
     prod_hi,
     prod_lo,
-):
+    ) = rest
     rows = block + ROW
     half = block
     rank = lax.broadcasted_iota(jnp.int32, (ROW, LANES), 0)
@@ -235,8 +241,8 @@
             du_fix = du_fix + held * h_flip[col, pl.ds(ROW - 1 - place, ROW), :]
         z = jnp.concatenate([z[0:ROW] + z_fix, z[ROW:]], axis=0)
         du = jnp.concatenate([du[0:block], du[block:] + du_fix], axis=0)
-        g_med[0, 0 : block - ROW, lanes] = gm[0 : block - ROW]
-        g_med[0, block - ROW : block, lanes] = gm[block - ROW : block] + g_fix
+        gm = jnp.concatenate([gm[0 : block - ROW], gm[block - ROW : block] + g_fix], axis=0)
+        g_part[0, 0:block, lanes] = gm.astype(BF)
         mixed[0, :, lanes] = (s_q[col, 0:block, :] * z[0:block]).astype(BF)
         g_pad[0, 0:block, :] = go[0, :, lanes].astype(F32) * z[0:block]
         g_pad[0, block:rows, :] = fore[3, :, lanes].astype(F32) * z[block:rows]
@@ -249,142 +255,163 @@
                 moved = g_pad[which, pl.ds(offset, block), :]
                 term = row_of(taps, which * width + offset, lanes) * moved
                 total = term if total is None else total + term
-                g_short[0, which * width + offset : which * width + offset + 1, lanes] = jnp.sum(
-                    values * moved, axis=0, keepdims=True
-                )
+                place = which * width + offset
+                sums[place : place + 1, :] = jnp.sum(values * moved, axis=0, keepdims=True)
             out[0, :, lanes] = total.astype(BF)
+        g_part[0, block : block + 3 * ROW, lanes] = sums[...].astype(BF)
 
 
 def halo_pairs(count):
     return [(i, i + 1) for i in range(count - 1)], [(i + 1, i) for i in range(count - 1)]
 
 
+def groups_of(n_context, n_dp, fine):
+    coarse = n_context // fine
+    inner = [[c * fine + f for f in range(fine)] for c in range(coarse)]
+    outer = [[c * fine + f for c in range(coarse)] for f in range(fine)]
+    both = [
+        [(c * fine + f) * n_dp + d for f in range(fine) for d in range(n_dp)] for c in range(coarse)
+    ]
+    return inner, outer, both
+
+
+def exchange(x, axes, groups=None):
+    return lax.all_to_all(x, axes, 0, 0, axis_index_groups=groups)
+
+
+def spread(x, count, axes, groups=None):
+    return exchange(jnp.broadcast_to(x, (count,) + x.shape), axes, groups)
+
+
 def per_device(n_context, n_dp, query_in, key_in, value_in, grad_out, med_filter, short_filter):
-    _, block, width_all = query_in.shape
+    _, block, _ = query_in.shape
     group, taps_own = med_filter.shape
     width = short_filter.shape[2]
     size = 2 * block
+    rows = block + ROW
+    held_short = 3 * ROW
+    parts = PARTS
+    coarse = n_context // parts
     ahead, behind = halo_pairs(n_context)
+    _, outer, both = groups_of(n_context, n_dp, parts)
     forward, inverse = transforms(block, width)
+    tables = [part for pair in forward + [inverse] for part in pair]
 
     back = jnp.concatenate([x[:, block - ROW :] for x in (query_in, key_in, value_in)], axis=0)
     fore = jnp.concatenate([x[:, :ROW] for x in (query_in, key_in, value_in, grad_out)], axis=0)
     back = lax.ppermute(back, "context", ahead)
     fore = lax.ppermute(fore, "context", behind)
 
-    h_all, taps = share_filters(med_filter, short_filter)
-
-    tile = 4 * LANES
-    cols = tile // LANES
-    tokens = pl.BlockSpec((1, block, tile), lambda i: (0, 0, i))
-    flat = lambda height: pl.BlockSpec((height, tile), lambda i: (0, i))
-    stack = lambda count: pl.BlockSpec((count, ROW, tile), lambda i: (0, 0, i))
+    short = short_filter.transpose(0, 2, 1).reshape(3 * width, group)
+    short = jnp.pad(short, ((0, held_short - 3 * width), (0, 0)))
+    taps = spread(short, n_context, "context")
+
+    mine = spread(med_filter.astype(BF).T, parts * n_dp, ("context", "dp"), both)
+    mine = mine.reshape(parts, block, group)
+    h_all = []
+    for place in range(2):
+        first = place * (parts // 2)
+        h_all.append(spread(mine[first : first + parts // 2], coarse, "context", outer))
+
+    cols = group // LANES
+    grid = (coarse,)
     padded = pltpu.VMEM((cols, block + 2 * ROW, LANES), F32)
-    u, dz = pl.pallas_call(
-        functools.partial(make_products, block, width, cols),
-        grid=(width_all // tile,),
-        in_specs=[tokens] * 4 + [stack(3), stack(4), flat(taps.shape[0])],
-        out_specs=[flat(block), flat(block + ROW)],
-        out_shape=[
-            jax.ShapeDtypeStruct((block, width_all), BF),
-            jax.ShapeDtypeStruct((block + ROW, width_all), BF),
-        ],
-        scratch_shapes=[padded] * 3,
-        name="products",
-    )(query_in, key_in, value_in, grad_out, back, fore, taps)
-
-    u_prev = lax.ppermute(u, "context", ahead)
-    dz_next = lax.ppermute(dz, "context", behind)
-
-    tile = group
-    cols = tile // LANES
-    tokens = pl.BlockSpec((1, block, tile), lambda i: (0, 0, i))
-    flat = lambda height: pl.BlockSpec((height, tile), lambda i: (0, i))
-    stack = lambda count: pl.BlockSpec((count, ROW, tile), lambda i: (0, 0, i))
+    shifted = pltpu.VMEM((cols, rows, LANES), F32)
     whole = lambda x: pl.BlockSpec(x.shape, lambda i: (0,) * x.ndim)
-    per_group = lambda height: pl.BlockSpec((1, height, tile), lambda i: (i, 0, 0))
-    tables = [part for pair in forward + [inverse] for part in pair]
-    padded = pltpu.VMEM((cols, block + 2 * ROW, LANES), F32)
-    shifted = pltpu.VMEM((cols, block + ROW, LANES), F32)
-    held_short = 3 * ROW
-    mixed, grad_q, grad_k, grad_v, part_med, part_short = pl.pallas_call(
-        functools.partial(mixer, block, width, cols),
-        grid=(width_all // tile,),
-        in_specs=[tokens] * 4
-        + [stack(3), stack(4), flat(taps.shape[0]), flat(block), flat(block + ROW), per_group(block)]
-        + [whole(x) for x in tables],
-        out_specs=[tokens] * 4 + [per_group(block), per_group(held_short)],
-        out_shape=[jax.ShapeDtypeStruct(query_in.shape, BF)] * 4
-        + [
-            jax.ShapeDtypeStruct((n_context, block, group), F32),
-            jax.ShapeDtypeStruct((n_context, held_short, group), F32),
-        ],
-        scratch_shapes=[
-            padded,
-            padded,
-            padded,
-            shifted,
-            shifted,
-            shifted,
-            pltpu.VMEM((3, block + ROW, LANES), F32),
-            pltpu.VMEM((cols, 3 * ROW, LANES), F32),
-            pltpu.VMEM((cols, 2 * ROW, LANES), F32),
-            pltpu.VMEM((cols, 2 * ROW, LANES), F32),
-            pltpu.VMEM((size, tile), BF),
-            pltpu.VMEM((block, tile), BF),
-            pltpu.VMEM((cols, ROW, LANES), F32),
-            pltpu.VMEM((cols, ROW, LANES), F32),
-            pltpu.VMEM((size, tile), F32),
-            pltpu.VMEM((size, tile), F32),
-            pltpu.VMEM((size, tile), F32),
-            pltpu.VMEM((size, tile), F32),
-            pltpu.VMEM((3, size, tile), BF),
-            pltpu.VMEM((3, size, tile), BF),
-        ],
-        name="mixer",
-    )(
-        query_in,
-        key_in,
-        value_in,
-        grad_out,
-        back,
-        fore,
-        taps,
-        u_prev,
-        dz_next,
-        h_all,
-        *tables,
-    )
-
-    grad_med, grad_short = reduce_filters(part_med, part_short, n_dp, width, taps_own)
-    return (mixed, grad_q, grad_k, grad_v, grad_med, grad_short)
-
-
-def share_filters(med_filter, short_filter):
-    mine = med_filter.astype(BF).T
-    column = lax.all_gather(mine, "dp", axis=0, tiled=True)
-    n = lax.axis_size("context")
-    h_all = lax.all_to_all(jnp.broadcast_to(column, (n,) + column.shape), "context", 0, 0)
-    short = short_filter.transpose(0, 2, 1).reshape(-1, short_filter.shape[1])
-    short = jnp.pad(short, ((0, -short.shape[0] % ROW), (0, 0)))
-    taps = lax.all_to_all(jnp.broadcast_to(short, (n,) + short.shape), "context", 0, 0)
-    return h_all, taps.transpose(1, 0, 2).reshape(short.shape[0], -1)
-
-
-def reduce_filters(part_med, part_short, n_dp, width, taps_own):
-    med = jnp.sum(lax.all_to_all(part_med, "context", 0, 0), axis=0)
-    med = lax.psum_scatter(med, "dp", scatter_dimension=0, tiled=True)
-    short = jnp.sum(lax.all_to_all(part_short, "context", 0, 0), axis=0)
-    short = lax.psum(short, "dp")
-    group = short.shape[1]
-    return med.T, short[: 3 * width].reshape(3, width, group).transpose(0, 2, 1)
+    packed = lambda height: pl.BlockSpec((height, group), lambda i: (0, i))
+    outs = None
+    partials = []
+    pieces = []
+    for part in range(parts):
+        tokens = pl.BlockSpec((1, block, group), lambda i, part=part: (0, 0, parts * i + part))
+        stack = lambda count, part=part: pl.BlockSpec(
+            (count, ROW, group), lambda i: (0, 0, parts * i + part)
+        )
+        filters = pl.BlockSpec((1, held_short, group), lambda i, part=part: (parts * i + part, 0, 0))
+        u, dz = pl.pallas_call(
+            functools.partial(make_products, block, width, cols),
+            grid=grid,
+            in_specs=[tokens] * 4 + [stack(3), stack(4), filters],
+            out_specs=[packed(block), packed(rows)],
+            out_shape=[
+                jax.ShapeDtypeStruct((block, coarse * group), BF),
+                jax.ShapeDtypeStruct((rows, coarse * group), BF),
+            ],
+            scratch_shapes=[padded] * 3,
+        )(query_in, key_in, value_in, grad_out, back, fore, taps)
+        u_prev = lax.ppermute(u, "context", ahead)
+        dz_next = lax.ppermute(dz, "context", behind)
+        pieces.append((u_prev, dz_next))
+    for part in range(parts):
+        tokens = pl.BlockSpec((1, block, group), lambda i, part=part: (0, 0, parts * i + part))
+        stack = lambda count, part=part: pl.BlockSpec(
+            (count, ROW, group), lambda i: (0, 0, parts * i + part)
+        )
+        filters = pl.BlockSpec((1, held_short, group), lambda i, part=part: (parts * i + part, 0, 0))
+        half = parts // 2
+        taps_h = pl.BlockSpec(
+            (1, None, block, group), lambda i, part=part: (i, part % half, 0, 0)
+        )
+        u_prev, dz_next = pieces[part]
+        carried = [] if outs is None else list(outs)
+        fixed = [query_in, key_in, value_in, grad_out, back, fore, taps, u_prev, dz_next]
+        fixed += [h_all[part // half], *tables]
+        *outs, partial = pl.pallas_call(
+            functools.partial(mixer, block, width, cols),
+            grid=grid,
+            in_specs=[tokens] * 4
+            + [stack(3), stack(4), filters, packed(block), packed(rows), taps_h]
+            + [whole(x) for x in tables]
+            + [pl.BlockSpec(memory_space=pl.ANY)] * len(carried),
+            out_specs=[tokens] * 4
+            + [pl.BlockSpec((1, block + held_short, group), lambda i: (i, 0, 0))],
+            out_shape=[jax.ShapeDtypeStruct(query_in.shape, BF)] * 4
+            + [jax.ShapeDtypeStruct((coarse, block + held_short, group), BF)],
+            scratch_shapes=[
+                pltpu.VMEM((held_short, LANES), F32),
+                padded,
+                padded,
+                padded,
+                shifted,
+                shifted,
+                shifted,
+                pltpu.VMEM((3, rows, LANES), F32),
+                pltpu.VMEM((cols, 3 * ROW, LANES), F32),
+                pltpu.VMEM((cols, 2 * ROW, LANES), F32),
+                pltpu.VMEM((cols, 2 * ROW, LANES), F32),
+                pltpu.VMEM((size, group), BF),
+                pltpu.VMEM((block, group), BF),
+                pltpu.VMEM((cols, ROW, LANES), F32),
+                pltpu.VMEM((cols, ROW, LANES), F32),
+                pltpu.VMEM((size, group), F32),
+                pltpu.VMEM((size, group), F32),
+                pltpu.VMEM((size, group), F32),
+                pltpu.VMEM((size, group), F32),
+                pltpu.VMEM((3, size, group), BF),
+                pltpu.VMEM((3, size, group), BF),
+            ],
+            input_output_aliases={len(fixed) + place: place for place in range(len(carried))},
+        )(*fixed, *carried)
+        arrived = exchange(partial, "context", outer)
+        partials.append(jnp.sum(arrived.astype(F32), axis=0))
+
+    total = jnp.stack(partials)
+    med = total[:, :block].reshape(parts, n_dp, taps_own, group)
+    extra = jnp.broadcast_to(total[:, None, block:], (parts, n_dp, held_short, group))
+    sent = jnp.concatenate([med, extra], axis=2).reshape(parts * n_dp, taps_own + held_short, group)
+    final = jnp.sum(exchange(sent, ("context", "dp"), both), axis=0)
+    grad_med = final[:taps_own].T
+    grad_short = final[taps_own : taps_own + 3 * width].reshape(3, width, group).transpose(0, 2, 1)
+    return (*outs, grad_med, grad_short)
 
 
 def solution(mesh):
     tokens = P("dp", "context", None)
     filters = (P("context", "dp"), P(None, "context", None))
+    inner = functools.partial(per_device, mesh.shape["context"], mesh.shape["dp"])
+
     return jax.shard_map(
-        functools.partial(per_device, mesh.shape["context"], mesh.shape["dp"]),
+        inner,
         mesh=mesh,
         in_specs=(tokens,) * 4 + filters,
         out_specs=(tokens,) * 4 + filters,

time: 295 us -> 267 us (0.905)
  blocking collectives: 154 us -> 70.5 us
  starting transfers between devices: 29.2 us -> 65 us
  Pallas kernels: 61.8 us -> 79.7 us
  between operations: 14.2 us -> 0.98 us
  waiting for transfers between devices: 23 us -> 33.3 us
  local copies, waits for them, and re-layouts: 8.15 us -> 12.6 us
    all_to_all x2 -> x4, blocking collectives: 133 us -> 70.5 us  [exchange(): return lax.all_to_all(x, axes, 0, 0, axis_index_groups=groups)]
    all_to_all x2 -> x5, starting transfers between devices: 17.8 us -> 37.1 us  [exchange(): return lax.all_to_all(x, axes, 0, 0, axis_index_groups=groups)]
    psum x1 -> x0, blocking collectives: 14.3 us -> none  [reduce_filters(): short = lax.psum(short, 'dp')]
    ppermute x1 -> x4, starting transfers between devices: 5.6 us -> 18.3 us  [per_device(): u_prev = lax.ppermute(u, 'context', ahead)]
    pallas_call x1 -> x4, Pallas kernels: 14.3 us -> 24.8 us  [per_device(): pl.pallas_call(functools.partial(make_products, block, width, cols), grid...]
    pallas_call x1 -> x4, Pallas kernels: 47.5 us -> 54.9 us  [per_device(): pl.pallas_call(functools.partial(mixer, block, width, cols), grid=grid, i...]
    all_to_all x2 -> x5, waiting for transfers between devices: 19.6 us -> 26.3 us  [exchange(): return lax.all_to_all(x, axes, 0, 0, axis_index_groups=groups)]
    all_gather x1 -> x0, blocking collectives: 6.62 us -> none  [share_filters(): column = lax.all_gather(mine, 'dp', axis=0, tiled=True)]
  transfers between devices with their start and end apart: 7 -> 15, of which waited for: 3 -> 4; matrix products, arithmetic and copies ran while one was open for 2% -> 2% of each run, Pallas kernels for 0% -> 25%
where the time goes in v2:
time: 267 us; the launch traced here: 264 us
  Pallas kernels  79.7 us (30%)
  blocking collectives  70.5 us (26%)
  starting transfers between devices  65 us (24%)
  waiting for transfers between devices  33.3 us (12%)
  local copies, waits for them, and re-layouts  12.6 us (5%)
    all_to_all x4, blocking collectives, exchange(): return lax.all_to_all(x, axes, 0, 0, axis_index_groups=groups)  70.5 us
    pallas_call x4, Pallas kernels, per_device(): pl.pallas_call(functools.partial(mixer, block, width, cols), grid=grid, i...  54.9 us
    all_to_all x5, starting transfers between devices, exchange(): return lax.all_to_all(x, axes, 0, 0, axis_index_groups=groups)  37.1 us
    all_to_all x5, waiting for transfers between devices, exchange(): return lax.all_to_all(x, axes, 0, 0, axis_index_groups=groups)  26.3 us
    pallas_call x4, Pallas kernels, per_device(): pl.pallas_call(functools.partial(make_products, block, width, cols), grid...  24.8 us
    ppermute x4, starting transfers between devices, per_device(): u_prev = lax.ppermute(u, 'context', ahead)  18.3 us
    ppermute x1, waiting for transfers between devices, per_device(): back = lax.ppermute(back, 'context', ahead)  6.95 us
  transfers between devices with their start and end apart: 15, of which 4 were waited for; matrix products, arithmetic and copies ran while one was open for 2% of the time, Pallas kernels for 25%

profile of v2, /device:TPU:1, one launch (start us, length us, event | category | flops | bytes accessed | tf_op | source)
XLA Modules:
  0.0 264.4 jit_solution(338092678682636730)
XLA Ops:
  2.1 7.8 %all-to-all-start.1 = ((bf16[16,32,256]{2,1,0:T(8,128)(2,1)}), bf16[16,32,256]{2,1,0:T(8,128)(2,1)S(1)}, u32[]{:S(2)}, u32[]{:S(2)}) async-start(bf16[16,32,256]{2,1,0:T(8,128)(2,1)} %broadcast_in_dim.19), calls=%async_computation.1 | async-start | bytes 524288 | tf_op jit(solution)/shard_map/all_to_all | solution.py:279
  10.0 1.9 fusion
  12.9 4.3 %all-to-all-done.1 = bf16[16,32,256]{2,1,0:T(8,128)(2,1)S(1)} async-done(((bf16[16,32,256]{2,1,0:T(8,128)(2,1)}), bf16[16,32,256]{2,1,0:T(8,128)(2,1)S(1)}, u32[]{:S(2)}, u32[]{:S(2)}) %all-to-all-start.1) | async-done | bytes 262176 | tf_op jit(solution)/shard_map/all_to_all | solution.py:279
  18.1 7.6 %all-to-all-start = ((f32[32,24,256]{2,1,0:T(8,128)}), f32[32,24,256]{2,1,0:T(8,128)S(1)}, u32[]{:S(2)}, u32[]{:S(2)}) async-start(f32[32,24,256]{2,1,0:T(8,128)} %broadcast_in_dim.18), calls=%async_computation | async-start | bytes 1572864 | tf_op jit(solution)/shard_map/all_to_all | solution.py:279
  25.8 1.3 collective-permute-start.1
  27.1 12.8 %all-to-all-done.taps = f32[32,24,256]{2,1,0:T(8,128)S(1)} async-done(((f32[32,24,256]{2,1,0:T(8,128)}), f32[32,24,256]{2,1,0:T(8,128)S(1)}, u32[]{:S(2)}, u32[]{:S(2)}) %all-to-all-start) | async-done | bytes 786464 | tf_op jit(solution)/shard_map/all_to_all | solution.py:279
  41.0 3.9 %all-to-all-start.3 = ((bf16[8,2,128,256]{3,2,1,0:T(8,128)(2,1)}), bf16[8,2,128,256]{3,2,1,0:T(8,128)(2,1)S(1)}, u32[]{:S(2)}, u32[]{:S(2)}) async-start(bf16[8,2,128,256]{3,2,1,0:T(8,128)(2,1)} %broadcast_in_dim.21), calls=%async_computation.3 | async-start | bytes 2097152 | tf_op jit(solution)/shard_map/all_to_all | solution.py:279
  45.9 3.2 %collective-permute-start = (bf16[3,8,8192]{2,1,0:T(8,128)(2,1)S(1)}, bf16[3,8,8192]{2,1,0:T(8,128)(2,1)S(1)}, u32[]{:S(2)}, u32[]{:S(2)}) collective-permute-start(bf16[3,8,8192]{2,1,0:T(8,128)(2,1)S(1)} %pad_maximum_fusion.3), channel_id=1, source_target_pairs={{0,1},{1,2},{2,3},{3,4},{4,5},{5,6},{6,7},{7,8},{8,9},{9,10},{10,1... | collective-permute-start | bytes 1179656 | tf_op jit(solution)/shard_map/ppermute | solution.py:302
  49.0 6.9 %collective-permute-done.back = bf16[3,8,8192]{2,1,0:T(8,128)(2,1)S(1)} collective-permute-done((bf16[3,8,8192]{2,1,0:T(8,128)(2,1)S(1)}, bf16[3,8,8192]{2,1,0:T(8,128)(2,1)S(1)}, u32[]{:S(2)}, u32[]{:S(2)}) %collective-permute-start) | collective-permute-done | bytes 393248 | tf_op jit(solution)/shard_map/ppermute | solution.py:302
  57.5 6.2 %shard_map.184 = (bf16[128,2048]{1,0:T(8,128)(2,1)}, bf16[136,2048]{1,0:T(8,128)(2,1)}) custom-call(bf16[1,128,8192]{2,1,0:T(8,128)(2,1)} %q.15, bf16[1,128,8192]{2,1,0:T(8,128)(2,1)} %k.15, bf16[1,128,8192]{2,1,0:T(8,128)(2,1)} %v.15, bf16[1,128,8192]{2,1,0:T(8,128)(2,1)} %go.15, bf16[3,8,8192]{2,1,0:T(8,128)(2,1)} %copy-done.2, ...), custom_call_target="tpu_custom_call" | custom-call | tf_op jit(solution)/shard_map/pallas_call | solution.py:331
  63.7 1.3 collective-permute-start.9
  65.0 4.8 %collective-permute-start.8 = (bf16[128,2048]{1,0:T(8,128)(2,1)}, bf16[128,2048]{1,0:T(8,128)(2,1)S(1)}, u32[]{:S(2)}, u32[]{:S(2)}) collective-permute-start(bf16[128,2048]{1,0:T(8,128)(2,1)} %get-tuple-element.40), channel_id=1, source_target_pairs={{0,1},{1,2},{2,3},{3,4},{4,5},{5,6},{6,7},{7,8},{8,9},{9,10},{10,1... | collective-permute-start | bytes 1572872 | tf_op jit(solution)/shard_map/ppermute | solution.py:342
  69.8 6.2 %shard_map.183 = (bf16[128,2048]{1,0:T(8,128)(2,1)}, bf16[136,2048]{1,0:T(8,128)(2,1)}) custom-call(bf16[1,128,8192]{2,1,0:T(8,128)(2,1)} %q.15, bf16[1,128,8192]{2,1,0:T(8,128)(2,1)} %k.15, bf16[1,128,8192]{2,1,0:T(8,128)(2,1)} %v.15, bf16[1,128,8192]{2,1,0:T(8,128)(2,1)} %go.15, bf16[3,8,8192]{2,1,0:T(8,128)(2,1)} %copy-done.2, ...), custom_call_target="tpu_custom_call" | custom-call | tf_op jit(solution)/shard_map/pallas_call | solution.py:331
  76.0 4.2 %collective-permute-start.6 = (bf16[128,2048]{1,0:T(8,128)(2,1)}, bf16[128,2048]{1,0:T(8,128)(2,1)}, u32[]{:S(2)}, u32[]{:S(2)}) collective-permute-start(bf16[128,2048]{1,0:T(8,128)(2,1)} %get-tuple-element.38), channel_id=1, source_target_pairs={{0,1},{1,2},{2,3},{3,4},{4,5},{5,6},{6,7},{7,8},{8,9},{9,10},{10,1... | collective-permute-start | bytes 1572872 | tf_op jit(solution)/shard_map/ppermute | solution.py:342
  81.3 14.3 %all-to-all-start.2 = ((bf16[8,2,128,256]{3,2,1,0:T(8,128)(2,1)}), bf16[8,2,128,256]{3,2,1,0:T(8,128)(2,1)S(1)}, u32[]{:S(2)}, u32[]{:S(2)}) async-start(bf16[8,2,128,256]{3,2,1,0:T(8,128)(2,1)} %broadcast_in_dim.20), calls=%async_computation.2 | async-start | bytes 2097152 | tf_op jit(solution)/shard_map/all_to_all | solution.py:279
  95.7 1.3 collective-permute-start.7
  97.0 6.2 %shard_map.182 = (bf16[128,2048]{1,0:T(8,128)(2,1)}, bf16[136,2048]{1,0:T(8,128)(2,1)}) custom-call(bf16[1,128,8192]{2,1,0:T(8,128)(2,1)} %q.15, bf16[1,128,8192]{2,1,0:T(8,128)(2,1)} %k.15, bf16[1,128,8192]{2,1,0:T(8,128)(2,1)} %v.15, bf16[1,128,8192]{2,1,0:T(8,128)(2,1)} %go.15, bf16[3,8,8192]{2,1,0:T(8,128)(2,1)} %copy-done.2, ...), custom_call_target="tpu_custom_call" | custom-call | tf_op jit(solution)/shard_map/pallas_call | solution.py:331
  103.2 1.3 collective-permute-start.5
  104.5 6.2 %shard_map.181 = (bf16[128,2048]{1,0:T(8,128)(2,1)}, bf16[136,2048]{1,0:T(8,128)(2,1)}) custom-call(bf16[1,128,8192]{2,1,0:T(8,128)(2,1)} %q.15, bf16[1,128,8192]{2,1,0:T(8,128)(2,1)} %k.15, bf16[1,128,8192]{2,1,0:T(8,128)(2,1)} %v.15, bf16[1,128,8192]{2,1,0:T(8,128)(2,1)} %go.15, bf16[3,8,8192]{2,1,0:T(8,128)(2,1)} %copy-done.2, ...), custom_call_target="tpu_custom_call" | custom-call | tf_op jit(solution)/shard_map/pallas_call | solution.py:331
  111.5 1.3 collective-permute-start.3
  112.8 6.1 %collective-permute-start.4 = (bf16[128,2048]{1,0:T(8,128)(2,1)}, bf16[128,2048]{1,0:T(8,128)(2,1)}, u32[]{:S(2)}, u32[]{:S(2)}) collective-permute-start(bf16[128,2048]{1,0:T(8,128)(2,1)} %get-tuple-element.36), channel_id=1, source_target_pairs={{0,1},{1,2},{2,3},{3,4},{4,5},{5,6},{6,7},{7,8},{8,9},{9,10},{10,1... | collective-permute-start | bytes 1572872 | tf_op jit(solution)/shard_map/ppermute | solution.py:342
  118.9 3.3 %collective-permute-start.2 = (bf16[128,2048]{1,0:T(8,128)(2,1)}, bf16[128,2048]{1,0:T(8,128)(2,1)S(1)}, u32[]{:S(2)}, u32[]{:S(2)}) collective-permute-start(bf16[128,2048]{1,0:T(8,128)(2,1)} %get-tuple-element.34), channel_id=1, source_target_pairs={{0,1},{1,2},{2,3},{3,4},{4,5},{5,6},{6,7},{7,8},{8,9},{9,10},{10,1... | collective-permute-start | bytes 1572872 | tf_op jit(solution)/shard_map/ppermute | solution.py:342
  122.2 13.7 %shard_map.185 = (bf16[1,128,8192]{2,1,0:T(8,128)(2,1)}, bf16[1,128,8192]{2,1,0:T(8,128)(2,1)}, bf16[1,128,8192]{2,1,0:T(8,128)(2,1)}, bf16[1,128,8192]{2,1,0:T(8,128)(2,1)}, bf16[8,152,256]{2,1,0:T(8,128)(2,1)}) custom-call(bf16[1,128,8192]{2,1,0:T(8,128)(2,1)} %q.15, bf16[1,128,8192]{2,1,0:T(8,128)(2,1)} %k.15, bf16[1,128,8192]{2,1,0:T(8,128)(2,1)} %v.15, ...), custom_call_target="tpu_custom_call" | custom-call | tf_op jit(solution)/shard_map/pallas_call | solution.py:359
  135.9 13.7 %shard_map.186 = (bf16[1,128,8192]{2,1,0:T(8,128)(2,1)}, bf16[1,128,8192]{2,1,0:T(8,128)(2,1)}, bf16[1,128,8192]{2,1,0:T(8,128)(2,1)}, bf16[1,128,8192]{2,1,0:T(8,128)(2,1)}, bf16[8,152,256]{2,1,0:T(8,128)(2,1)}) custom-call(bf16[1,128,8192]{2,1,0:T(8,128)(2,1)} %q.15, ...), custom_call_target="tpu_custom_call", output_to_operand_aliasing={{0}: (18, {}), {1}: (19, {}), {2}: (20, {}), {3}: (21, {})} | custom-call | tf_op jit(solution)/shard_map/pallas_call | solution.py:359
  150.8 13.7 %shard_map.187 = (bf16[1,128,8192]{2,1,0:T(8,128)(2,1)}, bf16[1,128,8192]{2,1,0:T(8,128)(2,1)}, bf16[1,128,8192]{2,1,0:T(8,128)(2,1)}, bf16[1,128,8192]{2,1,0:T(8,128)(2,1)}, bf16[8,152,256]{2,1,0:T(8,128)(2,1)}) custom-call(bf16[1,128,8192]{2,1,0:T(8,128)(2,1)} %q.15, ...), custom_call_target="tpu_custom_call", output_to_operand_aliasing={{0}: (18, {}), {1}: (19, {}), {2}: (20, {}), {3}: (21, {})} | custom-call | tf_op jit(solution)/shard_map/pallas_call | solution.py:359
  165.5 13.7 %shard_map.188 = (bf16[1,128,8192]{2,1,0:T(8,128)(2,1)}, bf16[1,128,8192]{2,1,0:T(8,128)(2,1)}, bf16[1,128,8192]{2,1,0:T(8,128)(2,1)}, bf16[1,128,8192]{2,1,0:T(8,128)(2,1)}, bf16[8,152,256]{2,1,0:T(8,128)(2,1)}) custom-call(bf16[1,128,8192]{2,1,0:T(8,128)(2,1)} %q.15, ...), custom_call_target="tpu_custom_call", output_to_operand_aliasing={{0}: (18, {}), {1}: (19, {}), {2}: (20, {}), {3}: (21, {})} | custom-call | tf_op jit(solution)/shard_map/pallas_call | solution.py:359
  179.2 19.8 %all_to_all.45 = bf16[8,152,256]{2,1,0:T(8,128)(2,1)S(1)} all-to-all(bf16[8,152,256]{2,1,0:T(8,128)(2,1)} %get-tuple-element.61), channel_id=1, replica_groups={{0,4,8,12,16,20,24,28},{1,5,9,13,17,21,25,29},{2,6,10,14,18,22,26,30},{..., dimensions={0} | all-to-all | bytes 1245184 | tf_op jit(solution)/shard_map/all_to_all | solution.py:279
  199.1 12.1 %all_to_all.46 = bf16[8,152,256]{2,1,0:T(8,128)(2,1)S(1)} all-to-all(bf16[8,152,256]{2,1,0:T(8,128)(2,1)S(1)} %copy-done.6), channel_id=1, replica_groups={{0,4,8,12,16,20,24,28},{1,5,9,13,17,21,25,29},{2,6,10,14,18,22,26,30},{..., dimensions={0} | all-to-all | bytes 1245184 | tf_op jit(solution)/shard_map/all_to_all | solution.py:279
  211.2 12.0 %all_to_all.47 = bf16[8,152,256]{2,1,0:T(8,128)(2,1)S(1)} all-to-all(bf16[8,152,256]{2,1,0:T(8,128)(2,1)S(1)} %copy-done.5), channel_id=1, replica_groups={{0,4,8,12,16,20,24,28},{1,5,9,13,17,21,25,29},{2,6,10,14,18,22,26,30},{..., dimensions={0} | all-to-all | bytes 1245184 | tf_op jit(solution)/shard_map/all_to_all | solution.py:279
  223.2 3.5 %all-to-all-start.4 = ((bf16[8,152,256]{2,1,0:T(8,128)(2,1)}), bf16[8,152,256]{2,1,0:T(8,128)(2,1)S(1)}, u32[]{:S(2)}, u32[]{:S(2)}) async-start(bf16[8,152,256]{2,1,0:T(8,128)(2,1)} %get-tuple-element.58), calls=%async_computation.4 | async-start | bytes 1245184 | tf_op jit(solution)/shard_map/all_to_all | solution.py:279
  227.0 9.2 %all-to-all-done.4 = bf16[8,152,256]{2,1,0:T(8,128)(2,1)S(1)} async-done(((bf16[8,152,256]{2,1,0:T(8,128)(2,1)}), bf16[8,152,256]{2,1,0:T(8,128)(2,1)S(1)}, u32[]{:S(2)}, u32[]{:S(2)}) %all-to-all-start.4) | async-done | bytes 622624 | tf_op jit(solution)/shard_map/all_to_all | solution.py:279
  236.5 26.6 %all_to_all.48 = f32[16,56,256]{2,1,0:T(8,128)S(1)} all-to-all(f32[16,56,256]{2,1,0:T(8,128)S(1)} %pad_maximum_fusion), channel_id=1, replica_groups={{0,32,64,96,1,33,65,97,2,34,66,98,3,35,67,99},{4,36,68,100,5,37,69,101,..., dimensions={0} | all-to-all | bytes 1835008 | tf_op jit(solution)/shard_map/all_to_all | solution.py:279
  (63 shorter events, 13.1 us)
Async XLA Ops:
  0.6 12.2 %copy-start.12 = (f32[3,256,7]{1,2,0:T(8,128)S(1)}, f32[3,256,7]{1,2,0:T(8,128)}, u32[]{:S(2)}) copy-start(f32[3,256,7]{1,2,0:T(8,128)} %param.19) | copy-start | bytes 64516
  2.1 15.0 %all-to-all-start.1 = ((bf16[16,32,256]{2,1,0:T(8,128)(2,1)}), bf16[16,32,256]{2,1,0:T(8,128)(2,1)S(1)}, u32[]{:S(2)}, u32[]{:S(2)}) async-start(bf16[16,32,256]{2,1,0:T(8,128)(2,1)} %broadcast_in_dim.19), calls=%async_computation.1 | async-start | bytes 524288 | tf_op jit(solution)/shard_map/all_to_all | solution.py:279
  10.0 15.7 %slice-start = ((bf16[1,128,8192]{2,1,0:T(8,128)(2,1)}), bf16[1,8,8192]{2,1,0:T(8,128)(2,1)S(1)}, s32[]{:S(2)}) async-start(bf16[1,128,8192]{2,1,0:T(8,128)(2,1)} %go.15), calls=%async_computation.9 | async-start | bytes 262144 | tf_op jit(solution)/shard_map/slice | solution.py:301
  18.1 21.7 %all-to-all-start = ((f32[32,24,256]{2,1,0:T(8,128)}), f32[32,24,256]{2,1,0:T(8,128)S(1)}, u32[]{:S(2)}, u32[]{:S(2)}) async-start(f32[32,24,256]{2,1,0:T(8,128)} %broadcast_in_dim.18), calls=%async_computation | async-start | bytes 1572864 | tf_op jit(solution)/shard_map/all_to_all | solution.py:279
  25.8 30.2 %collective-permute-start.1 = (bf16[4,8,8192]{2,1,0:T(8,128)(2,1)S(1)}, bf16[4,8,8192]{2,1,0:T(8,128)(2,1)S(1)}, u32[]{:S(2)}, u32[]{:S(2)}) collective-permute-start(bf16[4,8,8192]{2,1,0:T(8,128)(2,1)S(1)} %pad_maximum_fusion.2), channel_id=1, source_target_pairs={{1,0},{2,1},{3,2},{4,3},{5,4},{6,5},{7,6},{8,7},{9,8},{10,9},{11,1... | collective-permute-start | bytes 1572872 | tf_op jit(solution)/shard_map/ppermute | solution.py:303
  39.8 16.2 %copy-start = (f32[32,24,256]{2,1,0:T(8,128)}, f32[32,24,256]{2,1,0:T(8,128)S(1)}, u32[]{:S(2)}) copy-start(f32[32,24,256]{2,1,0:T(8,128)S(1)} %all-to-all-done.taps) | copy-start | bytes 2359300
  41.0 39.2 %all-to-all-start.3 = ((bf16[8,2,128,256]{3,2,1,0:T(8,128)(2,1)}), bf16[8,2,128,256]{3,2,1,0:T(8,128)(2,1)S(1)}, u32[]{:S(2)}, u32[]{:S(2)}) async-start(bf16[8,2,128,256]{3,2,1,0:T(8,128)(2,1)} %broadcast_in_dim.21), calls=%async_computation.3 | async-start | bytes 2097152 | tf_op jit(solution)/shard_map/all_to_all | solution.py:279
  45.9 10.1 %collective-permute-start = (bf16[3,8,8192]{2,1,0:T(8,128)(2,1)S(1)}, bf16[3,8,8192]{2,1,0:T(8,128)(2,1)S(1)}, u32[]{:S(2)}, u32[]{:S(2)}) collective-permute-start(bf16[3,8,8192]{2,1,0:T(8,128)(2,1)S(1)} %pad_maximum_fusion.3), channel_id=1, source_target_pairs={{0,1},{1,2},{2,3},{3,4},{4,5},{5,6},{6,7},{7,8},{8,9},{9,10},{10,1... | collective-permute-start | bytes 1179656 | tf_op jit(solution)/shard_map/ppermute | solution.py:302
  56.0 0.7 copy-start.2
  56.7 0.8 copy-start.1
  63.7 55.2 %collective-permute-start.9 = (bf16[136,2048]{1,0:T(8,128)(2,1)}, bf16[136,2048]{1,0:T(8,128)(2,1)S(1)}, u32[]{:S(2)}, u32[]{:S(2)}) collective-permute-start(bf16[136,2048]{1,0:T(8,128)(2,1)} %get-tuple-element.41), channel_id=1, source_target_pairs={{1,0},{2,1},{3,2},{4,3},{5,4},{6,5},{7,6},{8,7},{9,8},{10,9},{11,1... | collective-permute-start | bytes 1671176 | tf_op jit(solution)/shard_map/ppermute | solution.py:343
  65.0 45.7 %collective-permute-start.8 = (bf16[128,2048]{1,0:T(8,128)(2,1)}, bf16[128,2048]{1,0:T(8,128)(2,1)S(1)}, u32[]{:S(2)}, u32[]{:S(2)}) collective-permute-start(bf16[128,2048]{1,0:T(8,128)(2,1)} %get-tuple-element.40), channel_id=1, source_target_pairs={{0,1},{1,2},{2,3},{3,4},{4,5},{5,6},{6,7},{7,8},{8,9},{9,10},{10,1... | collective-permute-start | bytes 1572872 | tf_op jit(solution)/shard_map/ppermute | solution.py:342
  76.0 36.8 %collective-permute-start.6 = (bf16[128,2048]{1,0:T(8,128)(2,1)}, bf16[128,2048]{1,0:T(8,128)(2,1)}, u32[]{:S(2)}, u32[]{:S(2)}) collective-permute-start(bf16[128,2048]{1,0:T(8,128)(2,1)} %get-tuple-element.38), channel_id=1, source_target_pairs={{0,1},{1,2},{2,3},{3,4},{4,5},{5,6},{6,7},{7,8},{8,9},{9,10},{10,1... | collective-permute-start | bytes 1572872 | tf_op jit(solution)/shard_map/ppermute | solution.py:342
  80.2 23.0 %copy-start.4 = (bf16[8,2,128,256]{3,2,1,0:T(8,128)(2,1)}, bf16[8,2,128,256]{3,2,1,0:T(8,128)(2,1)S(1)}, u32[]{:S(2)}) copy-start(bf16[8,2,128,256]{3,2,1,0:T(8,128)(2,1)S(1)} %all-to-all-done.3.h_ref) | copy-start | bytes 3145732
  81.3 68.3 %all-to-all-start.2 = ((bf16[8,2,128,256]{3,2,1,0:T(8,128)(2,1)}), bf16[8,2,128,256]{3,2,1,0:T(8,128)(2,1)S(1)}, u32[]{:S(2)}, u32[]{:S(2)}) async-start(bf16[8,2,128,256]{3,2,1,0:T(8,128)(2,1)} %broadcast_in_dim.20), calls=%async_computation.2 | async-start | bytes 2097152 | tf_op jit(solution)/shard_map/all_to_all | solution.py:279
  95.7 40.2 %collective-permute-start.7 = (bf16[136,2048]{1,0:T(8,128)(2,1)}, bf16[136,2048]{1,0:T(8,128)(2,1)}, u32[]{:S(2)}, u32[]{:S(2)}) collective-permute-start(bf16[136,2048]{1,0:T(8,128)(2,1)} %get-tuple-element.39), channel_id=1, source_target_pairs={{1,0},{2,1},{3,2},{4,3},{5,4},{6,5},{7,6},{8,7},{9,8},{10,9},{11,1... | collective-permute-start | bytes 1671176 | tf_op jit(solution)/shard_map/ppermute | solution.py:343
  103.2 46.5 %collective-permute-start.5 = (bf16[136,2048]{1,0:T(8,128)(2,1)}, bf16[136,2048]{1,0:T(8,128)(2,1)S(1)}, u32[]{:S(2)}, u32[]{:S(2)}) collective-permute-start(bf16[136,2048]{1,0:T(8,128)(2,1)} %get-tuple-element.37), channel_id=1, source_target_pairs={{1,0},{2,1},{3,2},{4,3},{5,4},{6,5},{7,6},{8,7},{9,8},{10,9},{11,1... | collective-permute-start | bytes 1671176 | tf_op jit(solution)/shard_map/ppermute | solution.py:343
  110.7 0.8 copy-start.11
  111.5 53.0 %collective-permute-start.3 = (bf16[136,2048]{1,0:T(8,128)(2,1)}, bf16[136,2048]{1,0:T(8,128)(2,1)S(1)}, u32[]{:S(2)}, u32[]{:S(2)}) collective-permute-start(bf16[136,2048]{1,0:T(8,128)(2,1)} %get-tuple-element.35), channel_id=1, source_target_pairs={{1,0},{2,1},{3,2},{4,3},{5,4},{6,5},{7,6},{8,7},{9,8},{10,9},{11,1... | collective-permute-start | bytes 1671176 | tf_op jit(solution)/shard_map/ppermute | solution.py:343
  112.8 36.8 %collective-permute-start.4 = (bf16[128,2048]{1,0:T(8,128)(2,1)}, bf16[128,2048]{1,0:T(8,128)(2,1)}, u32[]{:S(2)}, u32[]{:S(2)}) collective-permute-start(bf16[128,2048]{1,0:T(8,128)(2,1)} %get-tuple-element.36), channel_id=1, source_target_pairs={{0,1},{1,2},{2,3},{3,4},{4,5},{5,6},{6,7},{7,8},{8,9},{9,10},{10,1... | collective-permute-start | bytes 1572872 | tf_op jit(solution)/shard_map/ppermute | solution.py:342
  118.9 3.3 %copy-start.9 = (bf16[136,2048]{1,0:T(8,128)(2,1)}, bf16[136,2048]{1,0:T(8,128)(2,1)S(1)}, u32[]{:S(2)}) copy-start(bf16[136,2048]{1,0:T(8,128)(2,1)S(1)} %collective-permute-done.9.dz_next) | copy-start | bytes 1671172
  118.9 45.6 %collective-permute-start.2 = (bf16[128,2048]{1,0:T(8,128)(2,1)}, bf16[128,2048]{1,0:T(8,128)(2,1)S(1)}, u32[]{:S(2)}, u32[]{:S(2)}) collective-permute-start(bf16[128,2048]{1,0:T(8,128)(2,1)} %get-tuple-element.34), channel_id=1, source_target_pairs={{0,1},{1,2},{2,3},{3,4},{4,5},{5,6},{6,7},{7,8},{8,9},{9,10},{10,1... | collective-permute-start | bytes 1572872 | tf_op jit(solution)/shard_map/ppermute | solution.py:342
  149.6 1.0 copy-start.3
  149.7 1.1 copy-start.8
  164.5 0.8 copy-start.10
  164.5 1.0 copy-start.7
  165.5 33.6 %copy-start.6 = (bf16[8,152,256]{2,1,0:T(8,128)(2,1)S(1)}, bf16[8,152,256]{2,1,0:T(8,128)(2,1)}, u32[]{:S(2)}) copy-start(bf16[8,152,256]{2,1,0:T(8,128)(2,1)} %get-tuple-element.60) | copy-start | bytes 1867780
  179.2 32.0 %copy-start.5 = (bf16[8,152,256]{2,1,0:T(8,128)(2,1)S(1)}, bf16[8,152,256]{2,1,0:T(8,128)(2,1)}, u32[]{:S(2)}) copy-start(bf16[8,152,256]{2,1,0:T(8,128)(2,1)} %get-tuple-element.59) | copy-start | bytes 1867780
  223.2 13.1 %all-to-all-start.4 = ((bf16[8,152,256]{2,1,0:T(8,128)(2,1)}), bf16[8,152,256]{2,1,0:T(8,128)(2,1)S(1)}, u32[]{:S(2)}, u32[]{:S(2)}) async-start(bf16[8,152,256]{2,1,0:T(8,128)(2,1)} %get-tuple-element.58), calls=%async_computation.4 | async-start | bytes 1245184 | tf_op jit(solution)/shard_map/all_to_all | solution.py:279

commit v3 on v2

--- a/solution.py
+++ b/solution.py
@@ -10,6 +10,7 @@
 
 
 PARTS = 4
+CHUNKS = ((0, 2), (2, 2))
 BF = jnp.bfloat16
 F32 = jnp.float32
 LANES = 128
@@ -53,8 +54,9 @@
     return jnp.dot(a, b, preferred_element_type=F32)
 
 
-def row_of(ref, index, lanes):
-    return ref[0, pl.ds(index, 1), lanes]
+def row_of(ref, index, col):
+    per = ref.shape[2] // LANES
+    return ref[col // per, pl.ds(index, 1), pl.ds(col % per * LANES, LANES)]
 
 
 def load_padded(dst, own_ref, before, after, lanes, block):
@@ -63,10 +65,10 @@
     dst[pl.ds(ROW + block, ROW), :] = after
 
 
-def causal(src, taps, first, width, lanes, rows):
+def causal(src, taps, first, width, col, rows):
     total = None
     for offset in range(width):
-        term = row_of(taps, first + offset, lanes) * src[pl.ds(ROW - offset, rows), :]
+        term = row_of(taps, first + offset, col) * src[pl.ds(ROW - offset, rows), :]
         total = term if total is None else total + term
     return total
 
@@ -83,10 +85,10 @@
                 lanes,
                 block,
             )
-        k_s = causal(x_k.at[col], taps, width, width, lanes, block)
-        v_s = causal(x_v.at[col], taps, 2 * width, width, lanes, block)
+        k_s = causal(x_k.at[col], taps, width, width, col, block)
+        v_s = causal(x_v.at[col], taps, 2 * width, width, col, block)
         u_out[:, lanes] = (k_s * v_s).astype(BF)
-        q_s = causal(x_q.at[col], taps, 0, width, lanes, block + ROW)
+        q_s = causal(x_q.at[col], taps, 0, width, col, block + ROW)
         dz_out[0:block, lanes] = (go[0, :, lanes].astype(F32) * q_s[0:block]).astype(BF)
         dz_out[block : block + ROW, lanes] = (
             fore[3, :, lanes].astype(F32) * q_s[block : block + ROW]
@@ -160,15 +162,15 @@
                 lanes,
                 block,
             )
-        q_s = causal(x_q.at[col], taps, 0, width, lanes, rows)
+        q_s = causal(x_q.at[col], taps, 0, width, col, rows)
         s_q[col] = q_s
         dz = (go[0, :, lanes].astype(F32) * q_s[0:block]).astype(BF)
         dz_own[:, lanes] = dz
         z_pad[col, 0:ROW, :] = jnp.zeros((ROW, LANES), F32)
         z_pad[col, ROW : 2 * ROW, :] = dz[0:ROW].astype(F32)
-        k_s = causal(x_k.at[col], taps, width, width, lanes, rows)
+        k_s = causal(x_k.at[col], taps, width, width, col, rows)
         s_k[col] = k_s
-        v_s = causal(x_v.at[col], taps, 2 * width, width, lanes, rows)
+        v_s = causal(x_v.at[col], taps, 2 * width, width, col, rows)
         s_v[col] = v_s
         u = (k_s * v_s).astype(BF)
         window[0:block, lanes] = u[0:block]
@@ -242,7 +244,7 @@
         z = jnp.concatenate([z[0:ROW] + z_fix, z[ROW:]], axis=0)
         du = jnp.concatenate([du[0:block], du[block:] + du_fix], axis=0)
         gm = jnp.concatenate([gm[0 : block - ROW], gm[block - ROW : block] + g_fix], axis=0)
-        g_part[0, 0:block, lanes] = gm.astype(BF)
+        g_part[0, 0, 0:block, lanes] = gm.astype(BF)
         mixed[0, :, lanes] = (s_q[col, 0:block, :] * z[0:block]).astype(BF)
         g_pad[0, 0:block, :] = go[0, :, lanes].astype(F32) * z[0:block]
         g_pad[0, block:rows, :] = fore[3, :, lanes].astype(F32) * z[block:rows]
@@ -253,12 +255,12 @@
             total = None
             for offset in range(width):
                 moved = g_pad[which, pl.ds(offset, block), :]
-                term = row_of(taps, which * width + offset, lanes) * moved
+                term = row_of(taps, which * width + offset, col) * moved
                 total = term if total is None else total + term
                 place = which * width + offset
                 sums[place : place + 1, :] = jnp.sum(values * moved, axis=0, keepdims=True)
             out[0, :, lanes] = total.astype(BF)
-        g_part[0, block : block + 3 * ROW, lanes] = sums[...].astype(BF)
+        g_part[0, 0, block : block + 3 * ROW, lanes] = sums[...].astype(BF)
 
 
 def halo_pairs(count):
@@ -297,6 +299,9 @@
     forward, inverse = transforms(block, width)
     tables = [part for pair in forward + [inverse] for part in pair]
 
+    mine = spread(med_filter.astype(BF).T, parts * n_dp, ("context", "dp"), both)
+    mine = mine.reshape(parts, block, group)
+
     back = jnp.concatenate([x[:, block - ROW :] for x in (query_in, key_in, value_in)], axis=0)
     fore = jnp.concatenate([x[:, :ROW] for x in (query_in, key_in, value_in, grad_out)], axis=0)
     back = lax.ppermute(back, "context", ahead)
@@ -305,68 +310,69 @@
     short = short_filter.transpose(0, 2, 1).reshape(3 * width, group)
     short = jnp.pad(short, ((0, held_short - 3 * width), (0, 0)))
     taps = spread(short, n_context, "context")
-
-    mine = spread(med_filter.astype(BF).T, parts * n_dp, ("context", "dp"), both)
-    mine = mine.reshape(parts, block, group)
-    h_all = []
-    for place in range(2):
-        first = place * (parts // 2)
-        h_all.append(spread(mine[first : first + parts // 2], coarse, "context", outer))
-
-    cols = group // LANES
-    grid = (coarse,)
-    padded = pltpu.VMEM((cols, block + 2 * ROW, LANES), F32)
-    shifted = pltpu.VMEM((cols, rows, LANES), F32)
-    whole = lambda x: pl.BlockSpec(x.shape, lambda i: (0,) * x.ndim)
-    packed = lambda height: pl.BlockSpec((height, group), lambda i: (0, i))
-    outs = None
-    partials = []
+    h_all = spread(mine, coarse, "context", outer)
+
+    whole = lambda x: pl.BlockSpec(x.shape, lambda *_: (0,) * x.ndim)
     pieces = []
-    for part in range(parts):
-        tokens = pl.BlockSpec((1, block, group), lambda i, part=part: (0, 0, parts * i + part))
-        stack = lambda count, part=part: pl.BlockSpec(
-            (count, ROW, group), lambda i: (0, 0, parts * i + part)
-        )
-        filters = pl.BlockSpec((1, held_short, group), lambda i, part=part: (parts * i + part, 0, 0))
+    for first, count in CHUNKS:
+        wide = count * group
+        per = parts // count
+        place = first // count
+        cols = wide // LANES
+        padded = pltpu.VMEM((cols, block + 2 * ROW, LANES), F32)
+        at = lambda i, per=per, place=place: per * i + place
+        tokens = pl.BlockSpec((1, block, wide), lambda i, at=at: (0, 0, at(i)))
+        stack = lambda height, at=at: pl.BlockSpec((height, ROW, wide), lambda i: (0, 0, at(i)))
+        filters = pl.BlockSpec((count, held_short, group), lambda i, at=at: (at(i), 0, 0))
+        packed = lambda height: pl.BlockSpec((height, wide), lambda i: (0, i))
         u, dz = pl.pallas_call(
             functools.partial(make_products, block, width, cols),
-            grid=grid,
+            grid=(coarse,),
             in_specs=[tokens] * 4 + [stack(3), stack(4), filters],
             out_specs=[packed(block), packed(rows)],
             out_shape=[
-                jax.ShapeDtypeStruct((block, coarse * group), BF),
-                jax.ShapeDtypeStruct((rows, coarse * group), BF),
+                jax.ShapeDtypeStruct((block, coarse * wide), BF),
+                jax.ShapeDtypeStruct((rows, coarse * wide), BF),
             ],
             scratch_shapes=[padded] * 3,
         )(query_in, key_in, value_in, grad_out, back, fore, taps)
         u_prev = lax.ppermute(u, "context", ahead)
         dz_next = lax.ppermute(dz, "context", behind)
         pieces.append((u_prev, dz_next))
-    for part in range(parts):
-        tokens = pl.BlockSpec((1, block, group), lambda i, part=part: (0, 0, parts * i + part))
-        stack = lambda count, part=part: pl.BlockSpec(
-            (count, ROW, group), lambda i: (0, 0, parts * i + part)
+
+    outs = None
+    partials = []
+    cols = group // LANES
+    padded = pltpu.VMEM((cols, block + 2 * ROW, LANES), F32)
+    shifted = pltpu.VMEM((cols, rows, LANES), F32)
+    for index, (first, count) in enumerate(CHUNKS):
+        at = lambda i, j, first=first: parts * i + first + j
+        tokens = pl.BlockSpec((1, block, group), lambda i, j, at=at: (0, 0, at(i, j)))
+        stack = lambda height, at=at: pl.BlockSpec(
+            (height, ROW, group), lambda i, j: (0, 0, at(i, j))
         )
-        filters = pl.BlockSpec((1, held_short, group), lambda i, part=part: (parts * i + part, 0, 0))
-        half = parts // 2
+        filters = pl.BlockSpec((1, held_short, group), lambda i, j, at=at: (at(i, j), 0, 0))
+        packed = lambda height, count=count: pl.BlockSpec(
+            (height, group), lambda i, j: (0, count * i + j)
+        )
         taps_h = pl.BlockSpec(
-            (1, None, block, group), lambda i, part=part: (i, part % half, 0, 0)
+            (1, None, block, group), lambda i, j, first=first: (i, first + j, 0, 0)
         )
-        u_prev, dz_next = pieces[part]
+        u_prev, dz_next = pieces[index]
         carried = [] if outs is None else list(outs)
         fixed = [query_in, key_in, value_in, grad_out, back, fore, taps, u_prev, dz_next]
-        fixed += [h_all[part // half], *tables]
+        fixed += [h_all, *tables]
         *outs, partial = pl.pallas_call(
             functools.partial(mixer, block, width, cols),
-            grid=grid,
+            grid=(coarse, count),
             in_specs=[tokens] * 4
             + [stack(3), stack(4), filters, packed(block), packed(rows), taps_h]
             + [whole(x) for x in tables]
             + [pl.BlockSpec(memory_space=pl.ANY)] * len(carried),
             out_specs=[tokens] * 4
-            + [pl.BlockSpec((1, block + held_short, group), lambda i: (i, 0, 0))],
+            + [pl.BlockSpec((1, 1, block + held_short, group), lambda i, j: (i, j, 0, 0))],
             out_shape=[jax.ShapeDtypeStruct(query_in.shape, BF)] * 4
-            + [jax.ShapeDtypeStruct((coarse, block + held_short, group), BF)],
+            + [jax.ShapeDtypeStruct((coarse, count, block + held_short, group), BF)],
             scratch_shapes=[
                 pltpu.VMEM((held_short, LANES), F32),
                 padded,
@@ -390,16 +396,17 @@
                 pltpu.VMEM((3, size, group), BF),
                 pltpu.VMEM((3, size, group), BF),
             ],
-            input_output_aliases={len(fixed) + place: place for place in range(len(carried))},
+            input_output_aliases={len(fixed) + k: k for k in range(len(carried))},
         )(*fixed, *carried)
         arrived = exchange(partial, "context", outer)
         partials.append(jnp.sum(arrived.astype(F32), axis=0))
 
-    total = jnp.stack(partials)
+    total = jnp.concatenate(partials, axis=0).astype(BF)
     med = total[:, :block].reshape(parts, n_dp, taps_own, group)
     extra = jnp.broadcast_to(total[:, None, block:], (parts, n_dp, held_short, group))
     sent = jnp.concatenate([med, extra], axis=2).reshape(parts * n_dp, taps_own + held_short, group)
-    final = jnp.sum(exchange(sent, ("context", "dp"), both), axis=0)
+    sent = exchange(sent, ("context", "dp"), both)
+    final = jnp.sum(sent.astype(F32), axis=0)
     grad_med = final[:taps_own].T
     grad_short = final[taps_own : taps_own + 3 * width].reshape(3, width, group).transpose(0, 2, 1)
     return (*outs, grad_med, grad_short)

time: 267 us -> 245 us (0.918)
  starting transfers between devices: 65 us -> 39.7 us
  waiting for transfers between devices: 33.3 us -> 57.1 us
  Pallas kernels: 79.7 us -> 67 us
  blocking collectives: 70.5 us -> 64.4 us
    ppermute x4 -> x2, waiting for transfers between devices: 0.01 us -> 16.1 us  [per_device(): u_prev = lax.ppermute(u, 'context', ahead)]
    all_to_all x5 -> x4, starting transfers between devices: 37.1 us -> 23 us  [exchange(): return lax.all_to_all(x, axes, 0, 0, axis_index_groups=groups)]
    pallas_call x4 -> x2, Pallas kernels: 24.8 us -> 15.6 us  [per_device(): pl.pallas_call(functools.partial(make_products, block, width, cols), grid...]
    ppermute x4 -> x2, starting transfers between devices: 18.3 us -> 9.7 us  [per_device(): u_prev = lax.ppermute(u, 'context', ahead)]
    all_to_all x5 -> x4, waiting for transfers between devices: 26.3 us -> 34 us  [exchange(): return lax.all_to_all(x, axes, 0, 0, axis_index_groups=groups)]
    all_to_all x4 -> x2, blocking collectives: 70.5 us -> 64.4 us  [exchange(): return lax.all_to_all(x, axes, 0, 0, axis_index_groups=groups)]
    pallas_call x4 -> x2, Pallas kernels: 54.9 us -> 51.4 us  [per_device(): pl.pallas_call(functools.partial(mixer, block, width, cols), grid=(coarse...]
  transfers between devices with their start and end apart: 15 -> 10, of which waited for: 4 -> 5; matrix products, arithmetic and copies ran while one was open for 2% -> 3% of each run, Pallas kernels for 25% -> 17%
where the time goes in v3:
time: 245 us; the launch traced here: 244 us
  Pallas kernels  67 us (27%)
  blocking collectives  64.4 us (26%)
  waiting for transfers between devices  57.1 us (23%)
  starting transfers between devices  39.7 us (16%)
  local copies, waits for them, and re-layouts  11.9 us (5%)
  other arithmetic  3.15 us (1%)
    all_to_all x2, blocking collectives, exchange(): return lax.all_to_all(x, axes, 0, 0, axis_index_groups=groups)  64.4 us
    pallas_call x2, Pallas kernels, per_device(): pl.pallas_call(functools.partial(mixer, block, width, cols), grid=(coarse...  51.4 us
    all_to_all x4, waiting for transfers between devices, exchange(): return lax.all_to_all(x, axes, 0, 0, axis_index_groups=groups)  34 us
    all_to_all x4, starting transfers between devices, exchange(): return lax.all_to_all(x, axes, 0, 0, axis_index_groups=groups)  23 us
    ppermute x2, waiting for transfers between devices, per_device(): u_prev = lax.ppermute(u, 'context', ahead)  16.1 us
    pallas_call x2, Pallas kernels, per_device(): pl.pallas_call(functools.partial(make_products, block, width, cols), grid...  15.6 us
    ppermute x2, starting transfers between devices, per_device(): u_prev = lax.ppermute(u, 'context', ahead)  9.7 us
    ppermute x1, waiting for transfers between devices, per_device(): back = lax.ppermute(back, 'context', ahead)  6.95 us
  transfers between devices with their start and end apart: 10, of which 5 were waited for; matrix products, arithmetic and copies ran while one was open for 3% of the time, Pallas kernels for 17%

profile of v3, /device:TPU:1, one launch (start us, length us, event | category | flops | bytes accessed | tf_op | source)
XLA Modules:
  0.0 244.1 jit_solution(12697174625677146866)
XLA Ops:
  0.6 0.8 convert_bitcast_fusion
  2.1 7.8 %all-to-all-start.1 = ((bf16[16,32,256]{2,1,0:T(8,128)(2,1)}), bf16[16,32,256]{2,1,0:T(8,128)(2,1)S(1)}, u32[]{:S(2)}, u32[]{:S(2)}) async-start(bf16[16,32,256]{2,1,0:T(8,128)(2,1)} %broadcast_in_dim.16), calls=%async_computation.1 | async-start | bytes 524288 | tf_op jit(solution)/shard_map/all_to_all | solution.py:281
  10.0 1.9 fusion.1
  11.8 1.6 fusion.3
  13.5 3.7 %all-to-all-done.1 = bf16[16,32,256]{2,1,0:T(8,128)(2,1)S(1)} async-done(((bf16[16,32,256]{2,1,0:T(8,128)(2,1)}), bf16[16,32,256]{2,1,0:T(8,128)(2,1)S(1)}, u32[]{:S(2)}, u32[]{:S(2)}) %all-to-all-start.1) | async-done | bytes 262176 | tf_op jit(solution)/shard_map/all_to_all | solution.py:281
  17.2 0.9 broadcast_in_dim.15
  18.1 7.6 %all-to-all-start = ((f32[32,24,256]{2,1,0:T(8,128)}), f32[32,24,256]{2,1,0:T(8,128)S(1)}, u32[]{:S(2)}, u32[]{:S(2)}) async-start(f32[32,24,256]{2,1,0:T(8,128)} %broadcast_in_dim.15), calls=%async_computation | async-start | bytes 1572864 | tf_op jit(solution)/shard_map/all_to_all | solution.py:281
  25.7 0.9 pad_maximum_fusion
  26.5 1.3 collective-permute-start.1
  27.8 12.0 %all-to-all-done.taps = f32[32,24,256]{2,1,0:T(8,128)S(1)} async-done(((f32[32,24,256]{2,1,0:T(8,128)}), f32[32,24,256]{2,1,0:T(8,128)S(1)}, u32[]{:S(2)}, u32[]{:S(2)}) %all-to-all-start) | async-done | bytes 786464 | tf_op jit(solution)/shard_map/all_to_all | solution.py:281
  39.8 1.6 broadcast_in_dim.17
  41.4 4.0 %all-to-all-start.2 = ((bf16[8,4,128,256]{3,2,1,0:T(8,128)(2,1)}), bf16[8,4,128,256]{3,2,1,0:T(8,128)(2,1)S(1)}, u32[]{:S(2)}, u32[]{:S(2)}) async-start(bf16[8,4,128,256]{3,2,1,0:T(8,128)(2,1)} %broadcast_in_dim.17), calls=%async_computation.2 | async-start | bytes 4194304 | tf_op jit(solution)/shard_map/all_to_all | solution.py:281
  45.4 1.0 pad_maximum_fusion.2
  46.4 3.2 %collective-permute-start = (bf16[3,8,8192]{2,1,0:T(8,128)(2,1)S(1)}, bf16[3,8,8192]{2,1,0:T(8,128)(2,1)S(1)}, u32[]{:S(2)}, u32[]{:S(2)}) collective-permute-start(bf16[3,8,8192]{2,1,0:T(8,128)(2,1)S(1)} %pad_maximum_fusion.2), channel_id=1, source_target_pairs={{0,1},{1,2},{2,3},{3,4},{4,5},{5,6},{6,7},{7,8},{8,9},{9,10},{10,1... | collective-permute-start | bytes 1179656 | tf_op jit(solution)/shard_map/ppermute | solution.py:307
  49.7 6.9 %collective-permute-done.back = bf16[3,8,8192]{2,1,0:T(8,128)(2,1)S(1)} collective-permute-done((bf16[3,8,8192]{2,1,0:T(8,128)(2,1)S(1)}, bf16[3,8,8192]{2,1,0:T(8,128)(2,1)S(1)}, u32[]{:S(2)}, u32[]{:S(2)}) %collective-permute-start) | collective-permute-done | bytes 393248 | tf_op jit(solution)/shard_map/ppermute | solution.py:307
  56.6 0.7 copy-done.3
  57.3 0.8 copy-done.2
  58.2 7.7 %shard_map.182 = (bf16[128,4096]{1,0:T(8,128)(2,1)}, bf16[136,4096]{1,0:T(8,128)(2,1)}) custom-call(bf16[1,128,8192]{2,1,0:T(8,128)(2,1)} %q.7, bf16[1,128,8192]{2,1,0:T(8,128)(2,1)} %k.7, bf16[1,128,8192]{2,1,0:T(8,128)(2,1)} %v.7, bf16[1,128,8192]{2,1,0:T(8,128)(2,1)} %go.7, bf16[3,8,8192]{2,1,0:T(8,128)(2,1)} %copy-done.3, bf16[4,8,8192]{2,1,0:T(8,128)(2,1)} %copy-done.2, ...), custom_call_target="tpu_custom_call" | custom-call | tf_op jit(solution)/shard_map/pallas_call | solution.py:328
  65.9 1.3 collective-permute-start.5
  67.2 7.9 %shard_map.181 = (bf16[128,4096]{1,0:T(8,128)(2,1)}, bf16[136,4096]{1,0:T(8,128)(2,1)}) custom-call(bf16[1,128,8192]{2,1,0:T(8,128)(2,1)} %q.7, bf16[1,128,8192]{2,1,0:T(8,128)(2,1)} %k.7, bf16[1,128,8192]{2,1,0:T(8,128)(2,1)} %v.7, bf16[1,128,8192]{2,1,0:T(8,128)(2,1)} %go.7, bf16[3,8,8192]{2,1,0:T(8,128)(2,1)} %copy-done.3, bf16[4,8,8192]{2,1,0:T(8,128)(2,1)} %copy-done.2, ...), custom_call_target="tpu_custom_call" | custom-call | tf_op jit(solution)/shard_map/pallas_call | solution.py:328
  75.0 1.3 collective-permute-start.3
  76.3 5.4 %collective-permute-start.4 = (bf16[128,4096]{1,0:T(8,128)(2,1)}, bf16[128,4096]{1,0:T(8,128)(2,1)S(1)}, u32[]{:S(2)}, u32[]{:S(2)}) collective-permute-start(bf16[128,4096]{1,0:T(8,128)(2,1)} %get-tuple-element.22), channel_id=1, source_target_pairs={{0,1},{1,2},{2,3},{3,4},{4,5},{5,6},{6,7},{7,8},{8,9},{9,10},{10,1... | collective-permute-start | bytes 3145736 | tf_op jit(solution)/shard_map/ppermute | solution.py:339
  81.8 4.3 %collective-permute-start.2 = (bf16[128,4096]{1,0:T(8,128)(2,1)}, bf16[128,4096]{1,0:T(8,128)(2,1)}, u32[]{:S(2)}, u32[]{:S(2)}) collective-permute-start(bf16[128,4096]{1,0:T(8,128)(2,1)} %get-tuple-element.20), channel_id=1, source_target_pairs={{0,1},{1,2},{2,3},{3,4},{4,5},{5,6},{6,7},{7,8},{8,9},{9,10},{10,1... | collective-permute-start | bytes 3145736 | tf_op jit(solution)/shard_map/ppermute | solution.py:339
  86.0 16.1 %collective-permute-done.4.u_prev = bf16[128,4096]{1,0:T(8,128)(2,1)S(1)} collective-permute-done((bf16[128,4096]{1,0:T(8,128)(2,1)}, bf16[128,4096]{1,0:T(8,128)(2,1)S(1)}, u32[]{:S(2)}, u32[]{:S(2)}) %collective-permute-start.4) | collective-permute-done | bytes 1048608 | tf_op jit(solution)/shard_map/ppermute | solution.py:339
  102.2 1.0 copy-done.4
  103.2 1.4 copy-done.1
  104.5 25.7 %shard_map.183 = (bf16[1,128,8192]{2,1,0:T(8,128)(2,1)}, bf16[1,128,8192]{2,1,0:T(8,128)(2,1)}, bf16[1,128,8192]{2,1,0:T(8,128)(2,1)}, bf16[1,128,8192]{2,1,0:T(8,128)(2,1)}, bf16[8,2,152,256]{3,2,1,0:T(8,128)(2,1)}) custom-call(bf16[1,128,8192]{2,1,0:T(8,128)(2,1)} %q.7, bf16[1,128,8192]{2,1,0:T(8,128)(2,1)} %k.7, bf16[1,128,8192]{2,1,0:T(8,128)(2,1)} %v.7, ...), custom_call_target="tpu_custom_call" | custom-call | tf_op jit(solution)/shard_map/pallas_call | solution.py:365
  130.2 25.8 %shard_map.184 = (bf16[1,128,8192]{2,1,0:T(8,128)(2,1)}, bf16[1,128,8192]{2,1,0:T(8,128)(2,1)}, bf16[1,128,8192]{2,1,0:T(8,128)(2,1)}, bf16[1,128,8192]{2,1,0:T(8,128)(2,1)}, bf16[8,2,152,256]{3,2,1,0:T(8,128)(2,1)}) custom-call(bf16[1,128,8192]{2,1,0:T(8,128)(2,1)} %q.7, ...), custom_call_target="tpu_custom_call", output_to_operand_aliasing={{0}: (18, {}), {1}: (19, {}), {2}: (20, {}), {3}: (21, {})} | custom-call | tf_op jit(solution)/shard_map/pallas_call | solution.py:365
  156.0 51.2 %all_to_all.30 = bf16[8,2,152,256]{3,2,1,0:T(8,128)(2,1)S(1)} all-to-all(bf16[8,2,152,256]{3,2,1,0:T(8,128)(2,1)} %get-tuple-element.33), channel_id=1, replica_groups={{0,4,8,12,16,20,24,28},{1,5,9,13,17,21,25,29},{2,6,10,14,18,22,26,30},{..., dimensions={0} | all-to-all | bytes 2490368 | tf_op jit(solution)/shard_map/all_to_all | solution.py:281
  207.2 3.6 %all-to-all-start.3 = ((bf16[8,2,152,256]{3,2,1,0:T(8,128)(2,1)}), bf16[8,2,152,256]{3,2,1,0:T(8,128)(2,1)S(1)}, u32[]{:S(2)}, u32[]{:S(2)}) async-start(bf16[8,2,152,256]{3,2,1,0:T(8,128)(2,1)} %get-tuple-element.32), calls=%async_computation.3 | async-start | bytes 2490368 | tf_op jit(solution)/shard_map/all_to_all | solution.py:281
  211.0 18.3 %all-to-all-done.3 = bf16[8,2,152,256]{3,2,1,0:T(8,128)(2,1)S(1)} async-done(((bf16[8,2,152,256]{3,2,1,0:T(8,128)(2,1)}), bf16[8,2,152,256]{3,2,1,0:T(8,128)(2,1)S(1)}, u32[]{:S(2)}, u32[]{:S(2)}) %all-to-all-start.3) | async-done | bytes 1245216 | tf_op jit(solution)/shard_map/all_to_all | solution.py:281
  229.6 13.2 %all_to_all.31 = bf16[16,56,256]{2,1,0:T(8,128)(2,1)S(1)} all-to-all(bf16[16,56,256]{2,1,0:T(8,128)(2,1)S(1)} %pad_maximum_fusion.1), channel_id=1, replica_groups={{0,32,64,96,1,33,65,97,2,34,66,98,3,35,67,99},{4,36,68,100,5,37,69,101,..., dimensions={0} | all-to-all | bytes 917504 | tf_op jit(solution)/shard_map/all_to_all | solution.py:281
  (30 shorter events, 2.5 us)
Async XLA Ops:
  0.6 12.8 %copy-start.6 = (f32[3,256,7]{1,2,0:T(8,128)S(1)}, f32[3,256,7]{1,2,0:T(8,128)}, u32[]{:S(2)}) copy-start(f32[3,256,7]{1,2,0:T(8,128)} %param.19) | copy-start | bytes 64516
  2.1 15.0 %all-to-all-start.1 = ((bf16[16,32,256]{2,1,0:T(8,128)(2,1)}), bf16[16,32,256]{2,1,0:T(8,128)(2,1)S(1)}, u32[]{:S(2)}, u32[]{:S(2)}) async-start(bf16[16,32,256]{2,1,0:T(8,128)(2,1)} %broadcast_in_dim.16), calls=%async_computation.1 | async-start | bytes 524288 | tf_op jit(solution)/shard_map/all_to_all | solution.py:281
  10.0 15.7 %slice-start = ((bf16[1,128,8192]{2,1,0:T(8,128)(2,1)}), bf16[1,8,8192]{2,1,0:T(8,128)(2,1)S(1)}, s32[]{:S(2)}) async-start(bf16[1,128,8192]{2,1,0:T(8,128)(2,1)} %go.7), calls=%async_computation.6 | async-start | bytes 262144 | tf_op jit(solution)/shard_map/slice | solution.py:306
  18.1 21.7 %all-to-all-start = ((f32[32,24,256]{2,1,0:T(8,128)}), f32[32,24,256]{2,1,0:T(8,128)S(1)}, u32[]{:S(2)}, u32[]{:S(2)}) async-start(f32[32,24,256]{2,1,0:T(8,128)} %broadcast_in_dim.15), calls=%async_computation | async-start | bytes 1572864 | tf_op jit(solution)/shard_map/all_to_all | solution.py:281
  26.5 30.1 %collective-permute-start.1 = (bf16[4,8,8192]{2,1,0:T(8,128)(2,1)}, bf16[4,8,8192]{2,1,0:T(8,128)(2,1)S(1)}, u32[]{:S(2)}, u32[]{:S(2)}) collective-permute-start(bf16[4,8,8192]{2,1,0:T(8,128)(2,1)} %pad_maximum_fusion), channel_id=1, source_target_pairs={{1,0},{2,1},{3,2},{4,3},{5,4},{6,5},{7,6},{8,7},{9,8},{10,9},{11,1... | collective-permute-start | bytes 1572872 | tf_op jit(solution)/shard_map/ppermute | solution.py:308
  39.8 1.6 copy-start
  41.4 4.0 %copy-start.5 = (bf16[1,8,8192]{2,1,0:T(8,128)(2,1)S(1)}, bf16[1,8,8192]{2,1,0:T(8,128)(2,1)}, u32[]{:S(2)}) copy-start(bf16[1,8,8192]{2,1,0:T(8,128)(2,1)} %get-tuple-element.39) | copy-start | bytes 393220
  41.4 61.7 %all-to-all-start.2 = ((bf16[8,4,128,256]{3,2,1,0:T(8,128)(2,1)}), bf16[8,4,128,256]{3,2,1,0:T(8,128)(2,1)S(1)}, u32[]{:S(2)}, u32[]{:S(2)}) async-start(bf16[8,4,128,256]{3,2,1,0:T(8,128)(2,1)} %broadcast_in_dim.17), calls=%async_computation.2 | async-start | bytes 4194304 | tf_op jit(solution)/shard_map/all_to_all | solution.py:281
  46.4 10.2 %collective-permute-start = (bf16[3,8,8192]{2,1,0:T(8,128)(2,1)S(1)}, bf16[3,8,8192]{2,1,0:T(8,128)(2,1)S(1)}, u32[]{:S(2)}, u32[]{:S(2)}) collective-permute-start(bf16[3,8,8192]{2,1,0:T(8,128)(2,1)S(1)} %pad_maximum_fusion.2), channel_id=1, source_target_pairs={{0,1},{1,2},{2,3},{3,4},{4,5},{5,6},{6,7},{7,8},{8,9},{9,10},{10,1... | collective-permute-start | bytes 1179656 | tf_op jit(solution)/shard_map/ppermute | solution.py:307
  56.6 0.7 copy-start.3
  57.3 0.8 copy-start.2
  65.9 37.3 %collective-permute-start.5 = (bf16[136,4096]{1,0:T(8,128)(2,1)}, bf16[136,4096]{1,0:T(8,128)(2,1)}, u32[]{:S(2)}, u32[]{:S(2)}) collective-permute-start(bf16[136,4096]{1,0:T(8,128)(2,1)} %get-tuple-element.23), channel_id=1, source_target_pairs={{1,0},{2,1},{3,2},{4,3},{5,4},{6,5},{7,6},{8,7},{9,8},{10,9},{11,1... | collective-permute-start | bytes 3342344 | tf_op jit(solution)/shard_map/ppermute | solution.py:340
  75.0 55.2 %collective-permute-start.3 = (bf16[136,4096]{1,0:T(8,128)(2,1)}, bf16[136,4096]{1,0:T(8,128)(2,1)}, u32[]{:S(2)}, u32[]{:S(2)}) collective-permute-start(bf16[136,4096]{1,0:T(8,128)(2,1)} %get-tuple-element.21), channel_id=1, source_target_pairs={{1,0},{2,1},{3,2},{4,3},{5,4},{6,5},{7,6},{8,7},{9,8},{10,9},{11,1... | collective-permute-start | bytes 3342344 | tf_op jit(solution)/shard_map/ppermute | solution.py:340
  76.3 25.8 %collective-permute-start.4 = (bf16[128,4096]{1,0:T(8,128)(2,1)}, bf16[128,4096]{1,0:T(8,128)(2,1)S(1)}, u32[]{:S(2)}, u32[]{:S(2)}) collective-permute-start(bf16[128,4096]{1,0:T(8,128)(2,1)} %get-tuple-element.22), channel_id=1, source_target_pairs={{0,1},{1,2},{2,3},{3,4},{4,5},{5,6},{6,7},{7,8},{8,9},{9,10},{10,1... | collective-permute-start | bytes 3145736 | tf_op jit(solution)/shard_map/ppermute | solution.py:339
  81.8 48.4 %collective-permute-start.2 = (bf16[128,4096]{1,0:T(8,128)(2,1)}, bf16[128,4096]{1,0:T(8,128)(2,1)}, u32[]{:S(2)}, u32[]{:S(2)}) collective-permute-start(bf16[128,4096]{1,0:T(8,128)(2,1)} %get-tuple-element.20), channel_id=1, source_target_pairs={{0,1},{1,2},{2,3},{3,4},{4,5},{5,6},{6,7},{7,8},{8,9},{9,10},{10,1... | collective-permute-start | bytes 3145736 | tf_op jit(solution)/shard_map/ppermute | solution.py:339
  102.2 1.0 copy-start.4
  103.2 1.4 copy-start.1
  207.2 22.1 %all-to-all-start.3 = ((bf16[8,2,152,256]{3,2,1,0:T(8,128)(2,1)}), bf16[8,2,152,256]{3,2,1,0:T(8,128)(2,1)S(1)}, u32[]{:S(2)}, u32[]{:S(2)}) async-start(bf16[8,2,152,256]{3,2,1,0:T(8,128)(2,1)} %get-tuple-element.32), calls=%async_computation.3 | async-start | bytes 2490368 | tf_op jit(solution)/shard_map/all_to_all | solution.py:281

commit v4 on v3

--- a/solution.py
+++ b/solution.py
@@ -15,6 +15,7 @@
 F32 = jnp.float32
 LANES = 128
 ROW = 8
+TALL = 64
 
 
 def phases(tokens, size):
@@ -25,7 +26,7 @@
 def split_host(table):
     high = table.astype(BF)
     low = (table - high.astype(np.float64)).astype(BF)
-    return jnp.asarray(high), jnp.asarray(low)
+    return jnp.asarray(np.concatenate([high, low], axis=1))
 
 
 def transforms(block, width):
@@ -44,14 +45,12 @@
     return forward, inverse
 
 
-def split_bf(x):
-    high = x.astype(BF)
-    low = (x - high.astype(F32)).astype(BF)
-    return high, low
-
-
 def dot(a, b):
     return jnp.dot(a, b, preferred_element_type=F32)
+
+
+def dot_twice(high_low, b):
+    return dot(high_low, jnp.concatenate([b, b], axis=0))
 
 
 def row_of(ref, index, col):
@@ -95,64 +94,20 @@
         ).astype(BF)
 
 
-def mixer(
-    block,
-    width,
-    cols,
-    q,
-    k,
-    v,
-    go,
-    back,
-    fore,
-    taps,
-    u_prev,
-    dz_next,
-    h_ref,
-    fx_hi,
-    fx_lo,
-    fo_hi,
-    fo_lo,
-    fa_hi,
-    fa_lo,
-    in_hi,
-    in_lo,
-    *rest,
-):
-    rest = rest[len(rest) - 26 :]
-    (
-    mixed,
-    g_q,
-    g_k,
-    g_v,
-    g_part,
-    sums,
-    x_q,
-    x_k,
-    x_v,
-    s_q,
-    s_k,
-    s_v,
-    g_pad,
-    h_pad,
-    h_flip,
-    z_pad,
-    window,
-    dz_own,
-    edge_u,
-    edge_z,
-    spec_u,
-    spec_h,
-    spec_d,
-    spec_w,
-    prod_hi,
-    prod_lo,
-    ) = rest
+def mixer(block, width, subs, q, k, v, go, back, fore, taps, u_prev, dz_next, h_ref, *rest):
     rows = block + ROW
     half = block
+    per = q.shape[2] // LANES // subs
+    group = per * LANES
+    t_window, t_own, t_ahead, t_inverse = rest[:4]
+    outs = rest[len(rest) - 24 :]
+    mixed, g_q, g_k, g_v, g_part, sums, x_q, x_k, x_v, s_q, s_k, s_v, g_pad = outs[:13]
+    h_pad, h_flip, z_pad, window, dz_own, edge_u, edge_z, spec_u, spec_h, spec_d, spec_w = outs[13:]
     rank = lax.broadcasted_iota(jnp.int32, (ROW, LANES), 0)
-    for col in range(cols):
+
+    def gather_rows(sub, col):
         lanes = pl.ds(col * LANES, LANES)
+        inside = pl.ds((col - sub * per) * LANES, LANES)
         for which, (src, dst) in enumerate(((q, x_q), (k, x_k), (v, x_v))):
             load_padded(
                 dst.at[col],
@@ -165,7 +120,7 @@
         q_s = causal(x_q.at[col], taps, 0, width, col, rows)
         s_q[col] = q_s
         dz = (go[0, :, lanes].astype(F32) * q_s[0:block]).astype(BF)
-        dz_own[:, lanes] = dz
+        dz_own[sub, :, inside] = dz
         z_pad[col, 0:ROW, :] = jnp.zeros((ROW, LANES), F32)
         z_pad[col, ROW : 2 * ROW, :] = dz[0:ROW].astype(F32)
         k_s = causal(x_k.at[col], taps, width, width, col, rows)
@@ -173,64 +128,53 @@
         v_s = causal(x_v.at[col], taps, 2 * width, width, col, rows)
         s_v[col] = v_s
         u = (k_s * v_s).astype(BF)
-        window[0:block, lanes] = u[0:block]
+        window[sub, 0:block, inside] = u[0:block]
         u_after = u[block:rows].astype(F32)
-        first = u_prev[0 : 2 * ROW, lanes]
-        u_before = first.astype(F32)[0:ROW]
+        first = u_prev[0 : 2 * ROW, lanes].astype(F32)
+        u_before = first[0:ROW]
         patched = jnp.where(rank < width - 1, u_after, u_before)
-        window[block : block + 2 * ROW, lanes] = jnp.concatenate(
-            [patched, first.astype(F32)[ROW : 2 * ROW]], axis=0
+        window[sub, block : block + 2 * ROW, inside] = jnp.concatenate(
+            [patched, first[ROW : 2 * ROW]], axis=0
         ).astype(BF)
-        window[block + 2 * ROW : 2 * block, lanes] = u_prev[2 * ROW : block, lanes]
+        window[sub, block + 2 * ROW : 2 * block, inside] = u_prev[2 * ROW : block, lanes]
         edge_u[col] = u_before + u_after
         edge_z[col] = dz_next[block : block + ROW, lanes].astype(F32) + dz[0:ROW].astype(F32)
-        taps_h = h_ref[0, :, lanes].astype(F32)
-        h_pad[col, 0 : 2 * ROW, :] = taps_h[block - 2 * ROW : block]
+        h_pad[col, 0 : 2 * ROW, :] = h_ref[0, sub, block - 2 * ROW : block, inside].astype(F32)
         h_pad[col, 2 * ROW : 3 * ROW, :] = jnp.zeros((ROW, LANES), F32)
         h_flip[col, 0:ROW, :] = jnp.zeros((ROW, LANES), F32)
-        for place in range(ROW):
+        for place in range(width - 2):
             h_flip[col, ROW + place : ROW + place + 1, :] = h_pad[
                 col, 2 * ROW - 1 - place : 2 * ROW - place, :
             ]
 
-    x = window[...]
-    spec_u[...] = dot(fx_hi[...], x) + dot(fx_lo[...], x)
-    h = h_ref[0]
-    spec_h[...] = dot(fo_hi[...], h) + dot(fo_lo[...], h)
-    d = dz_own[...]
-    spec_d[...] = dot(fo_hi[...], d) + dot(fo_lo[...], d)
-    a = dz_next[0:block, :]
-    spec_w[...] = spec_d[...] + (dot(fa_hi[...], a) + dot(fa_lo[...], a))
-
-    def inverse(slot, count):
-        high, low = prod_hi[slot], prod_lo[slot]
-        top, rest = in_hi[0:count, :], in_lo[0:count, :]
-        return dot(top, high) + (dot(rest, high) + dot(top, low))
-
-    def store(slot, cos_part, sin_part):
-        for place, part in ((0, cos_part), (half, sin_part)):
-            high, low = split_bf(part)
-            prod_hi[slot, place : place + half, :] = high
-            prod_lo[slot, place : place + half, :] = low
-
-    uc, us = spec_u[0:half, :], spec_u[half:, :]
-    hc, hs = spec_h[0:half, :], spec_h[half:, :]
-    store(0, uc * hc - us * hs, uc * hs + us * hc)
-    wc, ws = spec_w[0:half, :], spec_w[half:, :]
-    store(1, wc * hc + ws * hs, ws * hc - wc * hs)
-    dc, ds = spec_d[0:half, :], spec_d[half:, :]
-    store(2, dc * uc + ds * us, ds * uc - dc * us)
-
-    z_all = inverse(0, rows)
-    du_all = inverse(1, rows)
-    gm_all = inverse(2, block)
-
-    for col in range(cols):
+    def spectra(sub):
+        lanes = pl.ds(sub * group, group)
+        x = window[sub]
+        spec_u[sub] = dot_twice(t_window[...], x)
+        h = h_ref[0, sub]
+        spec_h[sub] = dot_twice(t_own[...], h)
+        d = dz_own[sub]
+        spec_d[sub] = dot_twice(t_own[...], d)
+        a = dz_next[0:block, lanes]
+        spec_w[sub] = spec_d[sub] + dot_twice(t_ahead[...], a)
+
+    def inverse(cos_part, sin_part, count):
+        high = jnp.concatenate([cos_part.astype(BF), sin_part.astype(BF)], axis=0)
+        return dot_twice(t_inverse[0:count, :], high)
+
+    def times(sub, lanes):
+        uc, us = spec_u[sub, 0:half, lanes], spec_u[sub, half:, lanes]
+        hc, hs = spec_h[sub, 0:half, lanes], spec_h[sub, half:, lanes]
+        z = inverse(uc * hc - us * hs, uc * hs + us * hc, rows)
+        wc, ws = spec_w[sub, 0:half, lanes], spec_w[sub, half:, lanes]
+        du = inverse(wc * hc + ws * hs, ws * hc - wc * hs, rows)
+        dc, ds = spec_d[sub, 0:half, lanes], spec_d[sub, half:, lanes]
+        gm = inverse(dc * uc + ds * us, ds * uc - dc * us, block)
+        return z, du, gm
+
+    def finish(sub, col, z, du, gm):
         lanes = pl.ds(col * LANES, LANES)
-        lo, hi = col * LANES, (col + 1) * LANES
-        z = z_all[:, lo:hi]
-        du = du_all[:, lo:hi]
-        gm = gm_all[:, lo:hi]
+        inside = pl.ds((col - sub * per) * LANES, LANES)
         z_fix = jnp.zeros((ROW, LANES), F32)
         g_fix = jnp.zeros((ROW, LANES), F32)
         for place in range(1, width - 1):
@@ -244,23 +188,41 @@
         z = jnp.concatenate([z[0:ROW] + z_fix, z[ROW:]], axis=0)
         du = jnp.concatenate([du[0:block], du[block:] + du_fix], axis=0)
         gm = jnp.concatenate([gm[0 : block - ROW], gm[block - ROW : block] + g_fix], axis=0)
-        g_part[0, 0, 0:block, lanes] = gm.astype(BF)
+        g_part[0, sub, 0:block, inside] = gm.astype(BF)
         mixed[0, :, lanes] = (s_q[col, 0:block, :] * z[0:block]).astype(BF)
-        g_pad[0, 0:block, :] = go[0, :, lanes].astype(F32) * z[0:block]
-        g_pad[0, block:rows, :] = fore[3, :, lanes].astype(F32) * z[block:rows]
-        g_pad[1] = du * s_v[col]
-        g_pad[2] = du * s_k[col]
+        g_pad[col, 0, 0:block, :] = go[0, :, lanes].astype(F32) * z[0:block]
+        g_pad[col, 0, block:rows, :] = fore[3, :, lanes].astype(F32) * z[block:rows]
+        g_pad[col, 1] = du * s_v[col]
+        g_pad[col, 2] = du * s_k[col]
         for which, (src, out) in enumerate(((x_q, g_q), (x_k, g_k), (x_v, g_v))):
-            values = src[col, ROW : ROW + block, :]
-            total = None
-            for offset in range(width):
-                moved = g_pad[which, pl.ds(offset, block), :]
-                term = row_of(taps, which * width + offset, col) * moved
-                total = term if total is None else total + term
-                place = which * width + offset
-                sums[place : place + 1, :] = jnp.sum(values * moved, axis=0, keepdims=True)
-            out[0, :, lanes] = total.astype(BF)
-        g_part[0, 0, block : block + 3 * ROW, lanes] = sums[...].astype(BF)
+            for start in range(0, block, TALL):
+                values = src[col, ROW + start : ROW + start + TALL, :]
+                total = None
+                for offset in range(width):
+                    moved = g_pad[col, which, pl.ds(start + offset, TALL), :]
+                    term = row_of(taps, which * width + offset, col) * moved
+                    total = term if total is None else total + term
+                    weight = values * moved
+                    held = weight[0:ROW]
+                    for r in range(ROW, TALL, ROW):
+                        held = held + weight[r : r + ROW]
+                    place = which * width + offset
+                    if start == 0:
+                        sums[col, place] = held
+                    else:
+                        sums[col, place] = sums[col, place] + held
+                out[0, start : start + TALL, lanes] = total.astype(BF)
+        g_part[0, sub, block : block + 3 * ROW, inside] = jnp.sum(sums[col], axis=1).astype(BF)
+
+    for sub in range(subs):
+        for col in range(sub * per, (sub + 1) * per):
+            gather_rows(sub, col)
+        spectra(sub)
+    for sub in range(subs):
+        found = times(sub, pl.ds(0, group))
+        for col in range(sub * per, (sub + 1) * per):
+            lo = (col - sub * per) * LANES
+            finish(sub, col, *(x[:, lo : lo + LANES] for x in found))
 
 
 def halo_pairs(count):
@@ -295,12 +257,9 @@
     parts = PARTS
     coarse = n_context // parts
     ahead, behind = halo_pairs(n_context)
-    _, outer, both = groups_of(n_context, n_dp, parts)
+    inner, outer, both = groups_of(n_context, n_dp, parts)
     forward, inverse = transforms(block, width)
-    tables = [part for pair in forward + [inverse] for part in pair]
-
-    mine = spread(med_filter.astype(BF).T, parts * n_dp, ("context", "dp"), both)
-    mine = mine.reshape(parts, block, group)
+    tables = forward + [inverse]
 
     back = jnp.concatenate([x[:, block - ROW :] for x in (query_in, key_in, value_in)], axis=0)
     fore = jnp.concatenate([x[:, :ROW] for x in (query_in, key_in, value_in, grad_out)], axis=0)
@@ -310,6 +269,8 @@
     short = short_filter.transpose(0, 2, 1).reshape(3 * width, group)
     short = jnp.pad(short, ((0, held_short - 3 * width), (0, 0)))
     taps = spread(short, n_context, "context")
+    mine = lax.all_gather(med_filter.astype(BF).T, "dp", axis=0, tiled=True)
+    mine = spread(mine, parts, "context", inner)
     h_all = spread(mine, coarse, "context", outer)
 
     whole = lambda x: pl.BlockSpec(x.shape, lambda *_: (0,) * x.ndim)
@@ -342,59 +303,56 @@
 
     outs = None
     partials = []
-    cols = group // LANES
-    padded = pltpu.VMEM((cols, block + 2 * ROW, LANES), F32)
-    shifted = pltpu.VMEM((cols, rows, LANES), F32)
     for index, (first, count) in enumerate(CHUNKS):
-        at = lambda i, j, first=first: parts * i + first + j
-        tokens = pl.BlockSpec((1, block, group), lambda i, j, at=at: (0, 0, at(i, j)))
-        stack = lambda height, at=at: pl.BlockSpec(
-            (height, ROW, group), lambda i, j: (0, 0, at(i, j))
-        )
-        filters = pl.BlockSpec((1, held_short, group), lambda i, j, at=at: (at(i, j), 0, 0))
-        packed = lambda height, count=count: pl.BlockSpec(
-            (height, group), lambda i, j: (0, count * i + j)
-        )
-        taps_h = pl.BlockSpec(
-            (1, None, block, group), lambda i, j, first=first: (i, first + j, 0, 0)
-        )
+        wide = count * group
+        per = parts // count
+        place = first // count
+        cols = wide // LANES
+        at = lambda i, per=per, place=place: per * i + place
+        tokens = pl.BlockSpec((1, block, wide), lambda i, at=at: (0, 0, at(i)))
+        stack = lambda height, at=at: pl.BlockSpec((height, ROW, wide), lambda i: (0, 0, at(i)))
+        filters = pl.BlockSpec((count, held_short, group), lambda i, at=at: (at(i), 0, 0))
+        packed = lambda height: pl.BlockSpec((height, wide), lambda i: (0, i))
+        taps_h = pl.BlockSpec((1, count, block, group), lambda i, place=place: (i, place, 0, 0))
+        padded = pltpu.VMEM((cols, block + 2 * ROW, LANES), F32)
+        shifted = pltpu.VMEM((cols, rows, LANES), F32)
+        strip = lambda height: pltpu.VMEM((cols, height * ROW, LANES), F32)
+        spectrum = pltpu.VMEM((count, size, group), F32)
         u_prev, dz_next = pieces[index]
         carried = [] if outs is None else list(outs)
         fixed = [query_in, key_in, value_in, grad_out, back, fore, taps, u_prev, dz_next]
         fixed += [h_all, *tables]
         *outs, partial = pl.pallas_call(
-            functools.partial(mixer, block, width, cols),
-            grid=(coarse, count),
+            functools.partial(mixer, block, width, count),
+            grid=(coarse,),
             in_specs=[tokens] * 4
             + [stack(3), stack(4), filters, packed(block), packed(rows), taps_h]
             + [whole(x) for x in tables]
             + [pl.BlockSpec(memory_space=pl.ANY)] * len(carried),
             out_specs=[tokens] * 4
-            + [pl.BlockSpec((1, 1, block + held_short, group), lambda i, j: (i, j, 0, 0))],
+            + [pl.BlockSpec((1, count, block + held_short, group), lambda i: (i, 0, 0, 0))],
             out_shape=[jax.ShapeDtypeStruct(query_in.shape, BF)] * 4
             + [jax.ShapeDtypeStruct((coarse, count, block + held_short, group), BF)],
             scratch_shapes=[
-                pltpu.VMEM((held_short, LANES), F32),
+                pltpu.VMEM((cols, held_short, ROW, LANES), F32),
                 padded,
                 padded,
                 padded,
                 shifted,
                 shifted,
                 shifted,
-                pltpu.VMEM((3, rows, LANES), F32),
-                pltpu.VMEM((cols, 3 * ROW, LANES), F32),
-                pltpu.VMEM((cols, 2 * ROW, LANES), F32),
-                pltpu.VMEM((cols, 2 * ROW, LANES), F32),
-                pltpu.VMEM((size, group), BF),
-                pltpu.VMEM((block, group), BF),
-                pltpu.VMEM((cols, ROW, LANES), F32),
-                pltpu.VMEM((cols, ROW, LANES), F32),
-                pltpu.VMEM((size, group), F32),
-                pltpu.VMEM((size, group), F32),
-                pltpu.VMEM((size, group), F32),
-                pltpu.VMEM((size, group), F32),
-                pltpu.VMEM((3, size, group), BF),
-                pltpu.VMEM((3, size, group), BF),
+                pltpu.VMEM((cols, 3, rows, LANES), F32),
+                strip(3),
+                strip(2),
+                strip(2),
+                pltpu.VMEM((count, size, group), BF),
+                pltpu.VMEM((count, block, group), BF),
+                strip(1),
+                strip(1),
+                spectrum,
+                spectrum,
+                spectrum,
+                spectrum,
             ],
             input_output_aliases={len(fixed) + k: k for k in range(len(carried))},
         )(*fixed, *carried)

time: 245 us -> 236 us (0.963)
  Pallas kernels: 67 us -> 55 us
  blocking collectives: 64.4 us -> 72.3 us
  waiting for transfers between devices: 57.1 us -> 53.8 us
    pallas_call x2, Pallas kernels: 51.4 us -> 39.4 us  [per_device(): pl.pallas_call(functools.partial(mixer, block, width, count), grid=(coars...]
    all_gather x0 -> x1, blocking collectives: none -> 6.44 us  [per_device(): mine = lax.all_gather(med_filter.astype(BF).T, 'dp', axis=0, tiled=True)]
    all_to_all x4, waiting for transfers between devices: 34 us -> 30.8 us  [exchange(): return lax.all_to_all(x, axes, 0, 0, axis_index_groups=groups)]
    all_to_all x4, starting transfers between devices: 23 us -> 20.1 us  [exchange(): return lax.all_to_all(x, axes, 0, 0, axis_index_groups=groups)]
  transfers between devices with their start and end apart: 10 -> 10, of which waited for: 5 -> 6; matrix products, arithmetic and copies ran while one was open for 3% -> 3% of each run, Pallas kernels for 17% -> 15%
where the time goes in v4:
time: 236 us; the launch traced here: 235 us
  blocking collectives  72.3 us (31%)
  Pallas kernels  55 us (23%)
  waiting for transfers between devices  53.8 us (23%)
  starting transfers between devices  37.6 us (16%)
  local copies, waits for them, and re-layouts  11.9 us (5%)
  other arithmetic  3.15 us (1%)
    all_to_all x2, blocking collectives, exchange(): return lax.all_to_all(x, axes, 0, 0, axis_index_groups=groups)  65.8 us
    pallas_call x2, Pallas kernels, per_device(): pl.pallas_call(functools.partial(mixer, block, width, count), grid=(coars...  39.4 us
    all_to_all x4, waiting for transfers between devices, exchange(): return lax.all_to_all(x, axes, 0, 0, axis_index_groups=groups)  30.8 us
    all_to_all x4, starting transfers between devices, exchange(): return lax.all_to_all(x, axes, 0, 0, axis_index_groups=groups)  20.1 us
    ppermute x2, waiting for transfers between devices, per_device(): u_prev = lax.ppermute(u, 'context', ahead)  16.3 us
    pallas_call x2, Pallas kernels, per_device(): pl.pallas_call(functools.partial(make_products, block, width, cols), grid...  15.6 us
    ppermute x2, starting transfers between devices, per_device(): u_prev = lax.ppermute(u, 'context', ahead)  9.7 us
    ppermute x1, waiting for transfers between devices, per_device(): back = lax.ppermute(back, 'context', ahead)  6.71 us
  transfers between devices with their start and end apart: 10, of which 6 were waited for; matrix products, arithmetic and copies ran while one was open for 3% of the time, Pallas kernels for 15%

profile of v4, /device:TPU:1, one launch (start us, length us, event | category | flops | bytes accessed | tf_op | source)
XLA Modules:
  0.0 234.5 jit_solution(6193311425040402780)
XLA Ops:
  0.6 0.8 convert_bitcast_fusion
  1.4 6.4 %all_gather.3 = bf16[128,256]{1,0:T(8,128)(2,1)S(1)} all-gather(bf16[32,256]{1,0:T(8,128)(2,1)S(1)} %convert_bitcast_fusion), channel_id=1, replica_groups=mesh['dp'=4,'context'=32] {'dp'}, dimensions={0}, use_global_device_ids=true | all-gather | bytes 81920 | tf_op jit(solution)/shard_map/all_gather | solution.py:272
  8.6 5.1 %all-to-all-start.1 = ((bf16[4,128,256]{2,1,0:T(8,128)(2,1)}), bf16[4,128,256]{2,1,0:T(8,128)(2,1)S(1)}, u32[]{:S(2)}, u32[]{:S(2)}) async-start(bf16[4,128,256]{2,1,0:T(8,128)(2,1)} %broadcast_in_dim.16), calls=%async_computation.1 | async-start | bytes 524288 | tf_op jit(solution)/shard_map/all_to_all | solution.py:243
  13.7 1.9 fusion.1
  15.6 1.6 fusion.3
  17.2 2.5 %all-to-all-done.1 = bf16[4,128,256]{2,1,0:T(8,128)(2,1)S(1)} async-done(((bf16[4,128,256]{2,1,0:T(8,128)(2,1)}), bf16[4,128,256]{2,1,0:T(8,128)(2,1)S(1)}, u32[]{:S(2)}, u32[]{:S(2)}) %all-to-all-start.1) | async-done | bytes 262176 | tf_op jit(solution)/shard_map/all_to_all | solution.py:243
  19.7 0.9 broadcast_in_dim.15
  20.7 7.6 %all-to-all-start = ((f32[32,24,256]{2,1,0:T(8,128)}), f32[32,24,256]{2,1,0:T(8,128)S(1)}, u32[]{:S(2)}, u32[]{:S(2)}) async-start(f32[32,24,256]{2,1,0:T(8,128)} %broadcast_in_dim.15), calls=%async_computation | async-start | bytes 1572864 | tf_op jit(solution)/shard_map/all_to_all | solution.py:243
  28.3 0.9 pad_maximum_fusion
  29.2 1.3 collective-permute-start.1
  30.5 11.3 %all-to-all-done.taps = f32[32,24,256]{2,1,0:T(8,128)S(1)} async-done(((f32[32,24,256]{2,1,0:T(8,128)}), f32[32,24,256]{2,1,0:T(8,128)S(1)}, u32[]{:S(2)}, u32[]{:S(2)}) %all-to-all-start) | async-done | bytes 786464 | tf_op jit(solution)/shard_map/all_to_all | solution.py:243
  41.7 1.6 broadcast_in_dim.17
  43.3 3.7 %all-to-all-start.2 = ((bf16[8,4,128,256]{3,2,1,0:T(8,128)(2,1)}), bf16[8,4,128,256]{3,2,1,0:T(8,128)(2,1)S(1)}, u32[]{:S(2)}, u32[]{:S(2)}) async-start(bf16[8,4,128,256]{3,2,1,0:T(8,128)(2,1)} %broadcast_in_dim.17), calls=%async_computation.2 | async-start | bytes 4194304 | tf_op jit(solution)/shard_map/all_to_all | solution.py:243
  47.1 1.0 pad_maximum_fusion.2
  48.1 4.0 %collective-permute-start = (bf16[3,8,8192]{2,1,0:T(8,128)(2,1)S(1)}, bf16[3,8,8192]{2,1,0:T(8,128)(2,1)S(1)}, u32[]{:S(2)}, u32[]{:S(2)}) collective-permute-start(bf16[3,8,8192]{2,1,0:T(8,128)(2,1)S(1)} %pad_maximum_fusion.2), channel_id=1, source_target_pairs={{0,1},{1,2},{2,3},{3,4},{4,5},{5,6},{6,7},{7,8},{8,9},{9,10},{10,1... | collective-permute-start | bytes 1179656 | tf_op jit(solution)/shard_map/ppermute | solution.py:266
  52.1 6.7 %collective-permute-done.back = bf16[3,8,8192]{2,1,0:T(8,128)(2,1)S(1)} collective-permute-done((bf16[3,8,8192]{2,1,0:T(8,128)(2,1)S(1)}, bf16[3,8,8192]{2,1,0:T(8,128)(2,1)S(1)}, u32[]{:S(2)}, u32[]{:S(2)}) %collective-permute-start) | collective-permute-done | bytes 393248 | tf_op jit(solution)/shard_map/ppermute | solution.py:266
  59.5 0.8 copy-done.2
  60.3 7.7 %shard_map.146 = (bf16[128,4096]{1,0:T(8,128)(2,1)}, bf16[136,4096]{1,0:T(8,128)(2,1)}) custom-call(bf16[1,128,8192]{2,1,0:T(8,128)(2,1)} %q.7, bf16[1,128,8192]{2,1,0:T(8,128)(2,1)} %k.7, bf16[1,128,8192]{2,1,0:T(8,128)(2,1)} %v.7, bf16[1,128,8192]{2,1,0:T(8,128)(2,1)} %go.7, bf16[3,8,8192]{2,1,0:T(8,128)(2,1)} %copy-done.3, bf16[4,8,8192]{2,1,0:T(8,128)(2,1)} %copy-done.2, ...), custom_call_target="tpu_custom_call" | custom-call | tf_op jit(solution)/shard_map/pallas_call | solution.py:289
  68.0 1.3 collective-permute-start.5
  69.3 7.9 %shard_map.145 = (bf16[128,4096]{1,0:T(8,128)(2,1)}, bf16[136,4096]{1,0:T(8,128)(2,1)}) custom-call(bf16[1,128,8192]{2,1,0:T(8,128)(2,1)} %q.7, bf16[1,128,8192]{2,1,0:T(8,128)(2,1)} %k.7, bf16[1,128,8192]{2,1,0:T(8,128)(2,1)} %v.7, bf16[1,128,8192]{2,1,0:T(8,128)(2,1)} %go.7, bf16[3,8,8192]{2,1,0:T(8,128)(2,1)} %copy-done.3, bf16[4,8,8192]{2,1,0:T(8,128)(2,1)} %copy-done.2, ...), custom_call_target="tpu_custom_call" | custom-call | tf_op jit(solution)/shard_map/pallas_call | solution.py:289
  77.2 1.3 collective-permute-start.3
  78.5 5.4 %collective-permute-start.4 = (bf16[128,4096]{1,0:T(8,128)(2,1)}, bf16[128,4096]{1,0:T(8,128)(2,1)S(1)}, u32[]{:S(2)}, u32[]{:S(2)}) collective-permute-start(bf16[128,4096]{1,0:T(8,128)(2,1)} %get-tuple-element.22), channel_id=1, source_target_pairs={{0,1},{1,2},{2,3},{3,4},{4,5},{5,6},{6,7},{7,8},{8,9},{9,10},{10,1... | collective-permute-start | bytes 3145736 | tf_op jit(solution)/shard_map/ppermute | solution.py:300
  83.9 4.3 %collective-permute-start.2 = (bf16[128,4096]{1,0:T(8,128)(2,1)}, bf16[128,4096]{1,0:T(8,128)(2,1)}, u32[]{:S(2)}, u32[]{:S(2)}) collective-permute-start(bf16[128,4096]{1,0:T(8,128)(2,1)} %get-tuple-element.20), channel_id=1, source_target_pairs={{0,1},{1,2},{2,3},{3,4},{4,5},{5,6},{6,7},{7,8},{8,9},{9,10},{10,1... | collective-permute-start | bytes 3145736 | tf_op jit(solution)/shard_map/ppermute | solution.py:300
  88.2 15.9 %collective-permute-done.4.u_prev = bf16[128,4096]{1,0:T(8,128)(2,1)S(1)} collective-permute-done((bf16[128,4096]{1,0:T(8,128)(2,1)}, bf16[128,4096]{1,0:T(8,128)(2,1)S(1)}, u32[]{:S(2)}, u32[]{:S(2)}) %collective-permute-start.4) | collective-permute-done | bytes 1048608 | tf_op jit(solution)/shard_map/ppermute | solution.py:300
  104.1 1.0 copy-done.4
  105.1 1.4 copy-done.1
  106.5 19.7 %shard_map.147 = (bf16[1,128,8192]{2,1,0:T(8,128)(2,1)}, bf16[1,128,8192]{2,1,0:T(8,128)(2,1)}, bf16[1,128,8192]{2,1,0:T(8,128)(2,1)}, bf16[1,128,8192]{2,1,0:T(8,128)(2,1)}, bf16[8,2,152,256]{3,2,1,0:T(8,128)(2,1)}) custom-call(bf16[1,128,8192]{2,1,0:T(8,128)(2,1)} %q.7, bf16[1,128,8192]{2,1,0:T(8,128)(2,1)} %k.7, bf16[1,128,8192]{2,1,0:T(8,128)(2,1)} %v.7, ...), custom_call_target="tpu_custom_call" | custom-call | tf_op jit(solution)/shard_map/pallas_call | solution.py:325
  126.6 19.7 %shard_map.148 = (bf16[1,128,8192]{2,1,0:T(8,128)(2,1)}, bf16[1,128,8192]{2,1,0:T(8,128)(2,1)}, bf16[1,128,8192]{2,1,0:T(8,128)(2,1)}, bf16[1,128,8192]{2,1,0:T(8,128)(2,1)}, bf16[8,2,152,256]{3,2,1,0:T(8,128)(2,1)}) custom-call(bf16[1,128,8192]{2,1,0:T(8,128)(2,1)} %q.7, ...), custom_call_target="tpu_custom_call", output_to_operand_aliasing={{0}: (14, {}), {1}: (15, {}), {2}: (16, {}), {3}: (17, {})} | custom-call | tf_op jit(solution)/shard_map/pallas_call | solution.py:325
  146.3 37.1 %all_to_all.30 = bf16[8,2,152,256]{3,2,1,0:T(8,128)(2,1)S(1)} all-to-all(bf16[8,2,152,256]{3,2,1,0:T(8,128)(2,1)} %get-tuple-element.33), channel_id=1, replica_groups={{0,4,8,12,16,20,24,28},{1,5,9,13,17,21,25,29},{2,6,10,14,18,22,26,30},{..., dimensions={0} | all-to-all | bytes 2490368 | tf_op jit(solution)/shard_map/all_to_all | solution.py:243
  183.4 3.6 %all-to-all-start.3 = ((bf16[8,2,152,256]{3,2,1,0:T(8,128)(2,1)}), bf16[8,2,152,256]{3,2,1,0:T(8,128)(2,1)S(1)}, u32[]{:S(2)}, u32[]{:S(2)}) async-start(bf16[8,2,152,256]{3,2,1,0:T(8,128)(2,1)} %get-tuple-element.32), calls=%async_computation.3 | async-start | bytes 2490368 | tf_op jit(solution)/shard_map/all_to_all | solution.py:243
  187.2 17.0 %all-to-all-done.3 = bf16[8,2,152,256]{3,2,1,0:T(8,128)(2,1)S(1)} async-done(((bf16[8,2,152,256]{3,2,1,0:T(8,128)(2,1)}), bf16[8,2,152,256]{3,2,1,0:T(8,128)(2,1)S(1)}, u32[]{:S(2)}, u32[]{:S(2)}) %all-to-all-start.3) | async-done | bytes 1245216 | tf_op jit(solution)/shard_map/all_to_all | solution.py:243
  204.5 28.7 %all_to_all.31 = bf16[16,56,256]{2,1,0:T(8,128)(2,1)S(1)} all-to-all(bf16[16,56,256]{2,1,0:T(8,128)(2,1)S(1)} %pad_maximum_fusion.1), channel_id=1, replica_groups={{0,32,64,96,1,33,65,97,2,34,66,98,3,35,67,99},{4,36,68,100,5,37,69,101,..., dimensions={0} | all-to-all | bytes 917504 | tf_op jit(solution)/shard_map/all_to_all | solution.py:243
  (31 shorter events, 3.7 us)
Async XLA Ops:
  0.6 16.6 %copy-start.6 = (f32[3,256,7]{1,2,0:T(8,128)S(1)}, f32[3,256,7]{1,2,0:T(8,128)}, u32[]{:S(2)}) copy-start(f32[3,256,7]{1,2,0:T(8,128)} %param.15) | copy-start | bytes 64516
  8.6 11.2 %all-to-all-start.1 = ((bf16[4,128,256]{2,1,0:T(8,128)(2,1)}), bf16[4,128,256]{2,1,0:T(8,128)(2,1)S(1)}, u32[]{:S(2)}, u32[]{:S(2)}) async-start(bf16[4,128,256]{2,1,0:T(8,128)(2,1)} %broadcast_in_dim.16), calls=%async_computation.1 | async-start | bytes 524288 | tf_op jit(solution)/shard_map/all_to_all | solution.py:243
  13.7 14.6 %slice-start = ((bf16[1,128,8192]{2,1,0:T(8,128)(2,1)}), bf16[1,8,8192]{2,1,0:T(8,128)(2,1)S(1)}, s32[]{:S(2)}) async-start(bf16[1,128,8192]{2,1,0:T(8,128)(2,1)} %go.7), calls=%async_computation.6 | async-start | bytes 262144 | tf_op jit(solution)/shard_map/slice | solution.py:265
  20.7 21.1 %all-to-all-start = ((f32[32,24,256]{2,1,0:T(8,128)}), f32[32,24,256]{2,1,0:T(8,128)S(1)}, u32[]{:S(2)}, u32[]{:S(2)}) async-start(f32[32,24,256]{2,1,0:T(8,128)} %broadcast_in_dim.15), calls=%async_computation | async-start | bytes 1572864 | tf_op jit(solution)/shard_map/all_to_all | solution.py:243
  29.2 29.6 %collective-permute-start.1 = (bf16[4,8,8192]{2,1,0:T(8,128)(2,1)}, bf16[4,8,8192]{2,1,0:T(8,128)(2,1)S(1)}, u32[]{:S(2)}, u32[]{:S(2)}) collective-permute-start(bf16[4,8,8192]{2,1,0:T(8,128)(2,1)} %pad_maximum_fusion), channel_id=1, source_target_pairs={{1,0},{2,1},{3,2},{4,3},{5,4},{6,5},{7,6},{8,7},{9,8},{10,9},{11,1... | collective-permute-start | bytes 1572872 | tf_op jit(solution)/shard_map/ppermute | solution.py:267
  41.7 1.6 copy-start
  43.3 3.8 %copy-start.5 = (bf16[1,8,8192]{2,1,0:T(8,128)(2,1)S(1)}, bf16[1,8,8192]{2,1,0:T(8,128)(2,1)}, u32[]{:S(2)}) copy-start(bf16[1,8,8192]{2,1,0:T(8,128)(2,1)} %get-tuple-element.39) | copy-start | bytes 393220
  43.3 61.8 %all-to-all-start.2 = ((bf16[8,4,128,256]{3,2,1,0:T(8,128)(2,1)}), bf16[8,4,128,256]{3,2,1,0:T(8,128)(2,1)S(1)}, u32[]{:S(2)}, u32[]{:S(2)}) async-start(bf16[8,4,128,256]{3,2,1,0:T(8,128)(2,1)} %broadcast_in_dim.17), calls=%async_computation.2 | async-start | bytes 4194304 | tf_op jit(solution)/shard_map/all_to_all | solution.py:243
  48.1 10.7 %collective-permute-start = (bf16[3,8,8192]{2,1,0:T(8,128)(2,1)S(1)}, bf16[3,8,8192]{2,1,0:T(8,128)(2,1)S(1)}, u32[]{:S(2)}, u32[]{:S(2)}) collective-permute-start(bf16[3,8,8192]{2,1,0:T(8,128)(2,1)S(1)} %pad_maximum_fusion.2), channel_id=1, source_target_pairs={{0,1},{1,2},{2,3},{3,4},{4,5},{5,6},{6,7},{7,8},{8,9},{9,10},{10,1... | collective-permute-start | bytes 1179656 | tf_op jit(solution)/shard_map/ppermute | solution.py:266
  58.8 0.7 copy-start.3
  59.5 0.8 copy-start.2
  68.0 37.0 %collective-permute-start.5 = (bf16[136,4096]{1,0:T(8,128)(2,1)}, bf16[136,4096]{1,0:T(8,128)(2,1)}, u32[]{:S(2)}, u32[]{:S(2)}) collective-permute-start(bf16[136,4096]{1,0:T(8,128)(2,1)} %get-tuple-element.23), channel_id=1, source_target_pairs={{1,0},{2,1},{3,2},{4,3},{5,4},{6,5},{7,6},{8,7},{9,8},{10,9},{11,1... | collective-permute-start | bytes 3342344 | tf_op jit(solution)/shard_map/ppermute | solution.py:301
  77.2 49.4 %collective-permute-start.3 = (bf16[136,4096]{1,0:T(8,128)(2,1)}, bf16[136,4096]{1,0:T(8,128)(2,1)}, u32[]{:S(2)}, u32[]{:S(2)}) collective-permute-start(bf16[136,4096]{1,0:T(8,128)(2,1)} %get-tuple-element.21), channel_id=1, source_target_pairs={{1,0},{2,1},{3,2},{4,3},{5,4},{6,5},{7,6},{8,7},{9,8},{10,9},{11,1... | collective-permute-start | bytes 3342344 | tf_op jit(solution)/shard_map/ppermute | solution.py:301
  78.5 25.6 %collective-permute-start.4 = (bf16[128,4096]{1,0:T(8,128)(2,1)}, bf16[128,4096]{1,0:T(8,128)(2,1)S(1)}, u32[]{:S(2)}, u32[]{:S(2)}) collective-permute-start(bf16[128,4096]{1,0:T(8,128)(2,1)} %get-tuple-element.22), channel_id=1, source_target_pairs={{0,1},{1,2},{2,3},{3,4},{4,5},{5,6},{6,7},{7,8},{8,9},{9,10},{10,1... | collective-permute-start | bytes 3145736 | tf_op jit(solution)/shard_map/ppermute | solution.py:300
  83.9 42.6 %collective-permute-start.2 = (bf16[128,4096]{1,0:T(8,128)(2,1)}, bf16[128,4096]{1,0:T(8,128)(2,1)}, u32[]{:S(2)}, u32[]{:S(2)}) collective-permute-start(bf16[128,4096]{1,0:T(8,128)(2,1)} %get-tuple-element.20), channel_id=1, source_target_pairs={{0,1},{1,2},{2,3},{3,4},{4,5},{5,6},{6,7},{7,8},{8,9},{9,10},{10,1... | collective-permute-start | bytes 3145736 | tf_op jit(solution)/shard_map/ppermute | solution.py:300
  104.1 1.0 copy-start.4
  105.1 1.4 copy-start.1
  183.4 20.8 %all-to-all-start.3 = ((bf16[8,2,152,256]{3,2,1,0:T(8,128)(2,1)}), bf16[8,2,152,256]{3,2,1,0:T(8,128)(2,1)S(1)}, u32[]{:S(2)}, u32[]{:S(2)}) async-start(bf16[8,2,152,256]{3,2,1,0:T(8,128)(2,1)} %get-tuple-element.32), calls=%async_computation.3 | async-start | bytes 2490368 | tf_op jit(solution)/shard_map/all_to_all | solution.py:243

commit v5 on v4

--- a/solution.py
+++ b/solution.py
@@ -257,7 +257,7 @@
     parts = PARTS
     coarse = n_context // parts
     ahead, behind = halo_pairs(n_context)
-    inner, outer, both = groups_of(n_context, n_dp, parts)
+    _, outer, both = groups_of(n_context, n_dp, parts)
     forward, inverse = transforms(block, width)
     tables = forward + [inverse]
 
@@ -269,8 +269,9 @@
     short = short_filter.transpose(0, 2, 1).reshape(3 * width, group)
     short = jnp.pad(short, ((0, held_short - 3 * width), (0, 0)))
     taps = spread(short, n_context, "context")
-    mine = lax.all_gather(med_filter.astype(BF).T, "dp", axis=0, tiled=True)
-    mine = spread(mine, parts, "context", inner)
+    mine = lax.all_gather(
+        med_filter.astype(BF).T, ("context", "dp"), axis_index_groups=both
+    ).reshape(parts, block, group)
     h_all = spread(mine, coarse, "context", outer)
 
     whole = lambda x: pl.BlockSpec(x.shape, lambda *_: (0,) * x.ndim)

time: 236 us -> 248 us (1.051)
  blocking collectives: 72.3 us -> 85.6 us
  starting transfers between devices: 37.6 us -> 46 us
  waiting for transfers between devices: 53.8 us -> 46.4 us
    all_gather x1, blocking collectives: 6.44 us -> 23.1 us  [per_device(): lax.all_gather(med_filter.astype(BF).T, ('context', 'dp'), axis_index_gro...]
    all_to_all x4 -> x3, waiting for transfers between devices: 30.8 us -> 19.2 us  [exchange(): return lax.all_to_all(x, axes, 0, 0, axis_index_groups=groups)]
    all_to_all x4 -> x3, starting transfers between devices: 20.1 us -> 31.1 us  [exchange(): return lax.all_to_all(x, axes, 0, 0, axis_index_groups=groups)]
    all_to_all x2, blocking collectives: 65.8 us -> 62.5 us  [exchange(): return lax.all_to_all(x, axes, 0, 0, axis_index_groups=groups)]
    ppermute x1, starting transfers between devices: 3.97 us -> 1.31 us  [per_device(): back = lax.ppermute(back, 'context', ahead)]
    ppermute x2, waiting for transfers between devices: 16.3 us -> 18.9 us  [per_device(): u_prev = lax.ppermute(u, 'context', ahead)]
  transfers between devices with their start and end apart: 10 -> 9, of which waited for: 6 -> 4; matrix products, arithmetic and copies ran while one was open for 3% -> 3% of each run, Pallas kernels for 15% -> 14%
where the time goes in v5:
time: 248 us; the launch traced here: 247 us
  blocking collectives  85.6 us (35%)
  Pallas kernels  55 us (22%)
  waiting for transfers between devices  46.4 us (19%)
  starting transfers between devices  46 us (19%)
  local copies, waits for them, and re-layouts  10.8 us (4%)
    all_to_all x2, blocking collectives, exchange(): return lax.all_to_all(x, axes, 0, 0, axis_index_groups=groups)  62.5 us
    pallas_call x2, Pallas kernels, per_device(): pl.pallas_call(functools.partial(mixer, block, width, count), grid=(coars...  39.4 us
    all_to_all x3, starting transfers between devices, exchange(): return lax.all_to_all(x, axes, 0, 0, axis_index_groups=groups)  31.1 us
    all_gather x1, blocking collectives, per_device(): lax.all_gather(med_filter.astype(BF).T, ('context', 'dp'), axis_index_gro...  23.1 us
    all_to_all x3, waiting for transfers between devices, exchange(): return lax.all_to_all(x, axes, 0, 0, axis_index_groups=groups)  19.2 us
    ppermute x2, waiting for transfers between devices, per_device(): u_prev = lax.ppermute(u, 'context', ahead)  18.9 us
    pallas_call x2, Pallas kernels, per_device(): pl.pallas_call(functools.partial(make_products, block, width, cols), grid...  15.6 us
    ppermute x2, starting transfers between devices, per_device(): u_prev = lax.ppermute(u, 'context', ahead)  9.73 us
  transfers between devices with their start and end apart: 9, of which 4 were waited for; matrix products, arithmetic and copies ran while one was open for 3% of the time, Pallas kernels for 14%

profile of v5, /device:TPU:1, one launch (start us, length us, event | category | flops | bytes accessed | tf_op | source)
XLA Modules:
  0.0 247.0 jit_solution(375346975882981756)
XLA Ops:
  0.6 0.7 reshape.27
  1.4 0.9 broadcast_in_dim.12
  2.3 11.5 %all-to-all-start = ((f32[32,24,256]{2,1,0:T(8,128)}), f32[32,24,256]{2,1,0:T(8,128)S(1)}, u32[]{:S(2)}, u32[]{:S(2)}) async-start(f32[32,24,256]{2,1,0:T(8,128)} %broadcast_in_dim.12), calls=%async_computation | async-start | bytes 1572864 | tf_op jit(solution)/shard_map/all_to_all | solution.py:243
  13.8 1.6 fusion.3
  15.4 1.8 fusion.1
  17.3 0.9 pad_maximum_fusion
  18.1 1.3 collective-permute-start.1
  19.4 23.1 %all-gather = bf16[512,256]{1,0:T(8,128)(2,1)S(1)} all-gather(bf16[32,256]{1,0:T(8,128)(2,1)S(1)} %convert_bitcast_fusion), channel_id=2, replica_groups={{0,32,64,96,1,33,65,97,2,34,66,98,3,35,67,99},{4,36,68,100,5,37,69,101,..., dimensions={0}, use_global_device_ids=true | all-gather | bytes 278528 | tf_op jit(solution)/shard_map/all_gather | solution.py:272
  42.5 1.6 broadcast_in_dim.13
  44.1 16.1 %all-to-all-start.1 = ((bf16[8,4,128,256]{3,2,1,0:T(8,128)(2,1)}), bf16[8,4,128,256]{3,2,1,0:T(8,128)(2,1)S(1)}, u32[]{:S(2)}, u32[]{:S(2)}) async-start(bf16[8,4,128,256]{3,2,1,0:T(8,128)(2,1)} %broadcast_in_dim.13), calls=%async_computation.1 | async-start | bytes 4194304 | tf_op jit(solution)/shard_map/all_to_all | solution.py:243
  60.2 1.0 pad_maximum_fusion.2
  61.2 1.3 collective-permute-start
  62.5 8.3 %collective-permute-done.back = bf16[3,8,8192]{2,1,0:T(8,128)(2,1)S(1)} collective-permute-done((bf16[3,8,8192]{2,1,0:T(8,128)(2,1)S(1)}, bf16[3,8,8192]{2,1,0:T(8,128)(2,1)S(1)}, u32[]{:S(2)}, u32[]{:S(2)}) %collective-permute-start) | collective-permute-done | bytes 393248 | tf_op jit(solution)/shard_map/ppermute | solution.py:266
  70.8 0.7 copy-done.3
  71.6 0.8 copy-done.2
  72.4 7.7 %shard_map.146 = (bf16[128,4096]{1,0:T(8,128)(2,1)}, bf16[136,4096]{1,0:T(8,128)(2,1)}) custom-call(bf16[1,128,8192]{2,1,0:T(8,128)(2,1)} %q.7, bf16[1,128,8192]{2,1,0:T(8,128)(2,1)} %k.7, bf16[1,128,8192]{2,1,0:T(8,128)(2,1)} %v.7, bf16[1,128,8192]{2,1,0:T(8,128)(2,1)} %go.7, bf16[3,8,8192]{2,1,0:T(8,128)(2,1)} %copy-done.3, bf16[4,8,8192]{2,1,0:T(8,128)(2,1)} %copy-done.2, ...), custom_call_target="tpu_custom_call" | custom-call | tf_op jit(solution)/shard_map/pallas_call | solution.py:290
  80.1 1.3 collective-permute-start.5
  81.4 7.8 %shard_map.145 = (bf16[128,4096]{1,0:T(8,128)(2,1)}, bf16[136,4096]{1,0:T(8,128)(2,1)}) custom-call(bf16[1,128,8192]{2,1,0:T(8,128)(2,1)} %q.7, bf16[1,128,8192]{2,1,0:T(8,128)(2,1)} %k.7, bf16[1,128,8192]{2,1,0:T(8,128)(2,1)} %v.7, bf16[1,128,8192]{2,1,0:T(8,128)(2,1)} %go.7, bf16[3,8,8192]{2,1,0:T(8,128)(2,1)} %copy-done.3, bf16[4,8,8192]{2,1,0:T(8,128)(2,1)} %copy-done.2, ...), custom_call_target="tpu_custom_call" | custom-call | tf_op jit(solution)/shard_map/pallas_call | solution.py:290
  89.2 1.3 collective-permute-start.3
  90.5 6.4 %collective-permute-start.4 = (bf16[128,4096]{1,0:T(8,128)(2,1)}, bf16[128,4096]{1,0:T(8,128)(2,1)}, u32[]{:S(2)}, u32[]{:S(2)}) collective-permute-start(bf16[128,4096]{1,0:T(8,128)(2,1)} %get-tuple-element.22), channel_id=1, source_target_pairs={{0,1},{1,2},{2,3},{3,4},{4,5},{5,6},{6,7},{7,8},{8,9},{9,10},{10,1... | collective-permute-start | bytes 3145736 | tf_op jit(solution)/shard_map/ppermute | solution.py:301
  96.8 3.4 %collective-permute-start.2 = (bf16[128,4096]{1,0:T(8,128)(2,1)}, bf16[128,4096]{1,0:T(8,128)(2,1)}, u32[]{:S(2)}, u32[]{:S(2)}) collective-permute-start(bf16[128,4096]{1,0:T(8,128)(2,1)} %get-tuple-element.20), channel_id=1, source_target_pairs={{0,1},{1,2},{2,3},{3,4},{4,5},{5,6},{6,7},{7,8},{8,9},{9,10},{10,1... | collective-permute-start | bytes 3145736 | tf_op jit(solution)/shard_map/ppermute | solution.py:301
  100.2 17.4 %collective-permute-done.4.u_prev = bf16[128,4096]{1,0:T(8,128)(2,1)} collective-permute-done((bf16[128,4096]{1,0:T(8,128)(2,1)}, bf16[128,4096]{1,0:T(8,128)(2,1)}, u32[]{:S(2)}, u32[]{:S(2)}) %collective-permute-start.4) | collective-permute-done | bytes 1048608 | tf_op jit(solution)/shard_map/ppermute | solution.py:301
  117.7 1.3 copy-done.1
  119.0 19.7 %shard_map.147 = (bf16[1,128,8192]{2,1,0:T(8,128)(2,1)}, bf16[1,128,8192]{2,1,0:T(8,128)(2,1)}, bf16[1,128,8192]{2,1,0:T(8,128)(2,1)}, bf16[1,128,8192]{2,1,0:T(8,128)(2,1)}, bf16[8,2,152,256]{3,2,1,0:T(8,128)(2,1)}) custom-call(bf16[1,128,8192]{2,1,0:T(8,128)(2,1)} %q.7, bf16[1,128,8192]{2,1,0:T(8,128)(2,1)} %k.7, bf16[1,128,8192]{2,1,0:T(8,128)(2,1)} %v.7, ...), custom_call_target="tpu_custom_call" | custom-call | tf_op jit(solution)/shard_map/pallas_call | solution.py:326
  138.7 1.4 collective-permute-done.2.u_prev
  140.1 19.7 %shard_map.148 = (bf16[1,128,8192]{2,1,0:T(8,128)(2,1)}, bf16[1,128,8192]{2,1,0:T(8,128)(2,1)}, bf16[1,128,8192]{2,1,0:T(8,128)(2,1)}, bf16[1,128,8192]{2,1,0:T(8,128)(2,1)}, bf16[8,2,152,256]{3,2,1,0:T(8,128)(2,1)}) custom-call(bf16[1,128,8192]{2,1,0:T(8,128)(2,1)} %q.7, ...), custom_call_target="tpu_custom_call", output_to_operand_aliasing={{0}: (14, {}), {1}: (15, {}), {2}: (16, {}), {3}: (17, {})} | custom-call | tf_op jit(solution)/shard_map/pallas_call | solution.py:326
  159.9 50.3 %all_to_all.25 = bf16[8,2,152,256]{3,2,1,0:T(8,128)(2,1)S(1)} all-to-all(bf16[8,2,152,256]{3,2,1,0:T(8,128)(2,1)} %get-tuple-element.33), channel_id=1, replica_groups={{0,4,8,12,16,20,24,28},{1,5,9,13,17,21,25,29},{2,6,10,14,18,22,26,30},{..., dimensions={0} | all-to-all | bytes 2490368 | tf_op jit(solution)/shard_map/all_to_all | solution.py:243
  210.1 3.6 %all-to-all-start.2 = ((bf16[8,2,152,256]{3,2,1,0:T(8,128)(2,1)}), bf16[8,2,152,256]{3,2,1,0:T(8,128)(2,1)S(1)}, u32[]{:S(2)}, u32[]{:S(2)}) async-start(bf16[8,2,152,256]{3,2,1,0:T(8,128)(2,1)} %get-tuple-element.32), calls=%async_computation.2 | async-start | bytes 2490368 | tf_op jit(solution)/shard_map/all_to_all | solution.py:243
  213.9 19.2 %all-to-all-done.2 = bf16[8,2,152,256]{3,2,1,0:T(8,128)(2,1)S(1)} async-done(((bf16[8,2,152,256]{3,2,1,0:T(8,128)(2,1)}), bf16[8,2,152,256]{3,2,1,0:T(8,128)(2,1)S(1)}, u32[]{:S(2)}, u32[]{:S(2)}) %all-to-all-start.2) | async-done | bytes 1245216 | tf_op jit(solution)/shard_map/all_to_all | solution.py:243
  233.4 12.3 %all_to_all.26 = bf16[16,56,256]{2,1,0:T(8,128)(2,1)S(1)} all-to-all(bf16[16,56,256]{2,1,0:T(8,128)(2,1)S(1)} %pad_maximum_fusion.1), channel_id=1, replica_groups={{0,32,64,96,1,33,65,97,2,34,66,98,3,35,67,99},{4,36,68,100,5,37,69,101,..., dimensions={0} | all-to-all | bytes 917504 | tf_op jit(solution)/shard_map/all_to_all | solution.py:243
  245.8 0.6 slice_bitcast_fusion
  246.4 0.6 reshape.29
  (26 shorter events, 0.6 us)
Async XLA Ops:
  1.4 15.9 %slice-start = ((bf16[1,128,8192]{2,1,0:T(8,128)(2,1)}), bf16[1,8,8192]{2,1,0:T(8,128)(2,1)S(1)}, s32[]{:S(2)}) async-start(bf16[1,128,8192]{2,1,0:T(8,128)(2,1)} %go.7), calls=%async_computation.5 | async-start | bytes 262144 | tf_op jit(solution)/shard_map/slice | solution.py:265
  2.3 17.1 %copy-start.5 = (f32[256,32]{0,1:T(8,128)S(1)}, f32[256,32]{0,1:T(8,128)}, u32[]{:S(2)}) copy-start(f32[256,32]{0,1:T(8,128)} %param.14) | copy-start | bytes 98308
  2.3 40.2 %all-to-all-start = ((f32[32,24,256]{2,1,0:T(8,128)}), f32[32,24,256]{2,1,0:T(8,128)S(1)}, u32[]{:S(2)}, u32[]{:S(2)}) async-start(f32[32,24,256]{2,1,0:T(8,128)} %broadcast_in_dim.12), calls=%async_computation | async-start | bytes 1572864 | tf_op jit(solution)/shard_map/all_to_all | solution.py:243
  18.1 52.7 %collective-permute-start.1 = (bf16[4,8,8192]{2,1,0:T(8,128)(2,1)}, bf16[4,8,8192]{2,1,0:T(8,128)(2,1)S(1)}, u32[]{:S(2)}, u32[]{:S(2)}) collective-permute-start(bf16[4,8,8192]{2,1,0:T(8,128)(2,1)} %pad_maximum_fusion), channel_id=1, source_target_pairs={{1,0},{2,1},{3,2},{4,3},{5,4},{6,5},{7,6},{8,7},{9,8},{10,9},{11,1... | collective-permute-start | bytes 1572872 | tf_op jit(solution)/shard_map/ppermute | solution.py:267
  42.5 1.6 copy-start
  44.1 16.1 %copy-start.4 = (bf16[1,8,8192]{2,1,0:T(8,128)(2,1)S(1)}, bf16[1,8,8192]{2,1,0:T(8,128)(2,1)}, u32[]{:S(2)}) copy-start(bf16[1,8,8192]{2,1,0:T(8,128)(2,1)} %get-tuple-element.39) | copy-start | bytes 393220
  44.1 73.6 %all-to-all-start.1 = ((bf16[8,4,128,256]{3,2,1,0:T(8,128)(2,1)}), bf16[8,4,128,256]{3,2,1,0:T(8,128)(2,1)S(1)}, u32[]{:S(2)}, u32[]{:S(2)}) async-start(bf16[8,4,128,256]{3,2,1,0:T(8,128)(2,1)} %broadcast_in_dim.13), calls=%async_computation.1 | async-start | bytes 4194304 | tf_op jit(solution)/shard_map/all_to_all | solution.py:243
  61.2 9.6 %collective-permute-start = (bf16[3,8,8192]{2,1,0:T(8,128)(2,1)S(1)}, bf16[3,8,8192]{2,1,0:T(8,128)(2,1)S(1)}, u32[]{:S(2)}, u32[]{:S(2)}) collective-permute-start(bf16[3,8,8192]{2,1,0:T(8,128)(2,1)S(1)} %pad_maximum_fusion.2), channel_id=1, source_target_pairs={{0,1},{1,2},{2,3},{3,4},{4,5},{5,6},{6,7},{7,8},{8,9},{9,10},{10,1... | collective-permute-start | bytes 1179656 | tf_op jit(solution)/shard_map/ppermute | solution.py:266
  70.8 0.7 copy-start.3
  71.5 0.8 copy-start.2
  80.1 37.6 %collective-permute-start.5 = (bf16[136,4096]{1,0:T(8,128)(2,1)}, bf16[136,4096]{1,0:T(8,128)(2,1)}, u32[]{:S(2)}, u32[]{:S(2)}) collective-permute-start(bf16[136,4096]{1,0:T(8,128)(2,1)} %get-tuple-element.23), channel_id=1, source_target_pairs={{1,0},{2,1},{3,2},{4,3},{5,4},{6,5},{7,6},{8,7},{9,8},{10,9},{11,1... | collective-permute-start | bytes 3342344 | tf_op jit(solution)/shard_map/ppermute | solution.py:302
  89.2 50.9 %collective-permute-start.3 = (bf16[136,4096]{1,0:T(8,128)(2,1)}, bf16[136,4096]{1,0:T(8,128)(2,1)}, u32[]{:S(2)}, u32[]{:S(2)}) collective-permute-start(bf16[136,4096]{1,0:T(8,128)(2,1)} %get-tuple-element.21), channel_id=1, source_target_pairs={{1,0},{2,1},{3,2},{4,3},{5,4},{6,5},{7,6},{8,7},{9,8},{10,9},{11,1... | collective-permute-start | bytes 3342344 | tf_op jit(solution)/shard_map/ppermute | solution.py:302
  90.5 27.2 %collective-permute-start.4 = (bf16[128,4096]{1,0:T(8,128)(2,1)}, bf16[128,4096]{1,0:T(8,128)(2,1)}, u32[]{:S(2)}, u32[]{:S(2)}) collective-permute-start(bf16[128,4096]{1,0:T(8,128)(2,1)} %get-tuple-element.22), channel_id=1, source_target_pairs={{0,1},{1,2},{2,3},{3,4},{4,5},{5,6},{6,7},{7,8},{8,9},{9,10},{10,1... | collective-permute-start | bytes 3145736 | tf_op jit(solution)/shard_map/ppermute | solution.py:301
  96.8 43.3 %collective-permute-start.2 = (bf16[128,4096]{1,0:T(8,128)(2,1)}, bf16[128,4096]{1,0:T(8,128)(2,1)}, u32[]{:S(2)}, u32[]{:S(2)}) collective-permute-start(bf16[128,4096]{1,0:T(8,128)(2,1)} %get-tuple-element.20), channel_id=1, source_target_pairs={{0,1},{1,2},{2,3},{3,4},{4,5},{5,6},{6,7},{7,8},{8,9},{9,10},{10,1... | collective-permute-start | bytes 3145736 | tf_op jit(solution)/shard_map/ppermute | solution.py:301
  117.7 1.3 copy-start.1
  210.1 23.0 %all-to-all-start.2 = ((bf16[8,2,152,256]{3,2,1,0:T(8,128)(2,1)}), bf16[8,2,152,256]{3,2,1,0:T(8,128)(2,1)S(1)}, u32[]{:S(2)}, u32[]{:S(2)}) async-start(bf16[8,2,152,256]{3,2,1,0:T(8,128)(2,1)} %get-tuple-element.32), calls=%async_computation.2 | async-start | bytes 2490368 | tf_op jit(solution)/shard_map/all_to_all | solution.py:243

commit v6 on v4

--- a/solution.py
+++ b/solution.py
@@ -271,7 +271,9 @@
     taps = spread(short, n_context, "context")
     mine = lax.all_gather(med_filter.astype(BF).T, "dp", axis=0, tiled=True)
     mine = spread(mine, parts, "context", inner)
-    h_all = spread(mine, coarse, "context", outer)
+    h_all = []
+    for first, count in CHUNKS:
+        h_all.append(spread(mine[first : first + count], coarse, "context", outer))
 
     whole = lambda x: pl.BlockSpec(x.shape, lambda *_: (0,) * x.ndim)
     pieces = []
@@ -313,7 +315,7 @@
         stack = lambda height, at=at: pl.BlockSpec((height, ROW, wide), lambda i: (0, 0, at(i)))
         filters = pl.BlockSpec((count, held_short, group), lambda i, at=at: (at(i), 0, 0))
         packed = lambda height: pl.BlockSpec((height, wide), lambda i: (0, i))
-        taps_h = pl.BlockSpec((1, count, block, group), lambda i, place=place: (i, place, 0, 0))
+        taps_h = pl.BlockSpec((1, count, block, group), lambda i: (i, 0, 0, 0))
         padded = pltpu.VMEM((cols, block + 2 * ROW, LANES), F32)
         shifted = pltpu.VMEM((cols, rows, LANES), F32)
         strip = lambda height: pltpu.VMEM((cols, height * ROW, LANES), F32)
@@ -321,7 +323,7 @@
         u_prev, dz_next = pieces[index]
         carried = [] if outs is None else list(outs)
         fixed = [query_in, key_in, value_in, grad_out, back, fore, taps, u_prev, dz_next]
-        fixed += [h_all, *tables]
+        fixed += [h_all[index], *tables]
         *outs, partial = pl.pallas_call(
             functools.partial(mixer, block, width, count),
             grid=(coarse,),

time: 236 us -> 230 us (0.975)
  starting transfers between devices: 37.6 us -> 46.5 us
  blocking collectives: 72.3 us -> 65.9 us
  waiting for transfers between devices: 53.8 us -> 48.5 us
    all_to_all x4 -> x5, starting transfers between devices: 20.1 us -> 28.9 us  [exchange(): return lax.all_to_all(x, axes, 0, 0, axis_index_groups=groups)]
    ppermute x2, waiting for transfers between devices: 16.3 us -> 8.43 us  [per_device(): u_prev = lax.ppermute(u, 'context', ahead)]
    all_to_all x2, blocking collectives: 65.8 us -> 59.5 us  [exchange(): return lax.all_to_all(x, axes, 0, 0, axis_index_groups=groups)]
    all_to_all x4 -> x5, waiting for transfers between devices: 30.8 us -> 33.4 us  [exchange(): return lax.all_to_all(x, axes, 0, 0, axis_index_groups=groups)]
  transfers between devices with their start and end apart: 10 -> 11, of which waited for: 6 -> 6; matrix products, arithmetic and copies ran while one was open for 3% -> 3% of each run, Pallas kernels for 15% -> 15%
where the time goes in v6:
time: 230 us; the launch traced here: 229 us
  blocking collectives  65.9 us (29%)
  Pallas kernels  55 us (24%)
  waiting for transfers between devices  48.5 us (21%)
  starting transfers between devices  46.5 us (20%)
  local copies, waits for them, and re-layouts  9.71 us (4%)
  other arithmetic  2.36 us (1%)
    all_to_all x2, blocking collectives, exchange(): return lax.all_to_all(x, axes, 0, 0, axis_index_groups=groups)  59.5 us
    pallas_call x2, Pallas kernels, per_device(): pl.pallas_call(functools.partial(mixer, block, width, count), grid=(coars...  39.4 us
    all_to_all x5, waiting for transfers between devices, exchange(): return lax.all_to_all(x, axes, 0, 0, axis_index_groups=groups)  33.4 us
    all_to_all x5, starting transfers between devices, exchange(): return lax.all_to_all(x, axes, 0, 0, axis_index_groups=groups)  28.9 us
    pallas_call x2, Pallas kernels, per_device(): pl.pallas_call(functools.partial(make_products, block, width, cols), grid...  15.6 us
    ppermute x2, starting transfers between devices, per_device(): u_prev = lax.ppermute(u, 'context', ahead)  9.72 us
    ppermute x2, waiting for transfers between devices, per_device(): u_prev = lax.ppermute(u, 'context', ahead)  8.43 us
    ppermute x1, waiting for transfers between devices, per_device(): back = lax.ppermute(back, 'context', ahead)  6.71 us
  transfers between devices with their start and end apart: 11, of which 6 were waited for; matrix products, arithmetic and copies ran while one was open for 3% of the time, Pallas kernels for 15%

profile of v6, /device:TPU:1, one launch (start us, length us, event | category | flops | bytes accessed | tf_op | source)
XLA Modules:
  0.0 228.8 jit_solution(17647115933133175176)
XLA Ops:
  0.6 0.8 convert_bitcast_fusion
  1.4 6.4 %all_gather.3 = bf16[128,256]{1,0:T(8,128)(2,1)S(1)} all-gather(bf16[32,256]{1,0:T(8,128)(2,1)S(1)} %convert_bitcast_fusion), channel_id=1, replica_groups=mesh['dp'=4,'context'=32] {'dp'}, dimensions={0}, use_global_device_ids=true | all-gather | bytes 81920 | tf_op jit(solution)/shard_map/all_gather | solution.py:272
  8.6 5.1 %all-to-all-start.1 = ((bf16[4,128,256]{2,1,0:T(8,128)(2,1)}), bf16[4,128,256]{2,1,0:T(8,128)(2,1)S(1)}, u32[]{:S(2)}, u32[]{:S(2)}) async-start(bf16[4,128,256]{2,1,0:T(8,128)(2,1)} %broadcast_in_dim.19), calls=%async_computation.1 | async-start | bytes 524288 | tf_op jit(solution)/shard_map/all_to_all | solution.py:243
  13.7 1.9 fusion.1
  15.6 1.0 fusion.3
  16.6 3.1 %all-to-all-done.1 = bf16[4,128,256]{2,1,0:T(8,128)(2,1)S(1)} async-done(((bf16[4,128,256]{2,1,0:T(8,128)(2,1)}), bf16[4,128,256]{2,1,0:T(8,128)(2,1)S(1)}, u32[]{:S(2)}, u32[]{:S(2)}) %all-to-all-start.1) | async-done | bytes 262176 | tf_op jit(solution)/shard_map/all_to_all | solution.py:243
  19.7 0.9 broadcast_in_dim.18
  20.7 7.6 %all-to-all-start = ((f32[32,24,256]{2,1,0:T(8,128)}), f32[32,24,256]{2,1,0:T(8,128)S(1)}, u32[]{:S(2)}, u32[]{:S(2)}) async-start(f32[32,24,256]{2,1,0:T(8,128)} %broadcast_in_dim.18), calls=%async_computation | async-start | bytes 1572864 | tf_op jit(solution)/shard_map/all_to_all | solution.py:243
  28.4 1.3 collective-permute-start.1
  29.7 12.0 %all-to-all-done.taps = f32[32,24,256]{2,1,0:T(8,128)S(1)} async-done(((f32[32,24,256]{2,1,0:T(8,128)}), f32[32,24,256]{2,1,0:T(8,128)S(1)}, u32[]{:S(2)}, u32[]{:S(2)}) %all-to-all-start) | async-done | bytes 786464 | tf_op jit(solution)/shard_map/all_to_all | solution.py:243
  41.7 1.2 broadcast_in_dim.21
  42.9 3.6 %all-to-all-start.3 = ((bf16[8,2,128,256]{3,2,1,0:T(8,128)(2,1)}), bf16[8,2,128,256]{3,2,1,0:T(8,128)(2,1)S(1)}, u32[]{:S(2)}, u32[]{:S(2)}) async-start(bf16[8,2,128,256]{3,2,1,0:T(8,128)(2,1)} %broadcast_in_dim.21), calls=%async_computation.3 | async-start | bytes 2097152 | tf_op jit(solution)/shard_map/all_to_all | solution.py:243
  46.5 1.0 pad_maximum_fusion.2
  47.5 4.0 %collective-permute-start = (bf16[3,8,8192]{2,1,0:T(8,128)(2,1)S(1)}, bf16[3,8,8192]{2,1,0:T(8,128)(2,1)S(1)}, u32[]{:S(2)}, u32[]{:S(2)}) collective-permute-start(bf16[3,8,8192]{2,1,0:T(8,128)(2,1)S(1)} %pad_maximum_fusion.2), channel_id=1, source_target_pairs={{0,1},{1,2},{2,3},{3,4},{4,5},{5,6},{6,7},{7,8},{8,9},{9,10},{10,1... | collective-permute-start | bytes 1179656 | tf_op jit(solution)/shard_map/ppermute | solution.py:266
  51.5 6.7 %collective-permute-done.back = bf16[3,8,8192]{2,1,0:T(8,128)(2,1)S(1)} collective-permute-done((bf16[3,8,8192]{2,1,0:T(8,128)(2,1)S(1)}, bf16[3,8,8192]{2,1,0:T(8,128)(2,1)S(1)}, u32[]{:S(2)}, u32[]{:S(2)}) %collective-permute-start) | collective-permute-done | bytes 393248 | tf_op jit(solution)/shard_map/ppermute | solution.py:266
  59.0 0.8 copy-done.1
  59.8 7.7 %shard_map.146 = (bf16[128,4096]{1,0:T(8,128)(2,1)}, bf16[136,4096]{1,0:T(8,128)(2,1)}) custom-call(bf16[1,128,8192]{2,1,0:T(8,128)(2,1)} %q.7, bf16[1,128,8192]{2,1,0:T(8,128)(2,1)} %k.7, bf16[1,128,8192]{2,1,0:T(8,128)(2,1)} %v.7, bf16[1,128,8192]{2,1,0:T(8,128)(2,1)} %go.7, bf16[3,8,8192]{2,1,0:T(8,128)(2,1)} %copy-done.2, bf16[4,8,8192]{2,1,0:T(8,128)(2,1)} %copy-done.1, ...), custom_call_target="tpu_custom_call" | custom-call | tf_op jit(solution)/shard_map/pallas_call | solution.py:291
  67.5 1.3 collective-permute-start.5
  68.8 7.9 %shard_map.145 = (bf16[128,4096]{1,0:T(8,128)(2,1)}, bf16[136,4096]{1,0:T(8,128)(2,1)}) custom-call(bf16[1,128,8192]{2,1,0:T(8,128)(2,1)} %q.7, bf16[1,128,8192]{2,1,0:T(8,128)(2,1)} %k.7, bf16[1,128,8192]{2,1,0:T(8,128)(2,1)} %v.7, bf16[1,128,8192]{2,1,0:T(8,128)(2,1)} %go.7, bf16[3,8,8192]{2,1,0:T(8,128)(2,1)} %copy-done.2, bf16[4,8,8192]{2,1,0:T(8,128)(2,1)} %copy-done.1, ...), custom_call_target="tpu_custom_call" | custom-call | tf_op jit(solution)/shard_map/pallas_call | solution.py:291
  76.6 1.3 collective-permute-start.3
  77.9 6.4 %collective-permute-start.4 = (bf16[128,4096]{1,0:T(8,128)(2,1)}, bf16[128,4096]{1,0:T(8,128)(2,1)}, u32[]{:S(2)}, u32[]{:S(2)}) collective-permute-start(bf16[128,4096]{1,0:T(8,128)(2,1)} %get-tuple-element.22), channel_id=1, source_target_pairs={{0,1},{1,2},{2,3},{3,4},{4,5},{5,6},{6,7},{7,8},{8,9},{9,10},{10,1... | collective-permute-start | bytes 3145736 | tf_op jit(solution)/shard_map/ppermute | solution.py:302
  84.3 3.3 %collective-permute-start.2 = (bf16[128,4096]{1,0:T(8,128)(2,1)}, bf16[128,4096]{1,0:T(8,128)(2,1)}, u32[]{:S(2)}, u32[]{:S(2)}) collective-permute-start(bf16[128,4096]{1,0:T(8,128)(2,1)} %get-tuple-element.20), channel_id=1, source_target_pairs={{0,1},{1,2},{2,3},{3,4},{4,5},{5,6},{6,7},{7,8},{8,9},{9,10},{10,1... | collective-permute-start | bytes 3145736 | tf_op jit(solution)/shard_map/ppermute | solution.py:302
  87.6 1.2 broadcast_in_dim.20
  88.8 9.0 %all-to-all-start.2 = ((bf16[8,2,128,256]{3,2,1,0:T(8,128)(2,1)}), bf16[8,2,128,256]{3,2,1,0:T(8,128)(2,1)S(1)}, u32[]{:S(2)}, u32[]{:S(2)}) async-start(bf16[8,2,128,256]{3,2,1,0:T(8,128)(2,1)} %broadcast_in_dim.20), calls=%async_computation.2 | async-start | bytes 2097152 | tf_op jit(solution)/shard_map/all_to_all | solution.py:243
  97.8 5.7 %collective-permute-done.4.u_prev = bf16[128,4096]{1,0:T(8,128)(2,1)} collective-permute-done((bf16[128,4096]{1,0:T(8,128)(2,1)}, bf16[128,4096]{1,0:T(8,128)(2,1)}, u32[]{:S(2)}, u32[]{:S(2)}) %collective-permute-start.4) | collective-permute-done | bytes 1048608 | tf_op jit(solution)/shard_map/ppermute | solution.py:302
  103.5 19.7 %shard_map.147 = (bf16[1,128,8192]{2,1,0:T(8,128)(2,1)}, bf16[1,128,8192]{2,1,0:T(8,128)(2,1)}, bf16[1,128,8192]{2,1,0:T(8,128)(2,1)}, bf16[1,128,8192]{2,1,0:T(8,128)(2,1)}, bf16[8,2,152,256]{3,2,1,0:T(8,128)(2,1)}) custom-call(bf16[1,128,8192]{2,1,0:T(8,128)(2,1)} %q.7, bf16[1,128,8192]{2,1,0:T(8,128)(2,1)} %k.7, bf16[1,128,8192]{2,1,0:T(8,128)(2,1)} %v.7, ...), custom_call_target="tpu_custom_call" | custom-call | tf_op jit(solution)/shard_map/pallas_call | solution.py:327
  123.2 2.8 %collective-permute-done.2.u_prev = bf16[128,4096]{1,0:T(8,128)(2,1)} collective-permute-done((bf16[128,4096]{1,0:T(8,128)(2,1)}, bf16[128,4096]{1,0:T(8,128)(2,1)}, u32[]{:S(2)}, u32[]{:S(2)}) %collective-permute-start.2) | collective-permute-done | bytes 1048608 | tf_op jit(solution)/shard_map/ppermute | solution.py:302
  126.0 19.7 %shard_map.148 = (bf16[1,128,8192]{2,1,0:T(8,128)(2,1)}, bf16[1,128,8192]{2,1,0:T(8,128)(2,1)}, bf16[1,128,8192]{2,1,0:T(8,128)(2,1)}, bf16[1,128,8192]{2,1,0:T(8,128)(2,1)}, bf16[8,2,152,256]{3,2,1,0:T(8,128)(2,1)}) custom-call(bf16[1,128,8192]{2,1,0:T(8,128)(2,1)} %q.7, ...), custom_call_target="tpu_custom_call", output_to_operand_aliasing={{0}: (14, {}), {1}: (15, {}), {2}: (16, {}), {3}: (17, {})} | custom-call | tf_op jit(solution)/shard_map/pallas_call | solution.py:327
  145.7 30.1 %all_to_all.35 = bf16[8,2,152,256]{3,2,1,0:T(8,128)(2,1)S(1)} all-to-all(bf16[8,2,152,256]{3,2,1,0:T(8,128)(2,1)} %get-tuple-element.33), channel_id=1, replica_groups={{0,4,8,12,16,20,24,28},{1,5,9,13,17,21,25,29},{2,6,10,14,18,22,26,30},{..., dimensions={0} | all-to-all | bytes 2490368 | tf_op jit(solution)/shard_map/all_to_all | solution.py:243
  175.9 3.6 %all-to-all-start.4 = ((bf16[8,2,152,256]{3,2,1,0:T(8,128)(2,1)}), bf16[8,2,152,256]{3,2,1,0:T(8,128)(2,1)S(1)}, u32[]{:S(2)}, u32[]{:S(2)}) async-start(bf16[8,2,152,256]{3,2,1,0:T(8,128)(2,1)} %get-tuple-element.32), calls=%async_computation.4 | async-start | bytes 2490368 | tf_op jit(solution)/shard_map/all_to_all | solution.py:243
  179.6 18.2 %all-to-all-done.4 = bf16[8,2,152,256]{3,2,1,0:T(8,128)(2,1)S(1)} async-done(((bf16[8,2,152,256]{3,2,1,0:T(8,128)(2,1)}), bf16[8,2,152,256]{3,2,1,0:T(8,128)(2,1)S(1)}, u32[]{:S(2)}, u32[]{:S(2)}) %all-to-all-start.4) | async-done | bytes 1245216 | tf_op jit(solution)/shard_map/all_to_all | solution.py:243
  198.1 29.3 %all_to_all.36 = bf16[16,56,256]{2,1,0:T(8,128)(2,1)S(1)} all-to-all(bf16[16,56,256]{2,1,0:T(8,128)(2,1)S(1)} %pad_maximum_fusion.1), channel_id=1, replica_groups={{0,32,64,96,1,33,65,97,2,34,66,98,3,35,67,99},{4,36,68,100,5,37,69,101,..., dimensions={0} | all-to-all | bytes 917504 | tf_op jit(solution)/shard_map/all_to_all | solution.py:243
  (33 shorter events, 3.4 us)
Async XLA Ops:
  0.6 15.9 %copy-start.5 = (f32[3,256,7]{1,2,0:T(8,128)S(1)}, f32[3,256,7]{1,2,0:T(8,128)}, u32[]{:S(2)}) copy-start(f32[3,256,7]{1,2,0:T(8,128)} %param.15) | copy-start | bytes 64516
  8.6 11.2 %all-to-all-start.1 = ((bf16[4,128,256]{2,1,0:T(8,128)(2,1)}), bf16[4,128,256]{2,1,0:T(8,128)(2,1)S(1)}, u32[]{:S(2)}, u32[]{:S(2)}) async-start(bf16[4,128,256]{2,1,0:T(8,128)(2,1)} %broadcast_in_dim.19), calls=%async_computation.1 | async-start | bytes 524288 | tf_op jit(solution)/shard_map/all_to_all | solution.py:243
  13.7 14.6 %slice-start = ((bf16[1,128,8192]{2,1,0:T(8,128)(2,1)}), bf16[1,8,8192]{2,1,0:T(8,128)(2,1)S(1)}, s32[]{:S(2)}) async-start(bf16[1,128,8192]{2,1,0:T(8,128)(2,1)} %go.7), calls=%async_computation.7 | async-start | bytes 262144 | tf_op jit(solution)/shard_map/slice | solution.py:265
  20.7 21.1 %all-to-all-start = ((f32[32,24,256]{2,1,0:T(8,128)}), f32[32,24,256]{2,1,0:T(8,128)S(1)}, u32[]{:S(2)}, u32[]{:S(2)}) async-start(f32[32,24,256]{2,1,0:T(8,128)} %broadcast_in_dim.18), calls=%async_computation | async-start | bytes 1572864 | tf_op jit(solution)/shard_map/all_to_all | solution.py:243
  28.4 29.8 %collective-permute-start.1 = (bf16[4,8,8192]{2,1,0:T(8,128)(2,1)S(1)}, bf16[4,8,8192]{2,1,0:T(8,128)(2,1)S(1)}, u32[]{:S(2)}, u32[]{:S(2)}) collective-permute-start(bf16[4,8,8192]{2,1,0:T(8,128)(2,1)S(1)} %pad_maximum_fusion), channel_id=1, source_target_pairs={{1,0},{2,1},{3,2},{4,3},{5,4},{6,5},{7,6},{8,7},{9,8},{10,9},{11,1... | collective-permute-start | bytes 1572872 | tf_op jit(solution)/shard_map/ppermute | solution.py:267
  41.7 16.5 %copy-start = (f32[32,24,256]{2,1,0:T(8,128)}, f32[32,24,256]{2,1,0:T(8,128)S(1)}, u32[]{:S(2)}) copy-start(f32[32,24,256]{2,1,0:T(8,128)S(1)} %all-to-all-done.taps) | copy-start | bytes 2359300
  42.9 44.7 %all-to-all-start.3 = ((bf16[8,2,128,256]{3,2,1,0:T(8,128)(2,1)}), bf16[8,2,128,256]{3,2,1,0:T(8,128)(2,1)S(1)}, u32[]{:S(2)}, u32[]{:S(2)}) async-start(bf16[8,2,128,256]{3,2,1,0:T(8,128)(2,1)} %broadcast_in_dim.21), calls=%async_computation.3 | async-start | bytes 2097152 | tf_op jit(solution)/shard_map/all_to_all | solution.py:243
  47.5 10.7 %collective-permute-start = (bf16[3,8,8192]{2,1,0:T(8,128)(2,1)S(1)}, bf16[3,8,8192]{2,1,0:T(8,128)(2,1)S(1)}, u32[]{:S(2)}, u32[]{:S(2)}) collective-permute-start(bf16[3,8,8192]{2,1,0:T(8,128)(2,1)S(1)} %pad_maximum_fusion.2), channel_id=1, source_target_pairs={{0,1},{1,2},{2,3},{3,4},{4,5},{5,6},{6,7},{7,8},{8,9},{9,10},{10,1... | collective-permute-start | bytes 1179656 | tf_op jit(solution)/shard_map/ppermute | solution.py:266
  58.2 0.8 copy-start.2
  59.0 0.8 copy-start.1
  67.5 36.0 %collective-permute-start.5 = (bf16[136,4096]{1,0:T(8,128)(2,1)}, bf16[136,4096]{1,0:T(8,128)(2,1)}, u32[]{:S(2)}, u32[]{:S(2)}) collective-permute-start(bf16[136,4096]{1,0:T(8,128)(2,1)} %get-tuple-element.23), channel_id=1, source_target_pairs={{1,0},{2,1},{3,2},{4,3},{5,4},{6,5},{7,6},{8,7},{9,8},{10,9},{11,1... | collective-permute-start | bytes 3342344 | tf_op jit(solution)/shard_map/ppermute | solution.py:303
  76.6 49.4 %collective-permute-start.3 = (bf16[136,4096]{1,0:T(8,128)(2,1)}, bf16[136,4096]{1,0:T(8,128)(2,1)}, u32[]{:S(2)}, u32[]{:S(2)}) collective-permute-start(bf16[136,4096]{1,0:T(8,128)(2,1)} %get-tuple-element.21), channel_id=1, source_target_pairs={{1,0},{2,1},{3,2},{4,3},{5,4},{6,5},{7,6},{8,7},{9,8},{10,9},{11,1... | collective-permute-start | bytes 3342344 | tf_op jit(solution)/shard_map/ppermute | solution.py:303
  77.9 25.6 %collective-permute-start.4 = (bf16[128,4096]{1,0:T(8,128)(2,1)}, bf16[128,4096]{1,0:T(8,128)(2,1)}, u32[]{:S(2)}, u32[]{:S(2)}) collective-permute-start(bf16[128,4096]{1,0:T(8,128)(2,1)} %get-tuple-element.22), channel_id=1, source_target_pairs={{0,1},{1,2},{2,3},{3,4},{4,5},{5,6},{6,7},{7,8},{8,9},{9,10},{10,1... | collective-permute-start | bytes 3145736 | tf_op jit(solution)/shard_map/ppermute | solution.py:302
  84.3 41.7 %collective-permute-start.2 = (bf16[128,4096]{1,0:T(8,128)(2,1)}, bf16[128,4096]{1,0:T(8,128)(2,1)}, u32[]{:S(2)}, u32[]{:S(2)}) collective-permute-start(bf16[128,4096]{1,0:T(8,128)(2,1)} %get-tuple-element.20), channel_id=1, source_target_pairs={{0,1},{1,2},{2,3},{3,4},{4,5},{5,6},{6,7},{7,8},{8,9},{9,10},{10,1... | collective-permute-start | bytes 3145736 | tf_op jit(solution)/shard_map/ppermute | solution.py:302
  87.6 15.9 %copy-start.3 = (bf16[8,2,128,256]{3,2,1,0:T(8,128)(2,1)}, bf16[8,2,128,256]{3,2,1,0:T(8,128)(2,1)S(1)}, u32[]{:S(2)}) copy-start(bf16[8,2,128,256]{3,2,1,0:T(8,128)(2,1)S(1)} %all-to-all-done.3.h_ref) | copy-start | bytes 3145732
  88.8 34.4 %all-to-all-start.2 = ((bf16[8,2,128,256]{3,2,1,0:T(8,128)(2,1)}), bf16[8,2,128,256]{3,2,1,0:T(8,128)(2,1)S(1)}, u32[]{:S(2)}, u32[]{:S(2)}) async-start(bf16[8,2,128,256]{3,2,1,0:T(8,128)(2,1)} %broadcast_in_dim.20), calls=%async_computation.2 | async-start | bytes 2097152 | tf_op jit(solution)/shard_map/all_to_all | solution.py:243
  123.2 2.8 %copy-start.4 = (bf16[8,2,128,256]{3,2,1,0:T(8,128)(2,1)}, bf16[8,2,128,256]{3,2,1,0:T(8,128)(2,1)S(1)}, u32[]{:S(2)}) copy-start(bf16[8,2,128,256]{3,2,1,0:T(8,128)(2,1)S(1)} %all-to-all-done.2.h_ref) | copy-start | bytes 3145732
  175.9 22.0 %all-to-all-start.4 = ((bf16[8,2,152,256]{3,2,1,0:T(8,128)(2,1)}), bf16[8,2,152,256]{3,2,1,0:T(8,128)(2,1)S(1)}, u32[]{:S(2)}, u32[]{:S(2)}) async-start(bf16[8,2,152,256]{3,2,1,0:T(8,128)(2,1)} %get-tuple-element.32), calls=%async_computation.4 | async-start | bytes 2490368 | tf_op jit(solution)/shard_map/all_to_all | solution.py:243

commit v7 on v4

--- a/solution.py
+++ b/solution.py
@@ -94,12 +94,12 @@
         ).astype(BF)
 
 
-def mixer(block, width, subs, q, k, v, go, back, fore, taps, u_prev, dz_next, h_ref, *rest):
+def mixer(block, width, subs, q, k, v, go, back, fore, taps, u_prev, dz_next, h_mine, h_other, h_last, *rest):
     rows = block + ROW
     half = block
     per = q.shape[2] // LANES // subs
     group = per * LANES
-    t_window, t_own, t_ahead, t_inverse = rest[:4]
+    t_window, t_own, t_ahead, t_inverse, t_taps = rest[:5]
     outs = rest[len(rest) - 24 :]
     mixed, g_q, g_k, g_v, g_part, sums, x_q, x_k, x_v, s_q, s_k, s_v, g_pad = outs[:13]
     h_pad, h_flip, z_pad, window, dz_own, edge_u, edge_z, spec_u, spec_h, spec_d, spec_w = outs[13:]
@@ -139,7 +139,7 @@
         window[sub, block + 2 * ROW : 2 * block, inside] = u_prev[2 * ROW : block, lanes]
         edge_u[col] = u_before + u_after
         edge_z[col] = dz_next[block : block + ROW, lanes].astype(F32) + dz[0:ROW].astype(F32)
-        h_pad[col, 0 : 2 * ROW, :] = h_ref[0, sub, block - 2 * ROW : block, inside].astype(F32)
+        h_pad[col, 0 : 2 * ROW, :] = h_last[0, sub, :, inside].astype(F32)
         h_pad[col, 2 * ROW : 3 * ROW, :] = jnp.zeros((ROW, LANES), F32)
         h_flip[col, 0:ROW, :] = jnp.zeros((ROW, LANES), F32)
         for place in range(width - 2):
@@ -151,8 +151,8 @@
         lanes = pl.ds(sub * group, group)
         x = window[sub]
         spec_u[sub] = dot_twice(t_window[...], x)
-        h = h_ref[0, sub]
-        spec_h[sub] = dot_twice(t_own[...], h)
+        h = jnp.concatenate([h_mine[0, sub], h_other[0, sub]], axis=0)
+        spec_h[sub] = dot_twice(t_taps[...], h)
         d = dz_own[sub]
         spec_d[sub] = dot_twice(t_own[...], d)
         a = dz_next[0:block, lanes]
@@ -269,9 +269,25 @@
     short = short_filter.transpose(0, 2, 1).reshape(3 * width, group)
     short = jnp.pad(short, ((0, held_short - 3 * width), (0, 0)))
     taps = spread(short, n_context, "context")
-    mine = lax.all_gather(med_filter.astype(BF).T, "dp", axis=0, tiled=True)
+    parity = lax.axis_index("dp") & 1
+    half = block // 2
+    mine = lax.all_gather(
+        med_filter.astype(BF).T,
+        "dp",
+        axis=0,
+        tiled=True,
+        axis_index_groups=[list(range(core, n_dp, 2)) for core in range(2)],
+    )
     mine = spread(mine, parts, "context", inner)
-    h_all = spread(mine, coarse, "context", outer)
+    h_mine = spread(mine, coarse, "context", outer)
+    h_other = lax.ppermute(h_mine, "dp", [(i, i + 1 - 2 * (i % 2)) for i in range(n_dp)])
+    h_last = jnp.where(parity == 1, h_mine, h_other)[:, :, half - 2 * ROW :]
+    own_taps = [
+        np.concatenate([np.arange(d * taps_own, (d + 1) * taps_own) for d in range(core, n_dp, 2)])
+        for core in range(2)
+    ]
+    choices = [split_host(phases(np.concatenate([own_taps[c], own_taps[1 - c]]), size)) for c in (0, 1)]
+    tables.append(jnp.where(parity == 0, choices[0], choices[1]))
 
     whole = lambda x: pl.BlockSpec(x.shape, lambda *_: (0,) * x.ndim)
     pieces = []
@@ -313,7 +329,9 @@
         stack = lambda height, at=at: pl.BlockSpec((height, ROW, wide), lambda i: (0, 0, at(i)))
         filters = pl.BlockSpec((count, held_short, group), lambda i, at=at: (at(i), 0, 0))
         packed = lambda height: pl.BlockSpec((height, wide), lambda i: (0, i))
-        taps_h = pl.BlockSpec((1, count, block, group), lambda i, place=place: (i, place, 0, 0))
+        taps_h = lambda height, place=place: pl.BlockSpec(
+            (1, count, height, group), lambda i: (i, place, 0, 0)
+        )
         padded = pltpu.VMEM((cols, block + 2 * ROW, LANES), F32)
         shifted = pltpu.VMEM((cols, rows, LANES), F32)
         strip = lambda height: pltpu.VMEM((cols, height * ROW, LANES), F32)
@@ -321,12 +339,13 @@
         u_prev, dz_next = pieces[index]
         carried = [] if outs is None else list(outs)
         fixed = [query_in, key_in, value_in, grad_out, back, fore, taps, u_prev, dz_next]
-        fixed += [h_all, *tables]
+        fixed += [h_mine, h_other, h_last, *tables]
         *outs, partial = pl.pallas_call(
             functools.partial(mixer, block, width, count),
             grid=(coarse,),
             in_specs=[tokens] * 4
-            + [stack(3), stack(4), filters, packed(block), packed(rows), taps_h]
+            + [stack(3), stack(4), filters, packed(block), packed(rows)]
+            + [taps_h(half), taps_h(half), taps_h(2 * ROW)]
             + [whole(x) for x in tables]
             + [pl.BlockSpec(memory_space=pl.ANY)] * len(carried),
             out_specs=[tokens] * 4

time: 236 us -> 218 us (0.924)
  blocking collectives: 72.3 us -> 51.7 us
  starting transfers between devices: 37.6 us -> 41.9 us
  local copies, waits for them, and re-layouts: 11.9 us -> 8.97 us
    all_to_all x2, blocking collectives: 65.8 us -> 47.8 us  [exchange(): return lax.all_to_all(x, axes, 0, 0, axis_index_groups=groups)]
    ppermute x0 -> x1, starting transfers between devices: none -> 5.54 us  [per_device(): lax.ppermute(h_mine, 'dp', [(i, i + 1 - 2 * (i % 2)) for i in range(n_dp)])]
    all_gather x1, blocking collectives: 6.44 us -> 3.88 us  [per_device(): lax.all_gather(med_filter.astype(BF).T, 'dp', axis=0, tiled=True, axis_in...]
  transfers between devices with their start and end apart: 10 -> 11, of which waited for: 6 -> 6; matrix products, arithmetic and copies ran while one was open for 3% -> 3% of each run, Pallas kernels for 15% -> 16%
where the time goes in v7:
time: 218 us; the launch traced here: 217 us
  Pallas kernels  55.2 us (25%)
  waiting for transfers between devices  54.7 us (25%)
  blocking collectives  51.7 us (24%)
  starting transfers between devices  41.9 us (19%)
  local copies, waits for them, and re-layouts  8.97 us (4%)
  other arithmetic  3.73 us (2%)
    all_to_all x2, blocking collectives, exchange(): return lax.all_to_all(x, axes, 0, 0, axis_index_groups=groups)  47.8 us
    pallas_call x2, Pallas kernels, per_device(): pl.pallas_call(functools.partial(mixer, block, width, count), grid=(coars...  39.6 us
    all_to_all x4, waiting for transfers between devices, exchange(): return lax.all_to_all(x, axes, 0, 0, axis_index_groups=groups)  30.9 us
    all_to_all x4, starting transfers between devices, exchange(): return lax.all_to_all(x, axes, 0, 0, axis_index_groups=groups)  19.5 us
    pallas_call x2, Pallas kernels, per_device(): pl.pallas_call(functools.partial(make_products, block, width, cols), grid...  15.6 us
    ppermute x2, waiting for transfers between devices, per_device(): u_prev = lax.ppermute(u, 'context', ahead)  14.8 us
    ppermute x2, starting transfers between devices, per_device(): u_prev = lax.ppermute(u, 'context', ahead)  9.81 us
    ppermute x1, waiting for transfers between devices, per_device(): back = lax.ppermute(back, 'context', ahead)  9.01 us
  transfers between devices with their start and end apart: 11, of which 6 were waited for; matrix products, arithmetic and copies ran while one was open for 3% of the time, Pallas kernels for 16%

profile of v7, /device:TPU:1, one launch (start us, length us, event | category | flops | bytes accessed | tf_op | source)
XLA Modules:
  0.0 216.9 jit_solution(682098500483573680)
XLA Ops:
  0.6 0.8 convert_bitcast_fusion
  1.4 3.9 %all_gather.3 = bf16[64,256]{1,0:T(8,128)(2,1)S(1)} all-gather(bf16[32,256]{1,0:T(8,128)(2,1)S(1)} %convert_bitcast_fusion), channel_id=1, replica_groups={{0,64},{32,96},{1,65},{33,97},{2,66},{34,98},{3,67},{35,99},{4,68},{36,..., dimensions={0}, use_global_device_ids=true | all-gather | bytes 49152 | tf_op jit(solution)/shard_map/all_gather | solution.py:274
  5.9 5.2 %all-to-all-start.1 = ((bf16[4,64,256]{2,1,0:T(8,128)(2,1)}), bf16[4,64,256]{2,1,0:T(8,128)(2,1)S(1)}, u32[]{:S(2)}, u32[]{:S(2)}) async-start(bf16[4,64,256]{2,1,0:T(8,128)(2,1)} %broadcast_in_dim.16), calls=%async_computation.1 | async-start | bytes 262144 | tf_op jit(solution)/shard_map/all_to_all | solution.py:243
  11.1 1.1 fusion.1
  12.3 3.7 %all-to-all-done.1 = bf16[4,64,256]{2,1,0:T(8,128)(2,1)S(1)} async-done(((bf16[4,64,256]{2,1,0:T(8,128)(2,1)}), bf16[4,64,256]{2,1,0:T(8,128)(2,1)S(1)}, u32[]{:S(2)}, u32[]{:S(2)}) %all-to-all-start.1) | async-done | bytes 131104 | tf_op jit(solution)/shard_map/all_to_all | solution.py:243
  16.0 1.1 broadcast_in_dim.17
  17.1 6.8 %all-to-all-start.2 = ((bf16[8,4,64,256]{3,2,1,0:T(8,128)(2,1)}), bf16[8,4,64,256]{3,2,1,0:T(8,128)(2,1)S(1)}, u32[]{:S(2)}, u32[]{:S(2)}) async-start(bf16[8,4,64,256]{3,2,1,0:T(8,128)(2,1)} %broadcast_in_dim.17), calls=%async_computation.2 | async-start | bytes 2097152 | tf_op jit(solution)/shard_map/all_to_all | solution.py:243
  23.8 1.0 fusion.3
  24.9 1.3 collective-permute-start.1
  26.3 14.2 %all-to-all-done.2.h_mine = bf16[8,4,64,256]{3,2,1,0:T(8,128)(2,1)S(1)} async-done(((bf16[8,4,64,256]{3,2,1,0:T(8,128)(2,1)}), bf16[8,4,64,256]{3,2,1,0:T(8,128)(2,1)S(1)}, u32[]{:S(2)}, u32[]{:S(2)}) %all-to-all-start.2) | async-done | bytes 1048608 | tf_op jit(solution)/shard_map/all_to_all | solution.py:243
  40.4 1.0 broadcast_in_dim.15
  41.5 3.9 %all-to-all-start = ((f32[32,24,256]{2,1,0:T(8,128)}), f32[32,24,256]{2,1,0:T(8,128)S(1)}, u32[]{:S(2)}, u32[]{:S(2)}) async-start(f32[32,24,256]{2,1,0:T(8,128)} %broadcast_in_dim.15), calls=%async_computation | async-start | bytes 1572864 | tf_op jit(solution)/shard_map/all_to_all | solution.py:243
  45.4 3.0 %collective-permute-start = (bf16[3,8,8192]{2,1,0:T(8,128)(2,1)S(1)}, bf16[3,8,8192]{2,1,0:T(8,128)(2,1)S(1)}, u32[]{:S(2)}, u32[]{:S(2)}) collective-permute-start(bf16[3,8,8192]{2,1,0:T(8,128)(2,1)S(1)} %pad_maximum_fusion.2), channel_id=1, source_target_pairs={{0,1},{1,2},{2,3},{3,4},{4,5},{5,6},{6,7},{7,8},{8,9},{9,10},{10,1... | collective-permute-start | bytes 1179656 | tf_op jit(solution)/shard_map/ppermute | solution.py:266
  48.5 5.5 %collective-permute-start.4 = (bf16[8,4,64,256]{3,2,1,0:T(8,128)(2,1)S(1)}, bf16[8,4,64,256]{3,2,1,0:T(8,128)(2,1)}, u32[]{:S(2)}, u32[]{:S(2)}) collective-permute-start(bf16[8,4,64,256]{3,2,1,0:T(8,128)(2,1)S(1)} %all-to-all-done.2.h_mine), channel_id=1, source_target_pairs={{0,32},{32,0},{64,96},{96,64},{1,33},{33,1},{65,97},{97,65},{2,34}... | collective-permute-start | bytes 3145736 | tf_op jit(solution)/shard_map/ppermute | solution.py:283
  54.0 9.0 %collective-permute-done.back = bf16[3,8,8192]{2,1,0:T(8,128)(2,1)S(1)} collective-permute-done((bf16[3,8,8192]{2,1,0:T(8,128)(2,1)S(1)}, bf16[3,8,8192]{2,1,0:T(8,128)(2,1)S(1)}, u32[]{:S(2)}, u32[]{:S(2)}) %collective-permute-start) | collective-permute-done | bytes 393248 | tf_op jit(solution)/shard_map/ppermute | solution.py:266
  64.0 0.9 copy-done
  64.8 7.7 %shard_map.164 = (bf16[128,4096]{1,0:T(8,128)(2,1)}, bf16[136,4096]{1,0:T(8,128)(2,1)}) custom-call(bf16[1,128,8192]{2,1,0:T(8,128)(2,1)} %q.7, bf16[1,128,8192]{2,1,0:T(8,128)(2,1)} %k.7, bf16[1,128,8192]{2,1,0:T(8,128)(2,1)} %v.7, bf16[1,128,8192]{2,1,0:T(8,128)(2,1)} %go.7, bf16[3,8,8192]{2,1,0:T(8,128)(2,1)} %copy-done.3, bf16[4,8,8192]{2,1,0:T(8,128)(2,1)} %copy-done.2, ...), custom_call_target="tpu_custom_call" | custom-call | tf_op jit(solution)/shard_map/pallas_call | solution.py:305
  72.6 1.4 collective-permute-start.6
  74.0 7.8 %shard_map.163 = (bf16[128,4096]{1,0:T(8,128)(2,1)}, bf16[136,4096]{1,0:T(8,128)(2,1)}) custom-call(bf16[1,128,8192]{2,1,0:T(8,128)(2,1)} %q.7, bf16[1,128,8192]{2,1,0:T(8,128)(2,1)} %k.7, bf16[1,128,8192]{2,1,0:T(8,128)(2,1)} %v.7, bf16[1,128,8192]{2,1,0:T(8,128)(2,1)} %go.7, bf16[3,8,8192]{2,1,0:T(8,128)(2,1)} %copy-done.3, bf16[4,8,8192]{2,1,0:T(8,128)(2,1)} %copy-done.2, ...), custom_call_target="tpu_custom_call" | custom-call | tf_op jit(solution)/shard_map/pallas_call | solution.py:305
  81.9 1.3 collective-permute-start.3
  83.1 6.4 %collective-permute-start.5 = (bf16[128,4096]{1,0:T(8,128)(2,1)}, bf16[128,4096]{1,0:T(8,128)(2,1)}, u32[]{:S(2)}, u32[]{:S(2)}) collective-permute-start(bf16[128,4096]{1,0:T(8,128)(2,1)} %get-tuple-element.22), channel_id=1, source_target_pairs={{0,1},{1,2},{2,3},{3,4},{4,5},{5,6},{6,7},{7,8},{8,9},{9,10},{10,1... | collective-permute-start | bytes 3145736 | tf_op jit(solution)/shard_map/ppermute | solution.py:316
  89.5 3.5 %collective-permute-start.2 = (bf16[128,4096]{1,0:T(8,128)(2,1)}, bf16[128,4096]{1,0:T(8,128)(2,1)}, u32[]{:S(2)}, u32[]{:S(2)}) collective-permute-start(bf16[128,4096]{1,0:T(8,128)(2,1)} %get-tuple-element.20), channel_id=1, source_target_pairs={{0,1},{1,2},{2,3},{3,4},{4,5},{5,6},{6,7},{7,8},{8,9},{9,10},{10,1... | collective-permute-start | bytes 3145736 | tf_op jit(solution)/shard_map/ppermute | solution.py:316
  93.6 1.7 slice_select_fusion.h_last
  95.3 13.2 %collective-permute-done.5.u_prev = bf16[128,4096]{1,0:T(8,128)(2,1)} collective-permute-done((bf16[128,4096]{1,0:T(8,128)(2,1)}, bf16[128,4096]{1,0:T(8,128)(2,1)}, u32[]{:S(2)}, u32[]{:S(2)}) %collective-permute-start.5) | collective-permute-done | bytes 1048608 | tf_op jit(solution)/shard_map/ppermute | solution.py:316
  108.5 1.0 copy-done.4
  109.5 19.9 %shard_map.165 = (bf16[1,128,8192]{2,1,0:T(8,128)(2,1)}, bf16[1,128,8192]{2,1,0:T(8,128)(2,1)}, bf16[1,128,8192]{2,1,0:T(8,128)(2,1)}, bf16[1,128,8192]{2,1,0:T(8,128)(2,1)}, bf16[8,2,152,256]{3,2,1,0:T(8,128)(2,1)}) custom-call(bf16[1,128,8192]{2,1,0:T(8,128)(2,1)} %q.7, bf16[1,128,8192]{2,1,0:T(8,128)(2,1)} %k.7, bf16[1,128,8192]{2,1,0:T(8,128)(2,1)} %v.7, ...), custom_call_target="tpu_custom_call" | custom-call | tf_op jit(solution)/shard_map/pallas_call | solution.py:343
  129.4 1.6 collective-permute-done.2.u_prev
  131.0 19.7 %shard_map.166 = (bf16[1,128,8192]{2,1,0:T(8,128)(2,1)}, bf16[1,128,8192]{2,1,0:T(8,128)(2,1)}, bf16[1,128,8192]{2,1,0:T(8,128)(2,1)}, bf16[1,128,8192]{2,1,0:T(8,128)(2,1)}, bf16[8,2,152,256]{3,2,1,0:T(8,128)(2,1)}) custom-call(bf16[1,128,8192]{2,1,0:T(8,128)(2,1)} %q.7, ...), custom_call_target="tpu_custom_call", output_to_operand_aliasing={{0}: (17, {}), {1}: (18, {}), {2}: (19, {}), {3}: (20, {})} | custom-call | tf_op jit(solution)/shard_map/pallas_call | solution.py:343
  150.7 29.3 %all_to_all.30 = bf16[8,2,152,256]{3,2,1,0:T(8,128)(2,1)S(1)} all-to-all(bf16[8,2,152,256]{3,2,1,0:T(8,128)(2,1)} %get-tuple-element.33), channel_id=1, replica_groups={{0,4,8,12,16,20,24,28},{1,5,9,13,17,21,25,29},{2,6,10,14,18,22,26,30},{..., dimensions={0} | all-to-all | bytes 2490368 | tf_op jit(solution)/shard_map/all_to_all | solution.py:243
  180.1 3.6 %all-to-all-start.3 = ((bf16[8,2,152,256]{3,2,1,0:T(8,128)(2,1)}), bf16[8,2,152,256]{3,2,1,0:T(8,128)(2,1)S(1)}, u32[]{:S(2)}, u32[]{:S(2)}) async-start(bf16[8,2,152,256]{3,2,1,0:T(8,128)(2,1)} %get-tuple-element.32), calls=%async_computation.3 | async-start | bytes 2490368 | tf_op jit(solution)/shard_map/all_to_all | solution.py:243
  183.8 13.0 %all-to-all-done.3 = bf16[8,2,152,256]{3,2,1,0:T(8,128)(2,1)S(1)} async-done(((bf16[8,2,152,256]{3,2,1,0:T(8,128)(2,1)}), bf16[8,2,152,256]{3,2,1,0:T(8,128)(2,1)S(1)}, u32[]{:S(2)}, u32[]{:S(2)}) %all-to-all-start.3) | async-done | bytes 1245216 | tf_op jit(solution)/shard_map/all_to_all | solution.py:243
  197.1 18.5 %all_to_all.31 = bf16[16,56,256]{2,1,0:T(8,128)(2,1)S(1)} all-to-all(bf16[16,56,256]{2,1,0:T(8,128)(2,1)S(1)} %pad_maximum_fusion.1), channel_id=1, replica_groups={{0,32,64,96,1,33,65,97,2,34,66,98,3,35,67,99},{4,36,68,100,5,37,69,101,..., dimensions={0} | all-to-all | bytes 917504 | tf_op jit(solution)/shard_map/all_to_all | solution.py:243
  (37 shorter events, 4.1 us)
Async XLA Ops:
  5.9 10.0 %all-to-all-start.1 = ((bf16[4,64,256]{2,1,0:T(8,128)(2,1)}), bf16[4,64,256]{2,1,0:T(8,128)(2,1)S(1)}, u32[]{:S(2)}, u32[]{:S(2)}) async-start(bf16[4,64,256]{2,1,0:T(8,128)(2,1)} %broadcast_in_dim.16), calls=%async_computation.1 | async-start | bytes 262144 | tf_op jit(solution)/shard_map/all_to_all | solution.py:243
  12.3 12.6 %slice-start = ((bf16[1,128,8192]{2,1,0:T(8,128)(2,1)}), bf16[1,8,8192]{2,1,0:T(8,128)(2,1)S(1)}, s32[]{:S(2)}) async-start(bf16[1,128,8192]{2,1,0:T(8,128)(2,1)} %go.7), calls=%async_computation.6 | async-start | bytes 262144 | tf_op jit(solution)/shard_map/slice | solution.py:265
  17.1 9.2 %copy-start.7 = (f32[3,256,7]{1,2,0:T(8,128)S(1)}, f32[3,256,7]{1,2,0:T(8,128)}, u32[]{:S(2)}) copy-start(f32[3,256,7]{1,2,0:T(8,128)} %param.17) | copy-start | bytes 64516
  17.1 23.4 %all-to-all-start.2 = ((bf16[8,4,64,256]{3,2,1,0:T(8,128)(2,1)}), bf16[8,4,64,256]{3,2,1,0:T(8,128)(2,1)S(1)}, u32[]{:S(2)}, u32[]{:S(2)}) async-start(bf16[8,4,64,256]{3,2,1,0:T(8,128)(2,1)} %broadcast_in_dim.17), calls=%async_computation.2 | async-start | bytes 2097152 | tf_op jit(solution)/shard_map/all_to_all | solution.py:243
  24.9 38.1 %collective-permute-start.1 = (bf16[4,8,8192]{2,1,0:T(8,128)(2,1)S(1)}, bf16[4,8,8192]{2,1,0:T(8,128)(2,1)S(1)}, u32[]{:S(2)}, u32[]{:S(2)}) collective-permute-start(bf16[4,8,8192]{2,1,0:T(8,128)(2,1)S(1)} %pad_maximum_fusion), channel_id=1, source_target_pairs={{1,0},{2,1},{3,2},{4,3},{5,4},{6,5},{7,6},{8,7},{9,8},{10,9},{11,1... | collective-permute-start | bytes 1572872 | tf_op jit(solution)/shard_map/ppermute | solution.py:267
  40.4 53.2 %copy-start.1 = (bf16[8,4,64,256]{3,2,1,0:T(8,128)(2,1)}, bf16[8,4,64,256]{3,2,1,0:T(8,128)(2,1)S(1)}, u32[]{:S(2)}) copy-start(bf16[8,4,64,256]{3,2,1,0:T(8,128)(2,1)S(1)} %all-to-all-done.2.h_mine) | copy-start | bytes 3145732
  41.5 21.6 %all-to-all-start = ((f32[32,24,256]{2,1,0:T(8,128)}), f32[32,24,256]{2,1,0:T(8,128)S(1)}, u32[]{:S(2)}, u32[]{:S(2)}) async-start(f32[32,24,256]{2,1,0:T(8,128)} %broadcast_in_dim.15), calls=%async_computation | async-start | bytes 1572864 | tf_op jit(solution)/shard_map/all_to_all | solution.py:243
  45.4 17.6 %collective-permute-start = (bf16[3,8,8192]{2,1,0:T(8,128)(2,1)S(1)}, bf16[3,8,8192]{2,1,0:T(8,128)(2,1)S(1)}, u32[]{:S(2)}, u32[]{:S(2)}) collective-permute-start(bf16[3,8,8192]{2,1,0:T(8,128)(2,1)S(1)} %pad_maximum_fusion.2), channel_id=1, source_target_pairs={{0,1},{1,2},{2,3},{3,4},{4,5},{5,6},{6,7},{7,8},{8,9},{9,10},{10,1... | collective-permute-start | bytes 1179656 | tf_op jit(solution)/shard_map/ppermute | solution.py:266
  48.5 45.1 %collective-permute-start.4 = (bf16[8,4,64,256]{3,2,1,0:T(8,128)(2,1)S(1)}, bf16[8,4,64,256]{3,2,1,0:T(8,128)(2,1)}, u32[]{:S(2)}, u32[]{:S(2)}) collective-permute-start(bf16[8,4,64,256]{3,2,1,0:T(8,128)(2,1)S(1)} %all-to-all-done.2.h_mine), channel_id=1, source_target_pairs={{0,32},{32,0},{64,96},{96,64},{1,33},{33,1},{65,97},{97,65},{2,34}... | collective-permute-start | bytes 3145736 | tf_op jit(solution)/shard_map/ppermute | solution.py:283
  63.0 0.8 copy-start.3
  63.0 0.9 copy-start.2
  64.0 0.9 copy-start
  72.6 20.4 %copy-start.5 = (bf16[256,256]{1,0:T(8,128)(2,1)S(1)}, bf16[256,256]{1,0:T(8,128)(2,1)}, u32[]{:S(2)}) copy-start(bf16[256,256]{1,0:T(8,128)(2,1)} %constant.30.clone) | copy-start | bytes 393220
  72.6 20.4 %copy-start.6 = (bf16[256,256]{1,0:T(8,128)(2,1)S(1)}, bf16[256,256]{1,0:T(8,128)(2,1)}, u32[]{:S(2)}) copy-start(bf16[256,256]{1,0:T(8,128)(2,1)} %constant.29.clone) | copy-start | bytes 393220
  72.6 35.9 %collective-permute-start.6 = (bf16[136,4096]{1,0:T(8,128)(2,1)}, bf16[136,4096]{1,0:T(8,128)(2,1)S(1)}, u32[]{:S(2)}, u32[]{:S(2)}) collective-permute-start(bf16[136,4096]{1,0:T(8,128)(2,1)} %get-tuple-element.23), channel_id=1, source_target_pairs={{1,0},{2,1},{3,2},{4,3},{5,4},{6,5},{7,6},{8,7},{9,8},{10,9},{11,1... | collective-permute-start | bytes 3342344 | tf_op jit(solution)/shard_map/ppermute | solution.py:317
  81.9 49.1 %collective-permute-start.3 = (bf16[136,4096]{1,0:T(8,128)(2,1)}, bf16[136,4096]{1,0:T(8,128)(2,1)}, u32[]{:S(2)}, u32[]{:S(2)}) collective-permute-start(bf16[136,4096]{1,0:T(8,128)(2,1)} %get-tuple-element.21), channel_id=1, source_target_pairs={{1,0},{2,1},{3,2},{4,3},{5,4},{6,5},{7,6},{8,7},{9,8},{10,9},{11,1... | collective-permute-start | bytes 3342344 | tf_op jit(solution)/shard_map/ppermute | solution.py:317
  83.1 25.4 %collective-permute-start.5 = (bf16[128,4096]{1,0:T(8,128)(2,1)}, bf16[128,4096]{1,0:T(8,128)(2,1)}, u32[]{:S(2)}, u32[]{:S(2)}) collective-permute-start(bf16[128,4096]{1,0:T(8,128)(2,1)} %get-tuple-element.22), channel_id=1, source_target_pairs={{0,1},{1,2},{2,3},{3,4},{4,5},{5,6},{6,7},{7,8},{8,9},{9,10},{10,1... | collective-permute-start | bytes 3145736 | tf_op jit(solution)/shard_map/ppermute | solution.py:316
  89.5 41.5 %collective-permute-start.2 = (bf16[128,4096]{1,0:T(8,128)(2,1)}, bf16[128,4096]{1,0:T(8,128)(2,1)}, u32[]{:S(2)}, u32[]{:S(2)}) collective-permute-start(bf16[128,4096]{1,0:T(8,128)(2,1)} %get-tuple-element.20), channel_id=1, source_target_pairs={{0,1},{1,2},{2,3},{3,4},{4,5},{5,6},{6,7},{7,8},{8,9},{9,10},{10,1... | collective-permute-start | bytes 3145736 | tf_op jit(solution)/shard_map/ppermute | solution.py:316
  108.5 1.0 copy-start.4
  180.1 16.8 %all-to-all-start.3 = ((bf16[8,2,152,256]{3,2,1,0:T(8,128)(2,1)}), bf16[8,2,152,256]{3,2,1,0:T(8,128)(2,1)S(1)}, u32[]{:S(2)}, u32[]{:S(2)}) async-start(bf16[8,2,152,256]{3,2,1,0:T(8,128)(2,1)} %get-tuple-element.32), calls=%async_computation.3 | async-start | bytes 2490368 | tf_op jit(solution)/shard_map/all_to_all | solution.py:243
